TPU v7x, 32 devices: a whole 2x2x4 slice. The times are simulated.
32 devices in a mesh: acct: 8 (over z, y), rep: 4 (over x, core).
Axes of the slice: x: 2, y: 2, z: 4, core: 2. Of those that a mesh axis runs over, the one named last changes fastest.
Arguments:
- memory: bfloat16 [262144, 256], P(('acct', 'rep')), may hold values from -4 to 4
- features: bfloat16 [4096, 128], P(('acct', 'rep')), may hold values from -6 to 6
- buckets: int32 [4096], P(('acct', 'rep')), may hold values from 0 to 4095
- src_owner: int32 [4096, 1], P(('acct', 'rep')), may hold values from 0 to 31; in each aligned block of 128 rows (0 to 127, 128 to 255, ...) at most 8 rows name the same one
- src_slot: int32 [4096], P(('acct', 'rep')), may hold values from 0 to 8191
- dst_owner: int32 [4096, 1], P(('acct', 'rep')), may hold values from 0 to 31; in each aligned block of 128 rows (0 to 127, 128 to 255, ...) at most 8 rows name the same one
- dst_slot: int32 [4096], P(('acct', 'rep')), may hold values from 0 to 8191
- nb_owner: int32 [4096, 10, 1], P(('acct', 'rep')), may hold values from 0 to 31; in each aligned block of 1280 rows (0 to 1279, 1280 to 2559, ..., all dimensions but the last counted through in order) at most 80 rows name the same one
- nb_slot: int32 [4096, 10], P(('acct', 'rep')), may hold values from 0 to 8191
- w_msg: bfloat16 [512, 128], replicated, may hold values from -0.25 to 0.25
- w_in: bfloat16 [128, 768], replicated, may hold values from -0.5 to 0.5
- u_zr: bfloat16 [256, 512], replicated, may hold values from -0.375 to 0.375
- u_h: bfloat16 [256, 256], replicated, may hold values from -0.375 to 0.375
- w_query: bfloat16 [256, 256], replicated, may hold values from -0.375 to 0.375
- w_key: bfloat16 [256, 256], replicated, may hold values from -0.375 to 0.375
- w_value: bfloat16 [256, 256], replicated, may hold values from -0.375 to 0.375
- emb_grad: bfloat16 [4096, 256], P(('acct', 'rep')), may hold values from -6 to 6
Outputs:
- new_memory: bfloat16 [262144, 256], P(('acct', 'rep'))
- embedding: bfloat16 [4096, 256], P(('acct', 'rep'))
- grad_msg: float32 [512, 128], replicated
- grad_in: float32 [128, 768], replicated
- grad_zr: float32 [256, 512], replicated
- grad_h: float32 [256, 256], replicated
- grad_query: float32 [256, 256], replicated
- grad_key: float32 [256, 256], replicated
- grad_value: float32 [256, 256], replicated
Inputs may be any that keep to these rules, and one draw needn't show every extreme that they name: `src_owner`: in each aligned block of 128 events (one device's events) at most 8 events name one owner, a bound that some block reaches. `dst_owner`: in each aligned block of 128 events at most 8 events name one owner, a bound that some block reaches. `nb_owner`: in each aligned block of 128 events (1280 entries) at most 80 entries name one owner, a bound that some block reaches.
All inputs are finite; a program needn't handle non-finite values.
Results may differ from a plain program's by a relative error of at most 0.01.
Values may be sent and summed in bfloat16 or wider, within the bound.
No kernel may reach another device: no remote copies, remote signals or barrier semaphores. Data moves between devices by JAX's collectives and lax.ppermute only.
A program may use at most 192 MiB of HBM per device.

v0:
```python
import math

import jax
import jax.numpy as jnp
from jax import lax
from jax.sharding import PartitionSpec as P

HEADS = 2


cap_value = 10.0


def widen(tensor):
    return lax.optimization_barrier(tensor).astype(jnp.float32)


def time_code(buckets, code_width):
    column = jnp.arange(code_width, dtype=jnp.float32)
    frequency = jnp.exp(column * (-11.5 / code_width))
    return jnp.cos(buckets.astype(jnp.float32)[:, None] * frequency[None, :])


def message_forward(own_rows, features, buckets, w_msg):
    code_width = w_msg.shape[0] - own_rows.shape[1] - features.shape[1]
    encoded = time_code(buckets, code_width).astype(jnp.bfloat16)
    inputs = jnp.concatenate([own_rows, features, encoded], axis=1)
    pre_act = jnp.dot(inputs, w_msg, preferred_element_type=jnp.float32)
    message = jax.nn.silu(pre_act).astype(jnp.bfloat16)
    return (inputs, pre_act, message)


def message_backward(inputs, pre_act, d_message):
    sigmoid_pre = jax.nn.sigmoid(pre_act)
    d_pre = (d_message * sigmoid_pre * (1.0 + pre_act * (1.0 - sigmoid_pre))).astype(jnp.bfloat16)
    return jnp.dot(inputs.T, d_pre, preferred_element_type=jnp.float32)


def gru_forward(mean_rows, state_rows, touched, w_in, u_zr, u_h):
    row_width = state_rows.shape[1]
    from_input = jnp.dot(mean_rows, w_in, preferred_element_type=jnp.float32)
    from_state = jnp.dot(state_rows, u_zr, preferred_element_type=jnp.float32)
    update_gate = jax.nn.sigmoid(from_input[:, :row_width] + from_state[:, :row_width])
    reset_gate = jax.nn.sigmoid(
        from_input[:, row_width : 2 * row_width] + from_state[:, row_width:]
    )
    state_wide = state_rows.astype(jnp.float32)
    reset_state = (reset_gate * state_wide).astype(jnp.bfloat16)
    candidate = jnp.tanh(
        from_input[:, 2 * row_width :]
        + jnp.dot(reset_state, u_h, preferred_element_type=jnp.float32)
    )
    updated = (1.0 - update_gate) * state_wide + update_gate * candidate
    new_rows = jnp.where(touched[:, None], updated, state_wide).astype(jnp.bfloat16)
    return (new_rows, (update_gate, reset_gate, candidate, reset_state, state_wide))


def gru_backward(d_rows, touched, kept_values, mean_rows, state_rows, w_in, u_h):
    update_gate, reset_gate, candidate, reset_state, state_wide = kept_values
    row_width = state_rows.shape[1]
    d_updated = jnp.where(touched[:, None], d_rows, jnp.zeros_like(d_rows))
    d_update = d_updated * (candidate - state_wide)
    d_candidate = (d_updated * update_gate * (1.0 - candidate * candidate)).astype(jnp.bfloat16)
    grad_h = jnp.dot(reset_state.T, d_candidate, preferred_element_type=jnp.float32)
    d_reset_state = jnp.dot(d_candidate, u_h.T, preferred_element_type=jnp.float32)
    d_reset = d_reset_state * state_wide * reset_gate * (1.0 - reset_gate)
    d_update_in = d_update * update_gate * (1.0 - update_gate)
    d_gates = jnp.concatenate(
        [d_update_in.astype(jnp.bfloat16), d_reset.astype(jnp.bfloat16), d_candidate], axis=1
    )
    grad_in = jnp.dot(mean_rows.T, d_gates, preferred_element_type=jnp.float32)
    grad_zr = jnp.dot(state_rows.T, d_gates[:, : 2 * row_width], preferred_element_type=jnp.float32)
    d_mean = jnp.dot(d_gates, w_in.T, preferred_element_type=jnp.float32)
    return (d_mean, grad_in, grad_zr, grad_h)


def attend(q_rows, k_rows, w_query, w_key, w_value, upstream):
    batch_rows, row_width = q_rows.shape
    neighbours = k_rows.shape[1]
    head_size = row_width // HEADS
    scaling = 1.0 / math.sqrt(head_size)
    flat_keys = k_rows.reshape(batch_rows * neighbours, row_width)
    query_proj = jnp.dot(q_rows, w_query, preferred_element_type=jnp.float32).astype(jnp.bfloat16)
    key_proj = jnp.dot(flat_keys, w_key, preferred_element_type=jnp.float32).astype(jnp.bfloat16)
    value_proj = jnp.dot(flat_keys, w_value, preferred_element_type=jnp.float32).astype(
        jnp.bfloat16
    )
    q_heads = widen(query_proj).reshape(batch_rows, HEADS, head_size)
    k_heads = widen(key_proj).reshape(batch_rows, neighbours, HEADS, head_size)
    v_heads = widen(value_proj).reshape(batch_rows, neighbours, HEADS, head_size)
    raw_scores = jnp.einsum("bhd,bkhd->bhk", q_heads, k_heads) * scaling
    capped = jnp.tanh(raw_scores / cap_value)
    weights = jnp.exp(cap_value * capped)
    attention = weights / jnp.sum(weights, axis=2, keepdims=True)
    attention_b = widen(attention.astype(jnp.bfloat16))
    mixture = jnp.einsum("bhk,bkhd->bhd", attention_b, v_heads).reshape(batch_rows, row_width)
    embedded = (q_rows.astype(jnp.float32) + mixture).astype(jnp.bfloat16)
    up_heads = upstream.reshape(batch_rows, HEADS, head_size)
    d_probs = jnp.einsum("bhd,bkhd->bhk", up_heads, v_heads)
    d_scores = attention * (d_probs - jnp.sum(attention * d_probs, axis=2, keepdims=True))
    d_raw = d_scores * (1.0 - capped * capped) * scaling
    d_query = (
        jnp.einsum("bhk,bkhd->bhd", d_raw, k_heads)
        .reshape(batch_rows, row_width)
        .astype(jnp.bfloat16)
    )
    d_keys = (
        jnp.einsum("bhk,bhd->bkhd", d_raw, q_heads)
        .reshape(batch_rows * neighbours, row_width)
        .astype(jnp.bfloat16)
    )
    d_values = (
        jnp.einsum("bhk,bhd->bkhd", attention_b, up_heads)
        .reshape(batch_rows * neighbours, row_width)
        .astype(jnp.bfloat16)
    )
    grad_query = jnp.dot(q_rows.T, d_query, preferred_element_type=jnp.float32)
    grad_key = jnp.dot(flat_keys.T, d_keys, preferred_element_type=jnp.float32)
    grad_value = jnp.dot(flat_keys.T, d_values, preferred_element_type=jnp.float32)
    d_q_rows = upstream + jnp.dot(d_query, w_query.T, preferred_element_type=jnp.float32)
    d_k_rows = (
        jnp.dot(d_keys, w_key.T, preferred_element_type=jnp.float32)
        + jnp.dot(d_values, w_value.T, preferred_element_type=jnp.float32)
    ).reshape(batch_rows, neighbours, row_width)
    return (embedded, d_q_rows, d_k_rows, grad_query, grad_key, grad_value)


def slot_positions(owners, devices):
    matches = (owners[:, None] == jnp.arange(devices, dtype=jnp.int32)[None, :]).astype(jnp.int32)
    before = jnp.cumsum(matches, axis=0) - matches
    return jnp.sum(before * matches, axis=1)


def body(
    memory,
    features,
    buckets,
    src_owner,
    src_slot,
    dst_owner,
    dst_slot,
    nb_owner,
    nb_slot,
    w_msg,
    w_in,
    u_zr,
    u_h,
    w_query,
    w_key,
    w_value,
    emb_grad,
):
    devices = lax.axis_size(("acct", "rep"))
    events, row_width = emb_grad.shape
    acc_rows = memory.shape[0]
    neighbours = nb_slot.shape[1]
    feat_width = features.shape[1]
    cap_event = 2 * events // devices
    cap_neigh = 2 * events * neighbours // devices
    src_owners = src_owner[:, 0]
    dst_owners = dst_owner[:, 0]
    nb_owners = nb_owner.reshape(-1)
    src_place = src_owners * cap_event + slot_positions(src_owners, devices)
    dst_place = dst_owners * cap_event + slot_positions(dst_owners, devices)
    nb_place = nb_owners * cap_neigh + slot_positions(nb_owners, devices)
    unused = jnp.full((devices * cap_event,), -1, jnp.int32)
    side_slots = jnp.stack(
        [
            unused.at[src_place].set(src_slot).reshape(devices, cap_event),
            unused.at[dst_place].set(dst_slot).reshape(devices, cap_event),
        ],
        axis=1,
    )
    zero_ints = jnp.zeros((devices * cap_event,), jnp.int32)
    side_times = jnp.stack(
        [
            zero_ints.at[src_place].set(buckets).reshape(devices, cap_event),
            zero_ints.at[dst_place].set(buckets).reshape(devices, cap_event),
        ],
        axis=1,
    )
    nb_requests = (
        jnp.full((devices * cap_neigh,), -1, jnp.int32)
        .at[nb_place]
        .set(nb_slot.reshape(-1))
        .reshape(devices, cap_neigh)
    )
    got_slots, got_times, got_neigh = (
        lax.all_to_all(side_slots, ("acct", "rep"), split_axis=0, concat_axis=0, tiled=True),
        lax.all_to_all(side_times, ("acct", "rep"), split_axis=0, concat_axis=0, tiled=True),
        lax.all_to_all(nb_requests, ("acct", "rep"), split_axis=0, concat_axis=0, tiled=True),
    )
    zero_rows = jnp.zeros((devices * cap_event, feat_width), jnp.bfloat16)
    side_feats = jnp.stack(
        [
            zero_rows.at[src_place].set(features).reshape(devices, cap_event, feat_width),
            zero_rows.at[dst_place].set(features).reshape(devices, cap_event, feat_width),
        ],
        axis=1,
    )
    got_feats = lax.all_to_all(side_feats, ("acct", "rep"), split_axis=0, concat_axis=0, tiled=True)
    slot_list = got_slots.reshape(-1)
    present = (slot_list >= 0).astype(jnp.float32)
    safe_slots = jnp.maximum(slot_list, 0)
    inputs, pre_act, message = message_forward(
        memory[safe_slots], got_feats.reshape(-1, feat_width), got_times.reshape(-1), w_msg
    )
    totals = jax.ops.segment_sum(
        message.astype(jnp.float32) * present[:, None], safe_slots, acc_rows
    )
    counts = jax.ops.segment_sum(present, safe_slots, acc_rows)
    divisor = jnp.maximum(counts, 1.0)[:, None]
    mean_rows = (totals / divisor).astype(jnp.bfloat16)
    touched = counts > 0.5
    new_memory, kept_values = gru_forward(mean_rows, memory, touched, w_in, u_zr, u_h)
    dst_rows_asked = jnp.maximum(got_slots[:, 1, :], 0)
    nb_rows_asked = jnp.maximum(got_neigh, 0)
    dst_reply = new_memory[dst_rows_asked]
    nb_reply = new_memory[nb_rows_asked]
    back_dst, back_nb = (
        lax.all_to_all(dst_reply, ("acct", "rep"), split_axis=0, concat_axis=0, tiled=True),
        lax.all_to_all(nb_reply, ("acct", "rep"), split_axis=0, concat_axis=0, tiled=True),
    )
    q_rows = back_dst.reshape(-1, row_width)[dst_place]
    k_rows = back_nb.reshape(-1, row_width)[nb_place].reshape(events, neighbours, row_width)
    embedding, d_q_rows, d_k_rows, grad_query, grad_key, grad_value = attend(
        q_rows, k_rows, w_query, w_key, w_value, emb_grad.astype(jnp.float32)
    )
    dst_grads = jnp.zeros((devices * cap_event, row_width), jnp.float32).at[dst_place].set(d_q_rows)
    nb_grads = (
        jnp.zeros((devices * cap_neigh, row_width), jnp.float32)
        .at[nb_place]
        .set(d_k_rows.reshape(-1, row_width))
    )
    got_dst_grads, got_nb_grads = (
        lax.all_to_all(
            dst_grads.reshape(devices, cap_event, row_width),
            ("acct", "rep"),
            split_axis=0,
            concat_axis=0,
            tiled=True,
        ),
        lax.all_to_all(
            nb_grads.reshape(devices, cap_neigh, row_width),
            ("acct", "rep"),
            split_axis=0,
            concat_axis=0,
            tiled=True,
        ),
    )
    d_memory = jax.ops.segment_sum(
        got_dst_grads.reshape(-1, row_width), dst_rows_asked.reshape(-1), acc_rows
    )
    d_memory = d_memory + jax.ops.segment_sum(
        got_nb_grads.reshape(-1, row_width), nb_rows_asked.reshape(-1), acc_rows
    )
    d_mean, grad_in, grad_zr, grad_h = gru_backward(
        d_memory, touched, kept_values, mean_rows, memory, w_in, u_h
    )
    d_message = (d_mean / divisor)[safe_slots] * present[:, None]
    grad_msg = message_backward(inputs, pre_act, d_message)
    grad_msg, grad_in, grad_zr, grad_h, grad_query, grad_key, grad_value = lax.psum(
        (grad_msg, grad_in, grad_zr, grad_h, grad_query, grad_key, grad_value), ("acct", "rep")
    )
    return (
        new_memory,
        embedding,
        grad_msg,
        grad_in,
        grad_zr,
        grad_h,
        grad_query,
        grad_key,
        grad_value,
    )


def solution(mesh):
    return jax.shard_map(
        body,
        mesh=mesh,
        in_specs=(
            P(("acct", "rep"), None),
            P(("acct", "rep"), None),
            P(("acct", "rep")),
            P(("acct", "rep"), None),
            P(("acct", "rep")),
            P(("acct", "rep"), None),
            P(("acct", "rep")),
            P(("acct", "rep"), None, None),
            P(("acct", "rep"), None),
            P(),
            P(),
            P(),
            P(),
            P(),
            P(),
            P(),
            P(("acct", "rep"), None),
        ),
        out_specs=(
            P(("acct", "rep"), None),
            P(("acct", "rep"), None),
            P(),
            P(),
            P(),
            P(),
            P(),
            P(),
            P(),
        ),
        check_vma=False,
    )
```

profile of v0, /device:TPU:0, one launch (start us, length us, event | category | flops | bytes accessed | tf_op | source)
XLA Modules:
  0.0 553.5 jit_solution(9245944277085125631)
XLA Ops:
  15.1 7.3 %all-to-all-start = ((s32[32,2,8]{2,1,0:T(2,128)}), s32[32,2,8]{2,1,0:T(2,128)S(1)}, u32[]{:S(2)}, u32[]{:S(2)}) async-start(s32[32,2,8]{2,1,0:T(2,128)} %copy.87), calls=%async_computation | async-start | bytes 65536 | tf_op jit(solution)/shard_map/all_to_all | solution.py:189
  29.2 9.1 %reduce-window.6 = s32[32,10,128]{2,1,0:T(8,128)S(1)} reduce-window(s32[32,10,128]{2,1,0:T(8,128)S(1)} %fusion.57, s32[]{:T(128)} %constant.17.clone.1), window={size=1x1x128 pad=0_0x0_0x127_0}, to_apply=%region_12.13 | reduce-window | flops 5201920 | bytes 327684 | tf_op jit(solution)/shard_map/reduce-window
  39.6 10.3 %fusion.117 = f32[8192,512]{0,1:T(8,128)} fusion(bf16[8192,256]{1,0:T(8,128)(2,1)} %param.17, bf16[256,512]{1,0:T(8,128)(2,1)S(1)} %copy-done), kind=kOutput, calls=%fused_computation.187 | convolution fusion | flops 2147483648 | bytes 21233664 | tf_op jit(solution)/shard_map/dot_general | solution.py:42
  50.0 6.4 %copy.91 = bf16[8192,256]{0,1:T(8,128)(2,1)} copy(bf16[8192,256]{1,0:T(8,128)(2,1)} %param.17) | data formatting | bytes 8388608 | tf_op args[0]
  57.3 5.3 scatter_custom_fusion.8
  63.2 5.8 %all-to-all-start.2 = ((s32[32,2,8]{2,1,0:T(2,128)}), s32[32,2,8]{2,1,0:T(2,128)S(1)}, u32[]{:S(2)}, u32[]{:S(2)}) async-start(s32[32,2,8]{2,1,0:T(2,128)} %copy.90), calls=%async_computation.2 | async-start | bytes 65536 | tf_op jit(solution)/shard_map/all_to_all | solution.py:190
  69.4 3.3 scatter_custom_fusion.2
  73.5 2.9 all-to-all-done.2
  76.3 3.2 all-to-all-start.1
  79.7 4.3 gather_fusion
  84.9 2.8 all-to-all-done.1
  87.8 3.1 all-to-all-start.4
  91.2 5.3 scatter_custom_fusion.7
  96.6 11.9 %fusion.113 = f32[8192,768]{0,1:T(8,128)} fusion(bf16[128,768]{1,0:T(8,128)(2,1)S(1)} %copy-done.27, f32[8192,128]{1,0:T(8,128)} %scatter_custom_fusion.7, f32[8192]{0:T(1024)S(1)} %broadcast_maximum_fusion), kind=kOutput, calls=%fused_computation.186 | convolution fusion | flops 1612709888 | bytes 29589504 | tf_op jit(solution)/shard_map/dot_general | solution.py:41
  108.5 19.9 %fusion.6 = (bf16[8192,256]{0,1:T(8,128)(2,1)}, f32[8192,256]{0,1:T(8,128)}) fusion(bf16[8192,256]{0,1:T(8,128)(2,1)S(1)} %copy-done.4, pred[8192]{0:T(1024)(128)(4,1)S(1)} %broadcast_compare_fusion, f32[8192,512]{0,1:T(8,128)} %fusion.117, f32[8192,768]{0,1:T(8,128)} %fusion.113, bf16[256,256]{1,0:T(8,128)(2,1)S(1)} %copy-done.44), kind=kOutput, calls=%fused_computation.32 | convolution fusion | flops 1113587712 | bytes 63053824 | tf_op jit(solution)/shard_map/dot_general | solution.py:51
  128.4 6.4 %copy.104 = bf16[8192,256]{1,0:T(8,128)(2,1)} copy(bf16[8192,256]{0,1:T(8,128)(2,1)} %get-tuple-element.71) | data formatting | bytes 8388608
  134.8 4.4 gather_fusion.1
  139.2 5.7 %all-to-all-start.3 = ((bf16[32,8,256]{2,1,0:T(8,128)(2,1)}), bf16[32,8,256]{2,1,0:T(8,128)(2,1)S(1)}, u32[]{:S(2)}, u32[]{:S(2)}) async-start(bf16[32,8,256]{2,1,0:T(8,128)(2,1)} %bitcast.11), calls=%async_computation.3 | async-start | bytes 262144 | tf_op jit(solution)/shard_map/all_to_all | solution.py:221
  145.6 9.6 %gather_fusion.3 = bf16[2560,256]{1,0:T(8,128)(2,1)} fusion(bf16[8192,256]{1,0:T(8,128)(2,1)} %copy.104, s32[3072]{0:T(1024)S(1)} %pad_clamp_fusion), kind=kCustom, calls=%fused_computation.3 | custom fusion | bytes 2631680 | tf_op jit(solution)/shard_map/gather | solution.py:219
  155.1 16.5 %all-to-all-start.5 = ((bf16[32,80,256]{2,1,0:T(8,128)(2,1)}), bf16[32,80,256]{2,1,0:T(8,128)(2,1)S(1)}, u32[]{:S(2)}, u32[]{:S(2)}) async-start(bf16[32,80,256]{2,1,0:T(8,128)(2,1)} %bitcast.15), calls=%async_computation.5 | async-start | bytes 2621440 | tf_op jit(solution)/shard_map/all_to_all | solution.py:222
  172.9 30.5 %all-to-all-done.5 = bf16[32,80,256]{2,1,0:T(8,128)(2,1)S(1)} async-done(((bf16[32,80,256]{2,1,0:T(8,128)(2,1)}), bf16[32,80,256]{2,1,0:T(8,128)(2,1)S(1)}, u32[]{:S(2)}, u32[]{:S(2)}) %all-to-all-start.5) | async-done | bytes 1310752 | tf_op jit(solution)/shard_map/all_to_all | solution.py:222
  203.4 4.1 gather_fusion.4
  213.2 1.7 scatter_custom_fusion.9
  214.8 3.6 all-to-all-start.6
  219.7 1.8 multiply_convert_fusion.1
  221.5 1.8 multiply_convert_fusion.2
  225.7 9.7 %scatter_custom_fusion.10 = f32[2560,256]{1,0:T(8,128)} fusion(s32[1280]{0:T(1024)} %copy-done.37, f32[1280,256]{1,0:T(8,128)S(1)} %convolution_add_fusion.1, f32[]{:T(128)} %constant.14.clone.1), kind=kCustom, calls=%fused_computation.66 | custom fusion | bytes 2621952 | tf_op jit(solution)/shard_map/scatter | solution.py:233
  235.4 5.8 %all-to-all-start.7 = ((f32[32,80,256]{2,1,0:T(8,128)}), f32[32,80,256]{2,1,0:T(8,128)S(1)}, u32[]{:S(2)}, u32[]{:S(2)}) async-start(f32[32,80,256]{2,1,0:T(8,128)} %bitcast.29), calls=%async_computation.7 | async-start | bytes 5242880 | tf_op jit(solution)/shard_map/all_to_all | solution.py:243
  244.1 1.8 fusion.69
  245.9 2.2 fusion.44
  248.0 2.2 fusion.47
  250.2 51.2 %all-to-all-done.7 = f32[32,80,256]{2,1,0:T(8,128)S(1)} async-done(((f32[32,80,256]{2,1,0:T(8,128)}), f32[32,80,256]{2,1,0:T(8,128)S(1)}, u32[]{:S(2)}, u32[]{:S(2)}) %all-to-all-start.7) | async-done | bytes 2621472 | tf_op jit(solution)/shard_map/all_to_all | solution.py:243
  301.4 23.4 %scatter_custom_fusion.11 = f32[8192,256]{1,0:T(8,128)} fusion(s32[2816]{0:T(1024)} %add_reduce_fusion, f32[]{:T(128)} %constant.14.clone.1, f32[2560,256]{1,0:T(8,128)S(1)} %bitcast.149, f32[]{:T(128)} %constant.74, f32[256,256]{1,0:T(8,128)S(1)} %bitcast.155), kind=kCustom, calls=%fused_computation.53 | custom fusion | flops 1441792 | bytes 11273216 | tf_op jit(solution)/shard_map/add | solution.py:254
  324.8 8.9 %copy.103 = f32[8192,256]{0,1:T(8,128)} copy(f32[8192,256]{1,0:T(8,128)} %scatter_custom_fusion.11) | data formatting | bytes 16777216 | tf_op jit(solution)/shard_map/add | solution.py:254
  333.7 17.8 %fusion.10 = (bf16[8192,256]{0,1:T(8,128)(2,1)}, bf16[8192,256]{0,1:T(8,128)(2,1)}) fusion(f32[8192,256]{0,1:T(8,128)} %get-tuple-element.72, bf16[8192,256]{0,1:T(8,128)(2,1)} %copy.91, f32[8192,256]{0,1:T(8,128)} %copy.103, pred[8192]{0:T(1024)(128)(4,1)S(1)} %copy-done.36, f32[8192,512]{0,1:T(8,128)} %fusion.117, f32[8192,768]{0,1:T(8,128)} %fusion.113), kind=kLoop, calls=%fused_computation.36 | loop fusion | flops 35651584 | bytes 46145536 | tf_op jit(solution)/shard_map/convert_element_type | solution.py:69
  351.6 10.3 %fusion.110 = f32[256,256]{1,0:T(8,128)} fusion(bf16[8192,256]{0,1:T(8,128)(2,1)} %get-tuple-element.64, bf16[8192,256]{0,1:T(8,128)(2,1)S(1)} %copy-done.5, f32[8192,512]{0,1:T(8,128)} %fusion.117, f32[8192,768]{0,1:T(8,128)} %fusion.113), kind=kOutput, calls=%fused_computation.185 | convolution fusion | flops 1088421888 | bytes 25427968 | tf_op jit(solution)/shard_map/dot_general | solution.py:64
  361.9 9.2 %fusion.3 = bf16[8192,256]{0,1:T(8,128)(2,1)} fusion(bf16[8192,256]{0,1:T(8,128)(2,1)S(1)} %copy-done.5, bf16[256,256]{1,0:T(8,128)(2,1)S(1)} %copy-done.45, bf16[8192,256]{0,1:T(8,128)(2,1)S(1)} %copy-done.7, f32[8192,512]{0,1:T(8,128)} %fusion.117, f32[8192,768]{0,1:T(8,128)} %fusion.113), kind=kOutput, calls=%fused_computation.28 | convolution fusion | flops 1094713344 | bytes 29491200 | tf_op jit(solution)/shard_map/dot_general | solution.py:65
  371.3 9.0 %fusion.23 = f32[128,768]{1,0:T(8,128)} fusion(bf16[8192,256]{0,1:T(8,128)(2,1)S(1)} %copy-done.7, bf16[8192,256]{0,1:T(8,128)(2,1)} %fusion.3, bf16[8192,256]{0,1:T(8,128)(2,1)S(1)} %copy-done.6, f32[8192,128]{1,0:T(8,128)S(1)} %copy-done.3, f32[8192]{0:T(1024)S(1)} %copy-done.26), kind=kOutput, calls=%fused_computation.52 | convolution fusion | flops 1650458624 | bytes 17203200 | tf_op jit(solution)/shard_map/dot_general | solution.py:71
  380.3 6.7 %convolution_divide_fusion = f32[8192,128]{1,0:T(8,128)} fusion(bf16[128,768]{1,0:T(8,128)(2,1)S(1)} %copy-done.28, bf16[8192,256]{0,1:T(8,128)(2,1)S(1)} %copy-done.8, bf16[8192,256]{0,1:T(8,128)(2,1)S(1)} %copy-done.46, bf16[8192,256]{0,1:T(8,128)(2,1)S(1)} %copy-done.6, f32[8192]{0:T(1024)S(1)} %copy-done.26), kind=kOutput, calls=%fused_computation.29 | convolution fusion | flops 1649410048 | bytes 17006592 | tf_op jit(solution)/shard_map/dot_general | solution.py:73
  387.1 5.4 fusion.33
  392.5 3.2 gather_fusion.5
  398.2 135.9 %all-reduce.3.cloned.1.call-done = (f32[512,128]{1,0:T(8,128)}, f32[128,768]{1,0:T(8,128)}, f32[256,512]{0,1:T(8,128)}, f32[256,256]{1,0:T(8,128)}, f32[256,256]...) async-done(((f32[512,128]{1,0:T(8,128)}, f32[128,768]{1,0:T(8,128)}, f32[256,512]{0,1:T(8,128)}, f32[256,256]{1,0:T(8,128)}, f32[256,256]{1,0:T(8,128)}, ...) | async-done | bytes 2228240 | tf_op jit(solution)/shard_map/psum | solution.py:262
  534.1 2.0 copy.105
  536.1 1.7 copy.164
  537.8 1.8 copy.165
  539.6 1.7 copy.166
  541.3 1.7 copy.167
  544.6 1.7 copy.169
  (195 shorter events, 38.1 us)
Async XLA Ops:
  7.2 32.5 %copy-start = (bf16[256,512]{1,0:T(8,128)(2,1)S(1)}, bf16[256,512]{1,0:T(8,128)(2,1)}, u32[]{:S(2)}) copy-start(bf16[256,512]{1,0:T(8,128)(2,1)} %param.28) | copy-start | bytes 786436
  15.1 48.1 %all-to-all-start = ((s32[32,2,8]{2,1,0:T(2,128)}), s32[32,2,8]{2,1,0:T(2,128)S(1)}, u32[]{:S(2)}, u32[]{:S(2)}) async-start(s32[32,2,8]{2,1,0:T(2,128)} %copy.87), calls=%async_computation | async-start | bytes 65536 | tf_op jit(solution)/shard_map/all_to_all | solution.py:189
  39.6 132.1 %copy-start.37 = (s32[1280]{0:T(1024)}, s32[1280]{0:T(1024)S(1)}, u32[]{:S(2)}) copy-start(s32[1280]{0:T(1024)S(1)} %fusion.91) | copy-start | bytes 15364
  49.9 41.0 %copy-start.43 = (bf16[512,128]{1,0:T(8,128)(2,1)S(1)}, bf16[512,128]{1,0:T(8,128)(2,1)}, u32[]{:S(2)}) copy-start(bf16[512,128]{1,0:T(8,128)(2,1)} %param.26) | copy-start | bytes 393220
  49.9 46.7 %copy-start.27 = (bf16[128,768]{1,0:T(8,128)(2,1)S(1)}, bf16[128,768]{1,0:T(8,128)(2,1)}, u32[]{:S(2)}) copy-start(bf16[128,768]{1,0:T(8,128)(2,1)} %param.27) | copy-start | bytes 589828
  63.2 13.1 %all-to-all-start.2 = ((s32[32,2,8]{2,1,0:T(2,128)}), s32[32,2,8]{2,1,0:T(2,128)S(1)}, u32[]{:S(2)}, u32[]{:S(2)}) async-start(s32[32,2,8]{2,1,0:T(2,128)} %copy.90), calls=%async_computation.2 | async-start | bytes 65536 | tf_op jit(solution)/shard_map/all_to_all | solution.py:190
  69.2 39.2 %copy-start.40 = (f32[512]{0:T(512)}, f32[512]{0:T(512)S(1)}, u32[]{:S(2)}) copy-start(f32[512]{0:T(512)S(1)} %reshape.286) | copy-start | bytes 6148
  72.7 35.8 %copy-start.35 = (pred[8192]{0:T(1024)(128)(4,1)}, pred[8192]{0:T(1024)(128)(4,1)S(1)}, u32[]{:S(2)}) copy-start(pred[8192]{0:T(1024)(128)(4,1)S(1)} %broadcast_compare_fusion) | copy-start | bytes 24580
  72.7 35.7 %copy-start.25 = (f32[8192]{0:T(1024)}, f32[8192]{0:T(1024)S(1)}, u32[]{:S(2)}) copy-start(f32[8192]{0:T(1024)S(1)} %broadcast_maximum_fusion) | copy-start | bytes 98308
  73.4 14.4 %copy-start.38 = (s32[1024]{0:T(1024)}, s32[1024]{0:T(1024)S(1)}, u32[]{:S(2)}) copy-start(s32[1024]{0:T(1024)S(1)} %pad_clamp_fusion.4) | copy-start | bytes 12292
  76.3 11.4 %all-to-all-start.1 = ((bf16[32,2,8,128]{3,2,1,0:T(8,128)(2,1)}), bf16[32,2,8,128]{3,2,1,0:T(8,128)(2,1)S(1)}, u32[]{:S(2)}, u32[]{:S(2)}) async-start(bf16[32,2,8,128]{3,2,1,0:T(8,128)(2,1)} %pad_maximum_fusion.6), calls=%async_computation.1 | async-start | bytes 262144 | tf_op jit(solution)/shard_map/all_to_all | solution.py:201
  84.0 24.5 %copy-start.23 = (bf16[512,256]{1,0:T(8,128)(2,1)}, bf16[512,256]{1,0:T(8,128)(2,1)S(1)}, u32[]{:S(2)}) copy-start(bf16[512,256]{1,0:T(8,128)(2,1)S(1)} %gather_fusion) | copy-start | bytes 786436
  84.9 23.6 %copy-start.31 = (bf16[512,128]{1,0:T(8,128)(2,1)}, bf16[512,128]{1,0:T(8,128)(2,1)S(1)}, u32[]{:S(2)}) copy-start(bf16[512,128]{1,0:T(8,128)(2,1)S(1)} %cosine_convert_fusion) | copy-start | bytes 393220
  87.8 20.7 %copy-start.29 = (bf16[32,2,8,128]{3,2,1,0:T(8,128)(2,1)}, bf16[32,2,8,128]{3,2,1,0:T(8,128)(2,1)S(1)}, u32[]{:S(2)}) copy-start(bf16[32,2,8,128]{3,2,1,0:T(8,128)(2,1)S(1)} %all-to-all-done.1) | copy-start | bytes 393220
  87.8 51.4 %all-to-all-start.4 = ((s32[32,1,80]{2,1,0:T(1,128)}), s32[32,1,80]{2,1,0:T(1,128)S(1)}, u32[]{:S(2)}, u32[]{:S(2)}) async-start(s32[32,1,80]{2,1,0:T(1,128)} %all_to_all.31), calls=%async_computation.4 | async-start | bytes 32768 | tf_op jit(solution)/shard_map/all_to_all | solution.py:191
  91.2 17.3 %copy-start.21 = (f32[512,128]{1,0:T(8,128)}, f32[512,128]{1,0:T(8,128)S(1)}, u32[]{:S(2)}) copy-start(f32[512,128]{1,0:T(8,128)S(1)} %fusion.59) | copy-start | bytes 786436
  96.6 11.9 %copy-start.4 = (bf16[8192,256]{0,1:T(8,128)(2,1)S(1)}, bf16[8192,256]{0,1:T(8,128)(2,1)}, u32[]{:S(2)}) copy-start(bf16[8192,256]{0,1:T(8,128)(2,1)} %copy.91) | copy-start | bytes 12582916
  96.6 11.9 %copy-start.44 = (bf16[256,256]{1,0:T(8,128)(2,1)S(1)}, bf16[256,256]{1,0:T(8,128)(2,1)}, u32[]{:S(2)}) copy-start(bf16[256,256]{1,0:T(8,128)(2,1)} %param.29) | copy-start | bytes 393220
  134.8 36.9 %copy-start.16 = (bf16[128,256]{1,0:T(8,128)(2,1)S(1)}, bf16[128,256]{1,0:T(8,128)(2,1)}, u32[]{:S(2)}) copy-start(bf16[128,256]{1,0:T(8,128)(2,1)} %param.33) | copy-start | bytes 196612
  134.8 37.9 %copy-start.18 = (bf16[256,256]{1,0:T(8,128)(2,1)S(1)}, bf16[256,256]{1,0:T(8,128)(2,1)}, u32[]{:S(2)}) copy-start(bf16[256,256]{1,0:T(8,128)(2,1)} %param.30) | copy-start | bytes 393220
  139.2 16.0 %all-to-all-start.3 = ((bf16[32,8,256]{2,1,0:T(8,128)(2,1)}), bf16[32,8,256]{2,1,0:T(8,128)(2,1)S(1)}, u32[]{:S(2)}, u32[]{:S(2)}) async-start(bf16[32,8,256]{2,1,0:T(8,128)(2,1)} %bitcast.11), calls=%async_computation.3 | async-start | bytes 262144 | tf_op jit(solution)/shard_map/all_to_all | solution.py:221
  145.6 61.9 %copy-start.20 = (bf16[256,256]{1,0:T(8,128)(2,1)S(1)}, bf16[256,256]{1,0:T(8,128)(2,1)}, u32[]{:S(2)}) copy-start(bf16[256,256]{1,0:T(8,128)(2,1)} %param.32) | copy-start | bytes 393220
  155.1 53.6 %copy-start.19 = (bf16[256,256]{1,0:T(8,128)(2,1)S(1)}, bf16[256,256]{1,0:T(8,128)(2,1)}, u32[]{:S(2)}) copy-start(bf16[256,256]{1,0:T(8,128)(2,1)} %param.31) | copy-start | bytes 393220
  155.1 48.3 %all-to-all-start.5 = ((bf16[32,80,256]{2,1,0:T(8,128)(2,1)}), bf16[32,80,256]{2,1,0:T(8,128)(2,1)S(1)}, u32[]{:S(2)}, u32[]{:S(2)}) async-start(bf16[32,80,256]{2,1,0:T(8,128)(2,1)} %bitcast.15), calls=%async_computation.5 | async-start | bytes 2621440 | tf_op jit(solution)/shard_map/all_to_all | solution.py:222
  172.6 38.6 %copy-start.11 = (bf16[128,256]{1,0:T(8,128)(2,1)}, bf16[128,256]{1,0:T(8,128)(2,1)S(1)}, u32[]{:S(2)}) copy-start(bf16[128,256]{1,0:T(8,128)(2,1)S(1)} %gather_fusion.2) | copy-start | bytes 196612
  214.8 20.6 %all-to-all-start.6 = ((f32[32,8,256]{2,1,0:T(8,128)}), f32[32,8,256]{2,1,0:T(8,128)S(1)}, u32[]{:S(2)}, u32[]{:S(2)}) async-start(f32[32,8,256]{2,1,0:T(8,128)} %bitcast.25), calls=%async_computation.6 | async-start | bytes 524288 | tf_op jit(solution)/shard_map/all_to_all | solution.py:236
  219.7 21.7 %copy-start.33 = (s32[32,1,8]{2,1,0:T(1,128)S(1)}, s32[32,1,8]{2,1,0:T(1,128)}, u32[]{:S(2)}) copy-start(s32[32,1,8]{2,1,0:T(1,128)} %get-tuple-element.65) | copy-start | bytes 3076
  235.4 66.0 %all-to-all-start.7 = ((f32[32,80,256]{2,1,0:T(8,128)}), f32[32,80,256]{2,1,0:T(8,128)S(1)}, u32[]{:S(2)}, u32[]{:S(2)}) async-start(f32[32,80,256]{2,1,0:T(8,128)} %bitcast.29), calls=%async_computation.7 | async-start | bytes 5242880 | tf_op jit(solution)/shard_map/all_to_all | solution.py:243
  241.3 292.8 %all-reduce.3.cloned.1.call-start = ((), (), s32[]{:S(2)}) async-start(), calls=%async_computation.8 | async-start | bytes 4456448 | tf_op jit(solution)/shard_map/psum | solution.py:262
  324.8 8.9 %copy-start.36 = (pred[8192]{0:T(1024)(128)(4,1)S(1)}, pred[8192]{0:T(1024)(128)(4,1)}, u32[]{:S(2)}) copy-start(pred[8192]{0:T(1024)(128)(4,1)} %copy-done.35) | copy-start | bytes 24580
  333.7 17.8 %copy-start.5 = (bf16[8192,256]{0,1:T(8,128)(2,1)S(1)}, bf16[8192,256]{0,1:T(8,128)(2,1)}, u32[]{:S(2)}) copy-start(bf16[8192,256]{0,1:T(8,128)(2,1)} %copy.91) | copy-start | bytes 12582916
  351.6 10.3 %copy-start.7 = (bf16[8192,256]{0,1:T(8,128)(2,1)S(1)}, bf16[8192,256]{0,1:T(8,128)(2,1)}, u32[]{:S(2)}) copy-start(bf16[8192,256]{0,1:T(8,128)(2,1)} %get-tuple-element.64) | copy-start | bytes 12582916
  351.6 10.3 %copy-start.45 = (bf16[256,256]{1,0:T(8,128)(2,1)S(1)}, bf16[256,256]{1,0:T(8,128)(2,1)}, u32[]{:S(2)}) copy-start(bf16[256,256]{1,0:T(8,128)(2,1)} %param.29) | copy-start | bytes 393220
  361.9 9.2 %copy-start.3 = (f32[8192,128]{1,0:T(8,128)S(1)}, f32[8192,128]{1,0:T(8,128)}, u32[]{:S(2)}) copy-start(f32[8192,128]{1,0:T(8,128)} %scatter_custom_fusion.7) | copy-start | bytes 12582916
  361.9 9.4 %copy-start.6 = (bf16[8192,256]{0,1:T(8,128)(2,1)S(1)}, bf16[8192,256]{0,1:T(8,128)(2,1)}, u32[]{:S(2)}) copy-start(bf16[8192,256]{0,1:T(8,128)(2,1)} %get-tuple-element.63) | copy-start | bytes 12582916
  361.9 9.4 %copy-start.26 = (f32[8192]{0:T(1024)S(1)}, f32[8192]{0:T(1024)}, u32[]{:S(2)}) copy-start(f32[8192]{0:T(1024)} %copy-done.25) | copy-start | bytes 98308
  371.3 9.0 %copy-start.8 = (bf16[8192,256]{0,1:T(8,128)(2,1)S(1)}, bf16[8192,256]{0,1:T(8,128)(2,1)}, u32[]{:S(2)}) copy-start(bf16[8192,256]{0,1:T(8,128)(2,1)} %get-tuple-element.64) | copy-start | bytes 12582916
  371.3 9.0 %copy-start.28 = (bf16[128,768]{1,0:T(8,128)(2,1)S(1)}, bf16[128,768]{1,0:T(8,128)(2,1)}, u32[]{:S(2)}) copy-start(bf16[128,768]{1,0:T(8,128)(2,1)} %param.27) | copy-start | bytes 589828
  371.3 9.0 %copy-start.46 = (bf16[8192,256]{0,1:T(8,128)(2,1)S(1)}, bf16[8192,256]{0,1:T(8,128)(2,1)}, u32[]{:S(2)}) copy-start(bf16[8192,256]{0,1:T(8,128)(2,1)} %fusion.3) | copy-start | bytes 12582916
  380.3 6.7 %copy-start.2 = (bf16[8192,256]{1,0:T(8,128)(2,1)S(1)}, bf16[8192,256]{1,0:T(8,128)(2,1)}, u32[]{:S(2)}) copy-start(bf16[8192,256]{1,0:T(8,128)(2,1)} %param.17) | copy-start | bytes 12582916
  387.0 8.8 %copy-start.22 = (f32[512,128]{1,0:T(8,128)S(1)}, f32[512,128]{1,0:T(8,128)}, u32[]{:S(2)}) copy-start(f32[512,128]{1,0:T(8,128)} %copy-done.21) | copy-start | bytes 786436
  387.0 8.8 %copy-start.24 = (bf16[512,256]{1,0:T(8,128)(2,1)S(1)}, bf16[512,256]{1,0:T(8,128)(2,1)}, u32[]{:S(2)}) copy-start(bf16[512,256]{1,0:T(8,128)(2,1)} %copy-done.23) | copy-start | bytes 786436
  387.0 8.8 %copy-start.30 = (bf16[32,2,8,128]{3,2,1,0:T(8,128)(2,1)S(1)}, bf16[32,2,8,128]{3,2,1,0:T(8,128)(2,1)}, u32[]{:S(2)}) copy-start(bf16[32,2,8,128]{3,2,1,0:T(8,128)(2,1)} %copy-done.29) | copy-start | bytes 393220
  387.0 8.8 %copy-start.32 = (bf16[512,128]{1,0:T(8,128)(2,1)S(1)}, bf16[512,128]{1,0:T(8,128)(2,1)}, u32[]{:S(2)}) copy-start(bf16[512,128]{1,0:T(8,128)(2,1)} %copy-done.31) | copy-start | bytes 393220
  387.0 8.8 %copy-start.41 = (f32[512]{0:T(512)S(1)}, f32[512]{0:T(512)}, u32[]{:S(2)}) copy-start(f32[512]{0:T(512)} %copy-done.40) | copy-start | bytes 6148
  387.1 9.9 %copy-start.34 = (bf16[128,2,10]{0,1,2:T(2,128)(2,1)S(1)}, bf16[128,2,10]{0,1,2:T(2,128)(2,1)}, u32[]{:S(2)}) copy-start(bf16[128,2,10]{0,1,2:T(2,128)(2,1)} %get-tuple-element.70) | copy-start | bytes 15364
  387.1 10.1 %copy-start.14 = (bf16[128,10,2,128]{3,2,1,0:T(2,128)(2,1)S(1)}, bf16[128,10,2,128]{3,2,1,0:T(2,128)(2,1)}, u32[]{:S(2)}) copy-start(bf16[128,10,2,128]{3,2,1,0:T(2,128)(2,1)} %copy-done.13) | copy-start | bytes 1966084
  387.1 159.2 %copy-start.1 = (bf16[256,512]{1,0:T(8,128)(2,1)S(1)}, bf16[256,512]{1,0:T(8,128)(2,1)}, u32[]{:S(2)}) copy-start(bf16[256,512]{1,0:T(8,128)(2,1)} %param.28) | copy-start | bytes 786436
  (8 other events, 26.9 us)
Sparse Core Ops, SparseCore 0:
  397.1 136.9 all-reduce.2
where the time goes:
time: 563 us; the launch traced here: 554 us
  waiting for transfers between devices  223 us (40%)
  matrix products  96 us (17%)
  local copies, waits for them, and re-layouts  93.5 us (17%)
  other arithmetic  74.1 us (13%)
  starting transfers between devices  51.1 us (9%)
  between operations  15.4 us (3%)
    psum x1, waiting for transfers between devices, body(): lax.psum((grad_msg, grad_in, grad_zr, grad_h, grad_query, grad_key, grad_...  136 us
    all_to_all x1, waiting for transfers between devices, body(): lax.all_to_all(nb_grads.reshape(devices, cap_neigh, row_width), ('acct',...  51.2 us
    all_to_all x1, waiting for transfers between devices, body(): lax.all_to_all(nb_reply, ('acct', 'rep'), split_axis=0, concat_axis=0, ti...  30.5 us
    unnamed x105, local copies, waits for them, and re-layouts  27 us
    add x1, other arithmetic, body(): d_memory + jax.ops.segment_sum(got_nb_grads.reshape(-1, row_width), nb_ro...  23.4 us
    dot_general x1, matrix products, gru_forward(): jnp.dot(reset_state, u_h, preferred_element_type=jnp.float32)  19.9 us
    convert_element_type x1, other arithmetic, gru_backward(): d_update_in.astype(jnp.bfloat16)  17.8 us
    all_to_all x1, starting transfers between devices, body(): lax.all_to_all(nb_reply, ('acct', 'rep'), split_axis=0, concat_axis=0, ti...  16.5 us
  transfers between devices with their start and end apart: 9, of which 5 were waited for; matrix products, arithmetic and copies ran while one was open for 24% of the time, Pallas kernels for 0%

commit v1 on v0

v1 whole, which is shorter than its diff:
```python
import functools
import math

import jax
import jax.numpy as jnp
from jax import lax
from jax.experimental import pallas as pl
from jax.experimental.pallas import tpu as pltpu
from jax.sharding import PartitionSpec as P

HEADS = 2
AXES = ("acct", "rep")
CAP_VALUE = 10.0
F32 = jnp.float32
BF16 = jnp.bfloat16
I32 = jnp.int32
EXACT = lax.Precision.HIGHEST
VMEM_LIMIT = 56 * 1024 * 1024


def dot(a, b, **kw):
    return jnp.dot(a, b, preferred_element_type=F32, **kw)


def dot_nt(a, b, **kw):
    return lax.dot_general(a, b, (((1,), (1,)), ((), ())), preferred_element_type=F32, **kw)


def dot_tn(a, b, **kw):
    return lax.dot_general(a, b, (((0,), (0,)), ((), ())), preferred_element_type=F32, **kw)


def iota(shape, axis):
    return lax.broadcasted_iota(I32, shape, axis)


def sigmoid(v):
    return 1.0 / (1.0 + jnp.exp(-v))


def call(body, outs, args, name, scratch=(), cost=None):
    vm = pl.BlockSpec(memory_space=pltpu.VMEM)
    return pl.pallas_call(
        body,
        out_shape=[jax.ShapeDtypeStruct(s, d) for s, d in outs],
        in_specs=[vm] * len(args),
        out_specs=[vm] * len(outs),
        scratch_shapes=list(scratch),
        compiler_params=pltpu.CompilerParams(vmem_limit_bytes=VMEM_LIMIT),
        cost_estimate=cost,
        name=name,
    )(*args)


def place_body(ce, cn, devices, so, ss, do, ds, no, ns, bk, feat, req, feats, dplace, nrank):
    events = so.shape[1]
    neighbours = no.shape[0]
    upper = (iota((events, events), 0) < iota((events, events), 1)).astype(BF16)
    own = iota((devices, events), 0)
    rows = iota((2 * devices * ce, events), 0)

    def fill(onehot, rank, value, cap):
        hits = (iota((cap, events), 0) == rank).astype(F32)
        return dot_nt(onehot, hits * value.astype(F32), precision=EXACT)

    chosen = jnp.zeros((2 * devices * ce, events), F32)
    for side, (o_ref, s_ref) in enumerate(((so, ss), (do, ds))):
        owner = o_ref[...]
        onehot = (own == owner).astype(F32)
        before = dot(onehot.astype(BF16), upper)
        rank = jnp.sum(onehot * before, axis=0, keepdims=True).astype(I32)
        req[:, side * ce : (side + 1) * ce] = (
            fill(onehot, rank, s_ref[...] + 1, ce).astype(I32) - 1
        )
        req[:, (2 + side) * ce : (3 + side) * ce] = fill(onehot, rank, bk[...], ce).astype(I32)
        chosen = chosen + (rows == owner * (2 * ce) + (side * ce + rank)).astype(F32)
        if side == 1:
            dplace[...] = owner * ce + rank
    feats[...] = dot(chosen.astype(BF16), feat[...]).astype(BF16)
    base = jnp.zeros((devices, 1), F32)
    total = jnp.zeros((devices, cn), F32)
    event = iota((1, events), 1)
    for k in range(neighbours):
        onehot = (own == no[k : k + 1, :]).astype(F32)
        before = dot(onehot.astype(BF16), upper) + base
        rank = jnp.sum(onehot * before, axis=0, keepdims=True).astype(I32)
        nrank[k : k + 1, :] = rank
        base = base + jnp.sum(onehot, axis=1, keepdims=True)
        total = total + fill(onehot, rank, ns[k : k + 1, :] * events + event + 1, cn)
    req[:, 4 * ce : 4 * ce + cn] = total.astype(I32) - 1


def owner_body(
    ce, rows, feats, scol, srow, bcol, w_msg, w_in, u_zr, u_h,
    new, dst_new, sfirst, fcol, code, pre, mean, div, upd, rst, cand, rstate, msg,
):
    n, m = rows.shape
    f = feats.shape[1]
    t = w_msg.shape[0] - m - f
    step = 128
    frequency = jnp.exp(iota((1, t), 1).astype(F32) * (-11.5 / t))

    def messages(i, carry):
        b = pl.ds(pl.multiple_of(i * step, step), step)
        enc = jnp.cos(bcol[b, :].astype(F32) * frequency).astype(BF16)
        code[b, :] = enc
        act = (
            dot(rows[b, :], w_msg[:m, :]) + dot(feats[b, :], w_msg[m : m + f, :])
        ) + dot(enc, w_msg[m + f :, :])
        pre[b, :] = act
        msg[b, :] = (act * sigmoid(act)).astype(BF16)
        return carry

    lax.fori_loop(0, n // step, messages, 0)
    slots = srow[...]

    def gru(i, early):
        b = pl.ds(pl.multiple_of(i * step, step), step)
        mine = scol[b, :]
        same = (mine == slots) & (mine >= 0)
        eq = same.astype(F32)
        eq_b = eq.astype(BF16)
        counts = dot(eq_b, jnp.ones((n, msg.shape[1]), BF16))
        divisor = jnp.maximum(counts, 1.0)
        div[b, :] = divisor
        earlier = jnp.where(iota((step, n), 1) < iota((step, n), 0) + i * step, eq, 0.0)
        fcol[b, :] = (jnp.sum(earlier, axis=1, keepdims=True) < 0.5).astype(F32)
        later = jnp.where(iota((step, n), 1) > iota((step, n), 0) + i * step, eq, 0.0)
        early = early + jnp.sum(later, axis=0, keepdims=True)
        mean_b = (dot(eq_b, msg[...]) / divisor).astype(BF16)
        mean[b, :] = mean_b
        state = rows[b, :]
        state_wide = state.astype(F32)
        from_input = dot(mean_b, w_in[...])
        from_state = dot(state, u_zr[...])
        update = sigmoid(from_input[:, :m] + from_state[:, :m])
        reset = sigmoid(from_input[:, m : 2 * m] + from_state[:, m:])
        reset_state = (reset * state_wide).astype(BF16)
        candidate = jnp.tanh(from_input[:, 2 * m :] + dot(reset_state, u_h[...]))
        upd[b, :] = update
        rst[b, :] = reset
        cand[b, :] = candidate
        rstate[b, :] = reset_state
        new[b, :] = ((1.0 - update) * state_wide + update * candidate).astype(BF16)
        return early

    early = lax.fori_loop(0, n // step, gru, jnp.zeros((1, n), F32))
    sfirst[...] = jnp.where(early < 0.5, slots, -2)
    half = n // 2
    r = iota((half, n), 0)
    pick = (iota((half, n), 1) == r + (r // ce + 1) * ce).astype(F32).astype(BF16)
    dst_new[...] = dot(pick, new[...]).astype(BF16)


def patch_body(old, ncol, sfirst, new, out):
    hit = (ncol[...] == sfirst[...]).astype(F32).astype(BF16)
    rows = dot(hit, new[...])
    found = dot(hit, jnp.ones((new.shape[0], 128), BF16)) > 0.5
    for h in range(rows.shape[1] // 128):
        c = slice(h * 128, (h + 1) * 128)
        out[:, c] = jnp.where(found, rows[:, c], old[:, c].astype(F32)).astype(BF16)


def patch(old, ncol, sfirst, new):
    n, m = old.shape
    s = new.shape[0]
    block = 512
    return pl.pallas_call(
        patch_body,
        grid=(n // block,),
        out_shape=jax.ShapeDtypeStruct((n, m), BF16),
        in_specs=[
            pl.BlockSpec((block, m), lambda i: (i, 0)),
            pl.BlockSpec((block, 1), lambda i: (i, 0)),
            pl.BlockSpec((1, s), lambda i: (0, 0)),
            pl.BlockSpec((s, m), lambda i: (0, 0)),
        ],
        out_specs=pl.BlockSpec((block, m), lambda i: (i, 0)),
        name="patch",
    )(old, ncol, sfirst, new)


def query_body(back, dplace, w_query, q_rows, q_proj):
    n = back.shape[0]
    events = dplace.shape[1]
    pick = (iota((n, events), 0) == dplace[...]).astype(F32).astype(BF16)
    q = dot_tn(pick, back[...]).astype(BF16)
    q_rows[...] = q
    q_proj[...] = dot(q, w_query[...]).astype(BF16)


def attend_body(
    cn, devices, keys, q_rows, q_proj, grad, w_query, w_key, w_value, dplace, no, nrank,
    emb, dq_out, scal, g_qkv, kp, vp, dk, dv,
):
    events, m = q_rows.shape
    neighbours = no.shape[0]
    hs = m // HEADS
    scaling = 1.0 / math.sqrt(hs)
    qf = q_proj[...].astype(F32)
    gf = grad[...].astype(F32)
    lane = iota((events, 128), 1)
    raw = jnp.zeros((events, 128), F32)
    probs = jnp.zeros((events, 128), F32)
    for k in range(neighbours):
        b = slice(k * events, (k + 1) * events)
        rows = keys[b, :]
        kpk = dot(rows, w_key[...]).astype(BF16)
        vpk = dot(rows, w_value[...]).astype(BF16)
        kp[b, :] = kpk
        vp[b, :] = vpk
        pk = qf * kpk.astype(F32)
        pv = gf * vpk.astype(F32)
        for h in range(HEADS):
            c = slice(h * hs, (h + 1) * hs)
            at = lane == h * 64 + k
            raw = jnp.where(at, jnp.sum(pk[:, c], axis=1, keepdims=True), raw)
            probs = jnp.where(at, jnp.sum(pv[:, c], axis=1, keepdims=True), probs)
    raw = raw * scaling
    capped = jnp.tanh(raw / CAP_VALUE)
    first = lane < 64
    live = jnp.where(first, lane, lane - 64) < neighbours
    weights = jnp.where(live, jnp.exp(CAP_VALUE * capped), 0.0)

    def per_head(v):
        a = jnp.sum(jnp.where(first, v, 0.0), axis=1, keepdims=True)
        b = jnp.sum(jnp.where(first, 0.0, v), axis=1, keepdims=True)
        return jnp.where(first, a, b)

    attention = weights / per_head(weights)
    att_b = attention.astype(BF16).astype(F32)
    d_scores = attention * (probs - per_head(attention * probs))
    d_raw = d_scores * (1.0 - capped * capped) * scaling
    mix = [jnp.zeros((events, hs), F32) for _ in range(HEADS)]
    dq = [jnp.zeros((events, hs), F32) for _ in range(HEADS)]
    for k in range(neighbours):
        b = slice(k * events, (k + 1) * events)
        for h in range(HEADS):
            c = slice(h * hs, (h + 1) * hs)
            i = h * 64 + k
            a = att_b[:, i : i + 1]
            d = d_raw[:, i : i + 1]
            mix[h] = mix[h] + a * vp[b, c].astype(F32)
            dq[h] = dq[h] + d * kp[b, c].astype(F32)
            dk[b, c] = (d * qf[:, c]).astype(BF16)
            dv[b, c] = (a * gf[:, c]).astype(BF16)
    q = q_rows[...]
    dq_b = jnp.concatenate(dq, axis=1).astype(BF16)
    emb[...] = (q.astype(F32) + jnp.concatenate(mix, axis=1)).astype(BF16)
    g_qkv[0:m, :] = dot_tn(q, dq_b).astype(BF16)
    g_qkv[m : 2 * m, :] = dot_tn(keys[...], dk[...]).astype(BF16)
    g_qkv[2 * m : 3 * m, :] = dot_tn(keys[...], dv[...]).astype(BF16)
    d_rows = (gf + dot_nt(dq_b, w_query[...])).astype(BF16)
    spots = (iota((dq_out.shape[0], events), 0) == dplace[...]).astype(F32).astype(BF16)
    dq_out[...] = dot(spots, d_rows).astype(BF16)
    att_t = att_b.T
    raw_t = d_raw.T
    own = iota((devices, events), 0)
    total = jnp.zeros((devices, 4 * cn), F32)
    for k in range(neighbours):
        onehot = (own == no[k : k + 1, :]).astype(F32).astype(BF16)
        hits = (iota((cn, events), 0) == nrank[k : k + 1, :]).astype(F32)
        values = jnp.concatenate(
            [
                hits * raw_t[k : k + 1, :],
                hits * raw_t[64 + k : 65 + k, :],
                hits * att_t[k : k + 1, :],
                hits * att_t[64 + k : 65 + k, :],
            ],
            axis=0,
        ).astype(BF16)
        total = total + dot_nt(onehot, values)
    scal[...] = total.astype(BF16)


def back_body(
    scal, nrow, qe, ge, dq, drow, scol, fcol, rows, feats, code, pre, mean, div,
    upd, rst, cand, rstate, w_in, u_h, w_key, w_value, out, gates, dpre,
):
    n, m = rows.shape
    f = feats.shape[1]
    hs = m // HEADS
    step = 256
    s = mean.shape[1]

    def block(i, carry):
        b = pl.ds(pl.multiple_of(i * step, step), step)
        mine = scol[b, :]
        mine = jnp.where(mine >= 0, mine, -7)
        hit = mine == nrow[...]
        parts = []
        for j in range(4):
            src = qe if j < 2 else ge
            h = j % 2
            a = jnp.where(hit, scal[j : j + 1, :].astype(F32), 0.0).astype(BF16)
            parts.append(dot(a, src[:, h * hs : (h + 1) * hs]).astype(BF16))
        dkey = jnp.concatenate(parts[:2], axis=1)
        dval = jnp.concatenate(parts[2:], axis=1)
        here = (mine == drow[...]).astype(F32).astype(BF16)
        du = dot(here, dq[...]) + dot_nt(dkey, w_key[...]) + dot_nt(dval, w_value[...])
        state = rows[b, :].astype(F32)
        update = upd[b, :]
        reset = rst[b, :]
        candidate = cand[b, :]
        d_cand = (du * update * (1.0 - candidate * candidate)).astype(BF16)
        d_reset = dot_nt(d_cand, u_h[...]) * state * reset * (1.0 - reset)
        d_update = du * (candidate - state) * update * (1.0 - update)
        d_gates = jnp.concatenate([d_update.astype(BF16), d_reset.astype(BF16), d_cand], axis=1)
        d_mean = dot_nt(d_gates, w_in[...]) / div[b, :]
        act = pre[b, :]
        sg = sigmoid(act)
        dpre[b, :] = (d_mean * sg * (1.0 + act * (1.0 - sg))).astype(BF16)
        gates[b, :] = jnp.where(fcol[b, :] > 0.5, d_gates.astype(F32), 0.0).astype(BF16)
        return carry

    lax.fori_loop(0, n // step, block, 0)
    at = 0
    g_in = dot_tn(mean[...], gates[...])
    for j in range(3):
        out[at : at + s, :] = g_in[:, j * m : (j + 1) * m].astype(BF16)
        at += s
    g_zr = dot_tn(rows[...], gates[:, : 2 * m])
    for j in range(2):
        out[at : at + m, :] = g_zr[:, j * m : (j + 1) * m].astype(BF16)
        at += m
    out[at : at + m, :] = dot_tn(rstate[...], gates[:, 2 * m :]).astype(BF16)
    at += m
    out[at : at + m, :s] = dot_tn(rows[...], dpre[...]).astype(BF16)
    out[at : at + f, s:] = dot_tn(feats[...], dpre[...]).astype(BF16)
    out[at + f : at + m, s:] = dot_tn(code[...], dpre[...]).astype(BF16)


def unpack_body(x, g_msg, g_in, g_zr, g_h, g_q, g_k, g_v):
    m = g_h.shape[0]
    s = g_in.shape[0]
    at = 0
    for j in range(3):
        g_in[:, j * m : (j + 1) * m] = x[at : at + s, :].astype(F32)
        at += s
    for j in range(2):
        g_zr[:, j * m : (j + 1) * m] = x[at : at + m, :].astype(F32)
        at += m
    g_h[...] = x[at : at + m, :].astype(F32)
    at += m
    g_msg[:m, :] = x[at : at + m, :s].astype(F32)
    g_msg[m:, :] = x[at : at + m, s:].astype(F32)
    at += m
    for ref in (g_q, g_k, g_v):
        ref[...] = x[at : at + m, :].astype(F32)
        at += m


def exchange(x):
    return lax.all_to_all(x, AXES, split_axis=0, concat_axis=0, tiled=True)


def body(
    memory, features, buckets, src_owner, src_slot, dst_owner, dst_slot, nb_owner, nb_slot,
    w_msg, w_in, u_zr, u_h, w_query, w_key, w_value, emb_grad,
):
    devices = lax.axis_size(AXES)
    events, m = emb_grad.shape
    acc_rows = memory.shape[0]
    neighbours = nb_slot.shape[1]
    feat = features.shape[1]
    width = w_msg.shape[1]
    ce = 2 * events // devices
    cn = 2 * events * neighbours // devices
    n_dst = devices * ce
    n_side = 2 * n_dst
    n_nb = devices * cn
    grad_all = lax.all_gather(emb_grad, AXES, axis=0, tiled=True)
    no = nb_owner.reshape(events, neighbours).T
    req, side_feats, dplace, nrank = call(
        functools.partial(place_body, ce, cn, devices),
        [
            ((devices, 4 * ce + cn), I32),
            ((n_side, feat), BF16),
            ((1, events), I32),
            ((neighbours, events), I32),
        ],
        (
            src_owner.reshape(1, events), src_slot.reshape(1, events),
            dst_owner.reshape(1, events), dst_slot.reshape(1, events),
            no, nb_slot.T, buckets.reshape(1, events), features,
        ),
        "place",
    )
    got = exchange(req.reshape(devices, 1, 4 * ce + cn)).reshape(devices, 4 * ce + cn)
    got_feats = exchange(side_feats.reshape(devices, 2 * ce, feat)).reshape(n_side, feat)
    side_slots = got[:, : 2 * ce].reshape(n_side)
    side_times = got[:, 2 * ce : 4 * ce].reshape(n_side)
    dst_slots = got[:, ce : 2 * ce].reshape(n_dst)
    nb_code = got[:, 4 * ce :].reshape(n_nb)
    nb_slots = jnp.where(nb_code >= 0, nb_code // events, -1)
    nb_event = jnp.maximum(nb_code, 0) % events
    nb_table = nb_event + (jnp.arange(n_nb, dtype=I32) // cn) * events
    fetched = memory[jnp.maximum(side_slots, 0)]
    old_nb = memory[jnp.maximum(nb_slots, 0)]
    (
        new_side, dst_new, sfirst, fcol, code, pre, mean, div, upd, rst, cand, rstate,
    ) = call(
        functools.partial(owner_body, ce),
        [
            ((n_side, m), BF16), ((n_dst, m), BF16), ((1, n_side), I32), ((n_side, 1), F32),
            ((n_side, w_msg.shape[0] - m - feat), BF16), ((n_side, width), F32),
            ((n_side, width), BF16), ((n_side, width), F32),
            ((n_side, m), F32), ((n_side, m), F32), ((n_side, m), F32), ((n_side, m), BF16),
        ],
        (
            fetched, got_feats, side_slots.reshape(n_side, 1), side_slots.reshape(1, n_side),
            side_times.reshape(n_side, 1), w_msg, w_in, u_zr, u_h,
        ),
        "owner",
        scratch=[pltpu.VMEM((n_side, width), BF16)],
    )
    back_dst = exchange(dst_new.reshape(devices, ce, m)).reshape(n_dst, m)
    nb_reply = patch(old_nb, nb_slots.reshape(n_nb, 1), sfirst, new_side)
    back_nb = exchange(nb_reply.reshape(devices, cn, m)).reshape(n_nb, m)
    new_memory = memory.at[jnp.where(side_slots >= 0, side_slots, acc_rows)].set(
        new_side, mode="drop"
    )
    q_rows, q_proj = call(
        query_body,
        [((events, m), BF16), ((events, m), BF16)],
        (back_dst, dplace, w_query),
        "query",
    )
    proj_all = lax.all_gather(q_proj, AXES, axis=0, tiled=True)
    ge = grad_all[nb_table]
    nb_place = (no * cn + nrank).reshape(-1)
    keys = back_nb[nb_place]
    embedding, dq_out, scal, g_qkv = call(
        functools.partial(attend_body, cn, devices),
        [
            ((events, m), BF16), ((n_dst, m), BF16), ((devices, 4 * cn), BF16),
            ((3 * m, m), BF16),
        ],
        (keys, q_rows, q_proj, emb_grad, w_query, w_key, w_value, dplace, no, nrank),
        "attend",
        scratch=[pltpu.VMEM((events * neighbours, m), BF16)] * 4,
    )
    scal_got = exchange(scal.reshape(devices, 4, cn))
    dq_got = exchange(dq_out.reshape(devices, ce, m)).reshape(n_dst, m)
    qe = proj_all[nb_table]
    late = call(
        back_body,
        [((3 * width + 4 * m, m), BF16)],
        (
            scal_got.transpose(1, 0, 2).reshape(4, n_nb), nb_slots.reshape(1, n_nb), qe, ge,
            dq_got, dst_slots.reshape(1, n_dst), side_slots.reshape(n_side, 1), fcol, fetched,
            got_feats, code, pre, mean, div, upd, rst, cand, rstate, w_in, u_h, w_key, w_value,
        ),
        "back",
        scratch=[pltpu.VMEM((n_side, 3 * m), BF16), pltpu.VMEM((n_side, width), BF16)],
    )[0]
    grads = jnp.concatenate([late, g_qkv], axis=0)
    rows = grads.shape[0] // devices
    shares = exchange(grads.reshape(devices, rows, m))
    mine = jnp.sum(shares.astype(F32), axis=0).astype(BF16)
    whole = exchange(jnp.broadcast_to(mine[None], (devices, rows, m)))
    g_msg, g_in, g_zr, g_h, g_q, g_k, g_v = call(
        unpack_body,
        [
            ((w_msg.shape[0], width), F32), ((width, 3 * m), F32), ((m, 2 * m), F32),
            ((m, m), F32), ((m, m), F32), ((m, m), F32), ((m, m), F32),
        ],
        (whole.reshape(devices * rows, m),),
        "unpack",
    )
    return (new_memory, embedding, g_msg, g_in, g_zr, g_h, g_q, g_k, g_v)


def solution(mesh):
    split = P(AXES)
    return jax.shard_map(
        body,
        mesh=mesh,
        in_specs=(split,) * 9 + (P(),) * 7 + (split,),
        out_specs=(split, split) + (P(),) * 7,
        check_vma=False,
    )
```

time: 563 us -> 262 us (0.47); the launches traced: 554 us -> 261 us
  waiting for transfers between devices: 223 us -> 76.1 us
  matrix products: 96 us -> 0 us
  other arithmetic: 74.1 us -> 5.22 us
  blocking collectives: 0 us -> 50.5 us
  Pallas kernels: 0 us -> 35 us
  local copies, waits for them, and re-layouts: 93.5 us -> 59.5 us
  starting transfers between devices: 51.1 us -> 20.7 us
    psum x1 -> x0, waiting for transfers between devices: 136 us -> none  [body(): lax.psum((grad_msg, grad_in, grad_zr, grad_h, grad_query, grad_key, grad_...]
    dot_general x23 -> x0, matrix products: 96 us -> none  [the longest x1 19.9 us: gru_forward(): jnp.dot(reset_state, u_h, preferred_element_type=jnp.float32)]
    all_to_all x0 -> x2, blocking collectives: none -> 50.5 us  [exchange(): return lax.all_to_all(x, AXES, split_axis=0, concat_axis=0, tiled=True)]
    pallas_call x0 -> x7, Pallas kernels: none -> 35 us  [the longest x6 29.3 us: call(): pl.pallas_call(body, out_shape=[jax.ShapeDtypeStruct(s, d) for s, d in ou...]
    all_to_all x8 -> x6, starting transfers between devices: 51.1 us -> 20.6 us  [exchange(): return lax.all_to_all(x, AXES, split_axis=0, concat_axis=0, tiled=True)]
    convert_element_type x11 -> x0, other arithmetic: 24.6 us -> none  [the longest x1 17.8 us: gru_backward(): d_update_in.astype(jnp.bfloat16)]
    add x1 -> x0, other arithmetic: 23.4 us -> none  [body(): d_memory + jax.ops.segment_sum(got_nb_grads.reshape(-1, row_width), nb_ro...]
    unnamed x105 -> x16, local copies, waits for them, and re-layouts: 27 us -> 7.05 us
  transfers between devices with their start and end apart: 9 -> 8, of which waited for: 5 -> 5; matrix products, arithmetic and copies ran while one was open for 24% -> 21% of each run, Pallas kernels for 0% -> 9%
where the time goes in v1:
time: 262 us; the launch traced here: 261 us
  waiting for transfers between devices  76.1 us (29%)
  local copies, waits for them, and re-layouts  59.5 us (23%)
  blocking collectives  50.5 us (19%)
  Pallas kernels  35 us (13%)
  starting transfers between devices  20.7 us (8%)
  between operations  14.2 us (5%)
  other arithmetic  5.22 us (2%)
    all_to_all x6, waiting for transfers between devices, exchange(): return lax.all_to_all(x, AXES, split_axis=0, concat_axis=0, tiled=True)  76.1 us
    all_to_all x2, blocking collectives, exchange(): return lax.all_to_all(x, AXES, split_axis=0, concat_axis=0, tiled=True)  50.5 us
    pallas_call x6, Pallas kernels, call(): pl.pallas_call(body, out_shape=[jax.ShapeDtypeStruct(s, d) for s, d in ou...  29.3 us
    all_to_all x6, starting transfers between devices, exchange(): return lax.all_to_all(x, AXES, split_axis=0, concat_axis=0, tiled=True)  20.6 us
    gather x1, local copies, waits for them, and re-layouts, body(): old_nb = memory[jnp.maximum(nb_slots, 0)]  9.55 us
    gather x1, local copies, waits for them, and re-layouts, body(): ge = grad_all[nb_table]  8.66 us
    gather x1, local copies, waits for them, and re-layouts, body(): qe = proj_all[nb_table]  8.63 us
    scatter x1, local copies, waits for them, and re-layouts, body(): memory.at[jnp.where(side_slots >= 0, side_slots, acc_rows)]  7.37 us
  transfers between devices with their start and end apart: 8, of which 5 were waited for; matrix products, arithmetic and copies ran while one was open for 21% of the time, Pallas kernels for 9%

profile of v1, /device:TPU:0, one launch (start us, length us, event | category | flops | bytes accessed | tf_op | source)
XLA Modules:
  0.0 261.2 jit_solution(14396895362808574291)
XLA Ops:
  7.2 4.5 %copy.57 = bf16[8192,256]{1,0:T(8,128)(2,1)} copy(bf16[8192,256]{1,0:T(8,128)(2,1)} %param.17) | data formatting | bytes 8388608
  11.7 0.6 copy.54
  12.3 4.0 %place.1 = (s32[32,112]{1,0:T(8,128)}, bf16[512,128]{1,0:T(8,128)(2,1)}, s32[1,128]{1,0:T(1,128)}, s32[10,128]{1,0:T(8,128)}) custom-call(s32[1,128]{1,0:T(1,128)} %bitcast.53, s32[1,128]{1,0:T(1,128)} %bitcast.54, s32[1,128]{1,0:T(1,128)} %bitcast.55, s32[1,128]{1,0:T(1,128)} %bitcast.56, s32[10,128]{1,0:T(8,128)} %bitcast.47, s32[10,128]{1,0:T(8,128)} %bitcast.51, ...), custom_call_target="tpu_custom_call" | custom-call | tf_op jit(solution)/shard_map/place/pallas_call | solution.py:43
  16.4 14.4 %all_to_all.41 = s32[32,1,112]{2,1,0:T(1,128)S(1)} all-to-all(s32[32,1,112]{2,1,0:T(1,128)} %bitcast.49), channel_id=1, replica_groups=mesh['acct'=8,'rep'=4] {'acct','rep'}, dimensions={0} | all-to-all | bytes 28672 | tf_op jit(solution)/shard_map/all_to_all | solution.py:354
  30.7 2.6 all-to-all-start.1
  33.3 0.1 fusion.11
  33.4 0.1 reshape.426
  33.5 0.7 reshape_reshape.11.srow
  34.1 0.9 copy.38.scol
  35.0 0.9 reshape_reshape.14.bcol
  35.9 4.9 %gather_fusion = bf16[512,256]{1,0:T(8,128)(2,1)} fusion(bf16[8192,256]{1,0:T(8,128)(2,1)} %copy.57, s32[1024]{0:T(1024)S(1)} %pad_clamp_fusion.3), kind=kCustom, calls=%fused_computation | custom fusion | bytes 526336 | tf_op jit(solution)/shard_map/gather | solution.py:398
  40.8 0.7 all-to-all-done.1
  41.5 0.7 copy-done
  42.2 7.2 %owner.1 = (bf16[512,256]{1,0:T(8,128)(2,1)}, bf16[256,256]{1,0:T(8,128)(2,1)}, s32[1,512]{1,0:T(1,128)}, f32[512,1]{1,0:T(8,128)}, bf16[512,128]{1,0:T(8,128)(2...) custom-call(bf16[512,256]{1,0:T(8,128)(2,1)} %gather_fusion, ...), custom_call_target="tpu_custom_call" | custom-call | tf_op jit(solution)/shard_map/owner/pallas_call | solution.py:43
  49.4 5.1 %all-to-all-start.3 = ((bf16[32,8,256]{2,1,0:T(8,128)(2,1)}), bf16[32,8,256]{2,1,0:T(8,128)(2,1)S(1)}, u32[]{:S(2)}, u32[]{:S(2)}) async-start(bf16[32,8,256]{2,1,0:T(8,128)(2,1)} %bitcast.45), calls=%async_computation.3 | async-start | bytes 262144 | tf_op jit(solution)/shard_map/all_to_all | solution.py:354
  54.6 0.6 reshape.490
  55.2 8.6 %all-to-all-done.3 = bf16[32,8,256]{2,1,0:T(8,128)(2,1)S(1)} async-done(((bf16[32,8,256]{2,1,0:T(8,128)(2,1)}), bf16[32,8,256]{2,1,0:T(8,128)(2,1)S(1)}, u32[]{:S(2)}, u32[]{:S(2)}) %all-to-all-start.3) | async-done | bytes 131104 | tf_op jit(solution)/shard_map/all_to_all | solution.py:354
  63.8 0.7 copy-done.3
  64.5 1.9 query.1
  66.4 3.1 %maximum_reduce_fusion = (s32[2560]{0:T(1024)S(1)}, s32[2560,1]{1,0:T(8,128)}, s32[2560]{0:T(1024)S(1)}) fusion(s32[2560,1]{1,0:T(8,128)S(1)} %reshape.490), kind=kLoop, calls=%fused_computation.23 | loop fusion | flops 97280 | bytes 40960 | tf_op jit(solution)/shard_map/max | solution.py:399
  69.6 9.5 %gather_fusion.1 = bf16[2560,256]{1,0:T(8,128)(2,1)} fusion(bf16[8192,256]{1,0:T(8,128)(2,1)} %copy.57, s32[3072]{0:T(1024)S(1)} %pad_clamp_fusion.1), kind=kCustom, calls=%fused_computation.1 | custom fusion | bytes 2631680 | tf_op jit(solution)/shard_map/gather | solution.py:399
  79.1 5.6 %patch.1 = bf16[2560,256]{1,0:T(8,128)(2,1)} custom-call(bf16[2560,256]{1,0:T(8,128)(2,1)} %gather_fusion.1, s32[2560,1]{1,0:T(8,128)} %get-tuple-element.68.ncol, s32[1,512]{1,0:T(1,128)} %get-tuple-element.41.sfirst, bf16[512,256]{1,0:T(8,128)(2,1)} %get-tuple-element.40.new), custom_call_target="tpu_custom_call" | custom-call | tf_op jit(solution)/shard_map/patch/pallas_call | solution.py:168
  84.8 3.3 %all-to-all-start.2 = ((bf16[32,80,256]{2,1,0:T(8,128)(2,1)}), bf16[32,80,256]{2,1,0:T(8,128)(2,1)S(1)}, u32[]{:S(2)}, u32[]{:S(2)}) async-start(bf16[32,80,256]{2,1,0:T(8,128)(2,1)} %bitcast.35), calls=%async_computation.2 | async-start | bytes 2621440 | tf_op jit(solution)/shard_map/all_to_all | solution.py:354
  88.2 37.8 %all-to-all-done.2 = bf16[32,80,256]{2,1,0:T(8,128)(2,1)S(1)} async-done(((bf16[32,80,256]{2,1,0:T(8,128)(2,1)}), bf16[32,80,256]{2,1,0:T(8,128)(2,1)S(1)}, u32[]{:S(2)}, u32[]{:S(2)}) %all-to-all-start.2) | async-done | bytes 1310752 | tf_op jit(solution)/shard_map/all_to_all | solution.py:354
  126.0 4.7 %gather_fusion.2 = bf16[1280,256]{1,0:T(8,128)(2,1)} fusion(bf16[2560,256]{1,0:T(8,128)(2,1)S(1)} %bitcast.34, s32[2048]{0:T(1024)S(1)} %pad_clamp_fusion.2), kind=kCustom, calls=%fused_computation.2 | custom fusion | bytes 1315840 | tf_op jit(solution)/shard_map/gather | solution.py:432
  130.7 4.8 %attend.1 = (bf16[128,256]{1,0:T(8,128)(2,1)}, bf16[256,256]{1,0:T(8,128)(2,1)}, bf16[32,320]{1,0:T(8,128)(2,1)}, bf16[768,256]{1,0:T(8,128)(2,1)}) custom-call(bf16[1280,256]{1,0:T(8,128)(2,1)} %gather_fusion.2, bf16[128,256]{1,0:T(8,128)(2,1)} %get-tuple-element.45.q_rows, bf16[128,256]{1,0:T(8,128)(2,1)} %get-tuple-element.46.q_proj, ...), custom_call_target="tpu_custom_call" | custom-call | tf_op jit(solution)/shard_map/attend/pallas_call | solution.py:43
  135.5 1.4 reshape.435
  136.9 4.1 %all-to-all-start.4 = ((bf16[32,4,80]{2,1,0:T(4,128)(2,1)}), bf16[32,4,80]{2,1,0:T(4,128)(2,1)S(1)}, u32[]{:S(2)}, u32[]{:S(2)}) async-start(bf16[32,4,80]{2,1,0:T(4,128)(2,1)} %reshape.435), calls=%async_computation.4 | async-start | bytes 65536 | tf_op jit(solution)/shard_map/all_to_all | solution.py:354
  141.0 0.1 reshape.437
  141.1 7.2 %all-to-all-done.4 = bf16[32,4,80]{2,1,0:T(4,128)(2,1)S(1)} async-done(((bf16[32,4,80]{2,1,0:T(4,128)(2,1)}), bf16[32,4,80]{2,1,0:T(4,128)(2,1)S(1)}, u32[]{:S(2)}, u32[]{:S(2)}) %all-to-all-start.4) | async-done | bytes 20512 | tf_op jit(solution)/shard_map/all_to_all | solution.py:354
  148.2 2.8 %all-to-all-start.5 = ((bf16[32,8,256]{2,1,0:T(8,128)(2,1)}), bf16[32,8,256]{2,1,0:T(8,128)(2,1)S(1)}, u32[]{:S(2)}, u32[]{:S(2)}) async-start(bf16[32,8,256]{2,1,0:T(8,128)(2,1)} %bitcast.43), calls=%async_computation.5 | async-start | bytes 262144 | tf_op jit(solution)/shard_map/all_to_all | solution.py:354
  151.0 0.6 compare_select_fusion.1.nrow
  151.7 0.7 reshape_reshape.13.drow
  152.4 0.7 reshape.436.scal
  153.1 8.7 %gather_fusion.4 = bf16[2560,256]{1,0:T(8,128)(2,1)} fusion(bf16[4096,256]{1,0:T(8,128)(2,1)} %all-gather.5.cloned.1.call-done, s32[3072]{0:T(1024)S(1)} %pad_clamp_fusion), kind=kCustom, calls=%fused_computation.4 | custom fusion | bytes 2631680 | tf_op jit(solution)/shard_map/gather | solution.py:430
  161.8 8.6 %gather_fusion.3 = bf16[2560,256]{1,0:T(8,128)(2,1)} fusion(bf16[4096,256]{1,0:T(8,128)(2,1)} %all-gather.3.cloned.1.call-done, s32[3072]{0:T(1024)S(1)} %pad_clamp_fusion), kind=kCustom, calls=%fused_computation.3 | custom fusion | bytes 2631680 | tf_op jit(solution)/shard_map/gather | solution.py:445
  170.4 0.7 copy-done.2
  171.1 8.8 %back.1 = bf16[1408,256]{1,0:T(8,128)(2,1)} custom-call(bf16[4,2560]{1,0:T(4,128)(2,1)} %reshape.436.scal, s32[1,2560]{1,0:T(1,128)} %compare_select_fusion.1.nrow, bf16[2560,256]{1,0:T(8,128)(2,1)} %gather_fusion.3, bf16[2560,256]{1,0:T(8,128)(2,1)} %gather_fusion.4, bf16[256,256]{1,0:T(8,128)(2,1)} %bitcast.38, s32[1,256]{1,0:T(1,128)} %reshape_reshape.13.drow, ...), custom_call_target="tpu_custom_call" | custom-call | tf_op jit(solution)/shard_map/back/pallas_call | solution.py:43
  179.9 1.2 pad_maximum_fusion
  181.1 0.2 reshape.440
  181.4 36.1 %all_to_all.40 = bf16[32,68,256]{2,1,0:T(8,128)(2,1)S(1)} all-to-all(bf16[32,68,256]{2,1,0:T(8,128)(2,1)S(1)} %reshape.440), channel_id=1, replica_groups=mesh['acct'=8,'rep'=4] {'acct','rep'}, dimensions={0} | all-to-all | bytes 2228224 | tf_op jit(solution)/shard_map/all_to_all | solution.py:354
  217.5 0.2 reduce_sum.12
  217.7 1.1 broadcast_in_dim.9
  218.8 2.8 %all-to-all-start.7 = ((bf16[32,68,256]{2,1,0:T(8,128)(2,1)}), bf16[32,68,256]{2,1,0:T(8,128)(2,1)S(1)}, u32[]{:S(2)}, u32[]{:S(2)}) async-start(bf16[32,68,256]{2,1,0:T(8,128)(2,1)} %broadcast_in_dim.9), calls=%async_computation.7 | async-start | bytes 2359296 | tf_op jit(solution)/shard_map/all_to_all | solution.py:354
  221.6 7.4 %scatter_fusion = bf16[8192,256]{1,0:T(8,128)(2,1)} fusion(bf16[8192,256]{1,0:T(8,128)(2,1)} %copy.57, s32[512]{0:T(512)S(1)} %bitcast.50, bf16[512,256]{1,0:T(8,128)(2,1)S(1)} %copy-done.1), kind=kCustom, calls=%fused_computation.5 | custom fusion | bytes 788480 | tf_op jit(solution)/shard_map/scatter | solution.py:420
  229.0 21.7 %all-to-all-done.7 = bf16[32,68,256]{2,1,0:T(8,128)(2,1)S(1)} async-done(((bf16[32,68,256]{2,1,0:T(8,128)(2,1)}), bf16[32,68,256]{2,1,0:T(8,128)(2,1)S(1)}, u32[]{:S(2)}, u32[]{:S(2)}) %all-to-all-start.7) | async-done | bytes 1114144 | tf_op jit(solution)/shard_map/all_to_all | solution.py:354
  250.7 1.1 reshape.441.x
  251.8 2.6 %unpack.1 = (f32[512,128]{1,0:T(8,128)}, f32[128,768]{1,0:T(8,128)}, f32[256,512]{1,0:T(8,128)}, f32[256,256]{1,0:T(8,128)}, f32[256,256]{1,0:T(8,128)}, /*index=5*/f32[256,256]{1,0:T(8,128)}, f32[256,256]{1,0:T(8,128)}) custom-call(bf16[2176,256]{1,0:T(8,128)(2,1)} %reshape.441.x), custom_call_target="tpu_custom_call" | custom-call | tf_op jit(solution)/shard_map/unpack/pallas_call | solution.py:43
  (28 shorter events, 0.3 us)
Async XLA Ops:
  7.2 146.0 %all-gather.5.cloned.1.call-start = ((), (), s32[]{:S(2)}) async-start(), calls=%async_computation.9 | async-start | bytes 2162688 | tf_op jit(solution)/shard_map/all_gather | solution.py:372
  7.2 4.5 %copy-start.6 = (s32[128,10,1]{0,2,1:T(1,128)S(1)}, s32[128,10,1]{0,2,1:T(1,128)}, u32[]{:S(2)}) copy-start(s32[128,10,1]{0,2,1:T(1,128)} %param.24) | copy-start | bytes 15364
  30.7 10.8 %all-to-all-start.1 = ((bf16[32,16,128]{2,1,0:T(8,128)(2,1)}), bf16[32,16,128]{2,1,0:T(8,128)(2,1)S(1)}, u32[]{:S(2)}, u32[]{:S(2)}) async-start(bf16[32,16,128]{2,1,0:T(8,128)(2,1)} %bitcast.44), calls=%async_computation.1 | async-start | bytes 262144 | tf_op jit(solution)/shard_map/all_to_all | solution.py:354
  41.5 0.7 copy-start
  49.4 14.5 %all-to-all-start.3 = ((bf16[32,8,256]{2,1,0:T(8,128)(2,1)}), bf16[32,8,256]{2,1,0:T(8,128)(2,1)S(1)}, u32[]{:S(2)}, u32[]{:S(2)}) async-start(bf16[32,8,256]{2,1,0:T(8,128)(2,1)} %bitcast.45), calls=%async_computation.3 | async-start | bytes 262144 | tf_op jit(solution)/shard_map/all_to_all | solution.py:354
  54.5 107.3 %all-gather.3.cloned.1.call-start = ((), (), s32[]{:S(2)}) async-start(), calls=%async_computation.8 | async-start | bytes 2162688 | tf_op jit(solution)/shard_map/all_gather | solution.py:429
  63.8 0.7 copy-start.3
  84.8 3.3 %copy-start.5 = (s32[10,128]{1,0:T(8,128)S(1)}, s32[10,128]{1,0:T(8,128)}, u32[]{:S(2)}) copy-start(s32[10,128]{1,0:T(8,128)} %get-tuple-element.42.nrank) | copy-start | bytes 15364
  84.8 41.2 %all-to-all-start.2 = ((bf16[32,80,256]{2,1,0:T(8,128)(2,1)}), bf16[32,80,256]{2,1,0:T(8,128)(2,1)S(1)}, u32[]{:S(2)}, u32[]{:S(2)}) async-start(bf16[32,80,256]{2,1,0:T(8,128)(2,1)} %bitcast.35), calls=%async_computation.2 | async-start | bytes 2621440 | tf_op jit(solution)/shard_map/all_to_all | solution.py:354
  136.9 11.4 %all-to-all-start.4 = ((bf16[32,4,80]{2,1,0:T(4,128)(2,1)}), bf16[32,4,80]{2,1,0:T(4,128)(2,1)S(1)}, u32[]{:S(2)}, u32[]{:S(2)}) async-start(bf16[32,4,80]{2,1,0:T(4,128)(2,1)} %reshape.435), calls=%async_computation.4 | async-start | bytes 65536 | tf_op jit(solution)/shard_map/all_to_all | solution.py:354
  148.2 22.2 %all-to-all-start.5 = ((bf16[32,8,256]{2,1,0:T(8,128)(2,1)}), bf16[32,8,256]{2,1,0:T(8,128)(2,1)S(1)}, u32[]{:S(2)}, u32[]{:S(2)}) async-start(bf16[32,8,256]{2,1,0:T(8,128)(2,1)} %bitcast.43), calls=%async_computation.5 | async-start | bytes 262144 | tf_op jit(solution)/shard_map/all_to_all | solution.py:354
  170.4 0.7 copy-start.2
  171.1 8.8 %copy-start.4 = (bf16[768,256]{1,0:T(8,128)(2,1)S(1)}, bf16[768,256]{1,0:T(8,128)(2,1)}, u32[]{:S(2)}) copy-start(bf16[768,256]{1,0:T(8,128)(2,1)} %get-tuple-element.59) | copy-start | bytes 1179652
  218.8 2.8 %copy-start.1 = (bf16[512,256]{1,0:T(8,128)(2,1)S(1)}, bf16[512,256]{1,0:T(8,128)(2,1)}, u32[]{:S(2)}) copy-start(bf16[512,256]{1,0:T(8,128)(2,1)} %get-tuple-element.40.new) | copy-start | bytes 786436
  218.8 31.8 %all-to-all-start.7 = ((bf16[32,68,256]{2,1,0:T(8,128)(2,1)}), bf16[32,68,256]{2,1,0:T(8,128)(2,1)S(1)}, u32[]{:S(2)}, u32[]{:S(2)}) async-start(bf16[32,68,256]{2,1,0:T(8,128)(2,1)} %broadcast_in_dim.9), calls=%async_computation.7 | async-start | bytes 2359296 | tf_op jit(solution)/shard_map/all_to_all | solution.py:354
Sparse Core Ops, SparseCore 0:
  11.9 59.7 all-gather.4
  74.5 58.5 all-gather.2

commit v2 on v1

--- a/solution.py
+++ b/solution.py
@@ -32,6 +32,24 @@
 
 def iota(shape, axis):
     return lax.broadcasted_iota(I32, shape, axis)
+
+
+def to_col(table, n, per, lane0, base=0):
+    devices, lanes = table.shape
+    pick = ((iota((n, devices), 0) + base) // per == iota((n, devices), 1)).astype(F32)
+    spread = dot(pick, table, precision=EXACT)
+    r = iota((n, lanes), 0) + base
+    at = iota((n, lanes), 1) == lane0 + r - r // per * per
+    return jnp.sum(jnp.where(at, spread, 0.0), axis=1, keepdims=True)
+
+
+def to_row(table, n, per, lane0):
+    devices, lanes = table.shape
+    c = iota((lanes, n), 1)
+    pick = (iota((lanes, n), 0) == lane0 + c - c // per * per).astype(F32)
+    spread = dot(table, pick, precision=EXACT)
+    mine = iota((devices, n), 0) == iota((devices, n), 1) // per
+    return jnp.sum(jnp.where(mine, spread, 0.0), axis=0, keepdims=True)
 
 
 def sigmoid(v):
@@ -91,18 +109,22 @@
 
 
 def owner_body(
-    ce, rows, feats, scol, srow, bcol, w_msg, w_in, u_zr, u_h,
-    new, dst_new, sfirst, fcol, code, pre, mean, div, upd, rst, cand, rstate, msg,
+    ce, rows, feats, got, w_msg, w_in, u_zr, u_h,
+    new, dst_new, sfirst, scol, fcol, code, pre, mean, div, upd, rst, cand, rstate, msg, bcol,
 ):
-    n, m = rows.shape
-    f = feats.shape[1]
+    n, f = feats.shape
+    m = rows.shape[1]
     t = w_msg.shape[0] - m - f
     step = 128
     frequency = jnp.exp(iota((1, t), 1).astype(F32) * (-11.5 / t))
+    table = got[:, : 4 * ce].astype(F32)
+    scol[...] = to_col(table, n, 2 * ce, 0).astype(I32)
+    bcol[...] = to_col(table, n, 2 * ce, 2 * ce)
+    slots = to_row(table, n, 2 * ce, 0).astype(I32)
 
     def messages(i, carry):
         b = pl.ds(pl.multiple_of(i * step, step), step)
-        enc = jnp.cos(bcol[b, :].astype(F32) * frequency).astype(BF16)
+        enc = jnp.cos(bcol[b, :] * frequency).astype(BF16)
         code[b, :] = enc
         act = (
             dot(rows[b, :], w_msg[:m, :]) + dot(feats[b, :], w_msg[m : m + f, :])
@@ -112,8 +134,6 @@
         return carry
 
     lax.fori_loop(0, n // step, messages, 0)
-    slots = srow[...]
-
     def gru(i, early):
         b = pl.ds(pl.multiple_of(i * step, step), step)
         mine = scol[b, :]
@@ -145,15 +165,17 @@
         return early
 
     early = lax.fori_loop(0, n // step, gru, jnp.zeros((1, n), F32))
-    sfirst[...] = jnp.where(early < 0.5, slots, -2)
+    sfirst[...] = jnp.where((early < 0.5) & (slots >= 0), slots, -2)
     half = n // 2
     r = iota((half, n), 0)
     pick = (iota((half, n), 1) == r + (r // ce + 1) * ce).astype(F32).astype(BF16)
     dst_new[...] = dot(pick, new[...]).astype(BF16)
 
 
-def patch_body(old, ncol, sfirst, new, out):
-    hit = (ncol[...] == sfirst[...]).astype(F32).astype(BF16)
+def patch_body(events, ce, cn, block, old, got, sfirst, new, out):
+    table = got[:, 4 * ce :].astype(F32)
+    code = to_col(table, block, cn, 0, pl.program_id(0) * block).astype(I32)
+    hit = (code // events == sfirst[...]).astype(F32).astype(BF16)
     rows = dot(hit, new[...])
     found = dot(hit, jnp.ones((new.shape[0], 128), BF16)) > 0.5
     for h in range(rows.shape[1] // 128):
@@ -161,23 +183,43 @@
         out[:, c] = jnp.where(found, rows[:, c], old[:, c].astype(F32)).astype(BF16)
 
 
-def patch(old, ncol, sfirst, new):
-    n, m = old.shape
-    s = new.shape[0]
+def patch(events, ce, cn, fetched, got, sfirst, new):
+    s, m = new.shape
+    n = fetched.shape[0] - s
     block = 512
+    skip = s // block
     return pl.pallas_call(
-        patch_body,
+        functools.partial(patch_body, events, ce, cn, block),
         grid=(n // block,),
         out_shape=jax.ShapeDtypeStruct((n, m), BF16),
         in_specs=[
-            pl.BlockSpec((block, m), lambda i: (i, 0)),
-            pl.BlockSpec((block, 1), lambda i: (i, 0)),
+            pl.BlockSpec((block, m), lambda i: (i + skip, 0)),
+            pl.BlockSpec(got.shape, lambda i: (0, 0)),
             pl.BlockSpec((1, s), lambda i: (0, 0)),
             pl.BlockSpec((s, m), lambda i: (0, 0)),
         ],
         out_specs=pl.BlockSpec((block, m), lambda i: (i, 0)),
         name="patch",
-    )(old, ncol, sfirst, new)
+    )(fetched, got, sfirst, new)
+
+
+def hot_body(events, ce, cn, block, got, out):
+    table = got[:, 4 * ce :].astype(F32)
+    code = to_col(table, block, cn, 0, pl.program_id(0) * block).astype(I32)
+    event = jnp.where(code >= 0, code % events, -1)
+    out[...] = (iota((block, events), 1) == event).astype(F32).astype(BF16)
+
+
+def hot(events, ce, cn, got, n):
+    block = 512
+    return pl.pallas_call(
+        functools.partial(hot_body, events, ce, cn, block),
+        grid=(n // block,),
+        out_shape=jax.ShapeDtypeStruct((n, events), BF16),
+        in_specs=[pl.BlockSpec(got.shape, lambda i: (0, 0))],
+        out_specs=pl.BlockSpec((block, events), lambda i: (i, 0)),
+        name="hot",
+    )(got)
 
 
 def query_body(back, dplace, w_query, q_rows, q_proj):
@@ -190,8 +232,8 @@
 
 
 def attend_body(
-    cn, devices, keys, q_rows, q_proj, grad, w_query, w_key, w_value, dplace, no, nrank,
-    emb, dq_out, scal, g_qkv, kp, vp, dk, dv,
+    cn, devices, each, keys, q_rows, q_proj, grad, w_query, w_key, w_value, dback, no, nrank,
+    emb, reply, g_qkv, kp, vp, dk, dv,
 ):
     events, m = q_rows.shape
     neighbours = no.shape[0]
@@ -251,37 +293,49 @@
     g_qkv[m : 2 * m, :] = dot_tn(keys[...], dk[...]).astype(BF16)
     g_qkv[2 * m : 3 * m, :] = dot_tn(keys[...], dv[...]).astype(BF16)
     d_rows = (gf + dot_nt(dq_b, w_query[...])).astype(BF16)
-    spots = (iota((dq_out.shape[0], events), 0) == dplace[...]).astype(F32).astype(BF16)
-    dq_out[...] = dot(spots, d_rows).astype(BF16)
+    n = devices * each
+    spots = (iota((n, events), 0) == dback[...]).astype(F32).astype(BF16)
+    sent = dot(spots, d_rows)
     att_t = att_b.T
     raw_t = d_raw.T
     own = iota((devices, events), 0)
-    total = jnp.zeros((devices, 4 * cn), F32)
+    totals = [jnp.zeros((devices, m), F32) for _ in range(4)]
     for k in range(neighbours):
         onehot = (own == no[k : k + 1, :]).astype(F32).astype(BF16)
-        hits = (iota((cn, events), 0) == nrank[k : k + 1, :]).astype(F32)
-        values = jnp.concatenate(
-            [
-                hits * raw_t[k : k + 1, :],
-                hits * raw_t[64 + k : 65 + k, :],
-                hits * att_t[k : k + 1, :],
-                hits * att_t[64 + k : 65 + k, :],
-            ],
-            axis=0,
-        ).astype(BF16)
-        total = total + dot_nt(onehot, values)
-    scal[...] = total.astype(BF16)
+        hits = (iota((m, events), 0) == nrank[k : k + 1, :]).astype(F32)
+        for j, v in enumerate((raw_t, raw_t, att_t, att_t)):
+            i = (j % 2) * 64 + k
+            values = (hits * v[i : i + 1, :]).astype(BF16)
+            totals[j] = totals[j] + dot_nt(onehot, values)
+    for j in range(4):
+        spot = iota((n, devices), 0) == iota((n, devices), 1) * each + j
+        sent = sent + dot(spot.astype(F32).astype(BF16), totals[j].astype(BF16))
+    reply[...] = sent.astype(BF16)
 
 
 def back_body(
-    scal, nrow, qe, ge, dq, drow, scol, fcol, rows, feats, code, pre, mean, div,
-    upd, rst, cand, rstate, w_in, u_h, w_key, w_value, out, gates, dpre,
+    direct, scal, nrow, qsrc, hots, ge, dq, drow, scol, fcol, rows, feats, code, pre, mean, div,
+    upd, rst, cand, rstate, w_in, u_h, w_key, w_value, g_qkv, parity, out, gates, dpre, qe,
 ):
-    n, m = rows.shape
+    n, m = mean.shape[0], rows.shape[1]
     f = feats.shape[1]
     hs = m // HEADS
     step = 256
     s = mean.shape[1]
+    if direct:
+        qe = qsrc
+    else:
+        events = hots.shape[1]
+        devices = qsrc.shape[0] // events
+        cn = hots.shape[0] // devices
+
+        def expand(d, carry):
+            b = pl.ds(pl.multiple_of(d * cn, cn), cn)
+            e = pl.ds(pl.multiple_of(d * events, events), events)
+            qe[b, :] = dot(hots[b, :], qsrc[e, :]).astype(BF16)
+            return carry
+
+        lax.fori_loop(0, devices, expand, 0)
 
     def block(i, carry):
         b = pl.ds(pl.multiple_of(i * step, step), step)
@@ -314,40 +368,64 @@
         return carry
 
     lax.fori_loop(0, n // step, block, 0)
-    at = 0
-    g_in = dot_tn(mean[...], gates[...])
+    half = out.shape[1]
+    me = parity[0, 0]
+    at = [0]
+
+    def put(value):
+        start, size = at[0], value.shape[0]
+        low = max(0, min(size, half - start))
+        if low:
+            out[me, start : start + low, :] = value[:low, :].astype(BF16)
+        if low < size:
+            out[1 - me, start + low - half : start + size - half, :] = value[low:, :].astype(BF16)
+        at[0] = start + size
+
+    def put_cols(value):
+        for j in range(value.shape[1] // 128):
+            put(value[:, j * 128 : (j + 1) * 128])
+
+    state_rows = rows[:n, :]
+    put_cols(dot_tn(mean[...], gates[...]))
+    put_cols(dot_tn(state_rows, gates[:, : 2 * m]))
+    put_cols(dot_tn(rstate[...], gates[:, 2 * m :]))
+    put_cols(dot_tn(state_rows, dpre[...]))
+    put_cols(dot_tn(feats[...], dpre[...]))
+    put_cols(dot_tn(code[...], dpre[...]))
     for j in range(3):
-        out[at : at + s, :] = g_in[:, j * m : (j + 1) * m].astype(BF16)
-        at += s
-    g_zr = dot_tn(rows[...], gates[:, : 2 * m])
-    for j in range(2):
-        out[at : at + m, :] = g_zr[:, j * m : (j + 1) * m].astype(BF16)
-        at += m
-    out[at : at + m, :] = dot_tn(rstate[...], gates[:, 2 * m :]).astype(BF16)
-    at += m
-    out[at : at + m, :s] = dot_tn(rows[...], dpre[...]).astype(BF16)
-    out[at : at + f, s:] = dot_tn(feats[...], dpre[...]).astype(BF16)
-    out[at + f : at + m, s:] = dot_tn(code[...], dpre[...]).astype(BF16)
-
-
-def unpack_body(x, g_msg, g_in, g_zr, g_h, g_q, g_k, g_v):
-    m = g_h.shape[0]
-    s = g_in.shape[0]
-    at = 0
-    for j in range(3):
-        g_in[:, j * m : (j + 1) * m] = x[at : at + s, :].astype(F32)
-        at += s
-    for j in range(2):
-        g_zr[:, j * m : (j + 1) * m] = x[at : at + m, :].astype(F32)
-        at += m
-    g_h[...] = x[at : at + m, :].astype(F32)
-    at += m
-    g_msg[:m, :] = x[at : at + m, :s].astype(F32)
-    g_msg[m:, :] = x[at : at + m, s:].astype(F32)
-    at += m
-    for ref in (g_q, g_k, g_v):
-        ref[...] = x[at : at + m, :].astype(F32)
-        at += m
+        put_cols(g_qkv[j * m : (j + 1) * m, :].astype(F32))
+
+
+def spread_body(x, out):
+    total = x[0].astype(F32)
+    for i in range(1, x.shape[0]):
+        total = total + x[i].astype(F32)
+    total = total.astype(BF16)
+    for i in range(x.shape[0]):
+        out[i] = total
+
+
+def unpack_body(mine, other, parity, g_in, g_zr, g_h, g_msg, g_q, g_k, g_v):
+    half = mine.shape[0]
+    even = parity[0, 0] == 0
+    at = [0]
+
+    def take(ref, r, c, size):
+        start = at[0]
+        low = max(0, min(size, half - start))
+        if low:
+            b = slice(start, start + low)
+            ref[r : r + low, c : c + 128] = jnp.where(even, mine[b, :], other[b, :]).astype(F32)
+        if low < size:
+            b = slice(start + low - half, start + size - half)
+            ref[r + low : r + size, c : c + 128] = jnp.where(
+                even, other[b, :], mine[b, :]
+            ).astype(F32)
+        at[0] = start + size
+
+    for ref in (g_in, g_zr, g_h, g_msg, g_q, g_k, g_v):
+        for c in range(0, ref.shape[1], 128):
+            take(ref, 0, c, ref.shape[0])
 
 
 def exchange(x):
@@ -389,37 +467,27 @@
     got = exchange(req.reshape(devices, 1, 4 * ce + cn)).reshape(devices, 4 * ce + cn)
     got_feats = exchange(side_feats.reshape(devices, 2 * ce, feat)).reshape(n_side, feat)
     side_slots = got[:, : 2 * ce].reshape(n_side)
-    side_times = got[:, 2 * ce : 4 * ce].reshape(n_side)
-    dst_slots = got[:, ce : 2 * ce].reshape(n_dst)
     nb_code = got[:, 4 * ce :].reshape(n_nb)
-    nb_slots = jnp.where(nb_code >= 0, nb_code // events, -1)
-    nb_event = jnp.maximum(nb_code, 0) % events
-    nb_table = nb_event + (jnp.arange(n_nb, dtype=I32) // cn) * events
-    fetched = memory[jnp.maximum(side_slots, 0)]
-    old_nb = memory[jnp.maximum(nb_slots, 0)]
+    wanted = jnp.concatenate([side_slots, nb_code // events])
+    fetched = memory[jnp.maximum(wanted, 0)]
     (
-        new_side, dst_new, sfirst, fcol, code, pre, mean, div, upd, rst, cand, rstate,
+        new_side, dst_new, sfirst, scol, fcol, code, pre, mean, div, upd, rst, cand, rstate,
     ) = call(
         functools.partial(owner_body, ce),
         [
-            ((n_side, m), BF16), ((n_dst, m), BF16), ((1, n_side), I32), ((n_side, 1), F32),
-            ((n_side, w_msg.shape[0] - m - feat), BF16), ((n_side, width), F32),
-            ((n_side, width), BF16), ((n_side, width), F32),
+            ((n_side, m), BF16), ((n_dst, m), BF16), ((1, n_side), I32), ((n_side, 1), I32),
+            ((n_side, 1), F32), ((n_side, w_msg.shape[0] - m - feat), BF16),
+            ((n_side, width), F32), ((n_side, width), BF16), ((n_side, width), F32),
             ((n_side, m), F32), ((n_side, m), F32), ((n_side, m), F32), ((n_side, m), BF16),
         ],
-        (
-            fetched, got_feats, side_slots.reshape(n_side, 1), side_slots.reshape(1, n_side),
-            side_times.reshape(n_side, 1), w_msg, w_in, u_zr, u_h,
-        ),
+        (fetched, got_feats, got, w_msg, w_in, u_zr, u_h),
         "owner",
-        scratch=[pltpu.VMEM((n_side, width), BF16)],
+        scratch=[pltpu.VMEM((n_side, width), BF16), pltpu.VMEM((n_side, 1), F32)],
     )
     back_dst = exchange(dst_new.reshape(devices, ce, m)).reshape(n_dst, m)
-    nb_reply = patch(old_nb, nb_slots.reshape(n_nb, 1), sfirst, new_side)
-    back_nb = exchange(nb_reply.reshape(devices, cn, m)).reshape(n_nb, m)
-    new_memory = memory.at[jnp.where(side_slots >= 0, side_slots, acc_rows)].set(
-        new_side, mode="drop"
-    )
+    nb_reply = patch(events, ce, cn, fetched, got, sfirst, new_side)
+    back_nb = exchange(nb_reply.reshape(devices, cn, m))
+    back_dst, nb_reply = lax.optimization_barrier((back_dst, nb_reply))
     q_rows, q_proj = call(
         query_body,
         [((events, m), BF16), ((events, m), BF16)],
@@ -427,47 +495,86 @@
         "query",
     )
     proj_all = lax.all_gather(q_proj, AXES, axis=0, tiled=True)
-    ge = grad_all[nb_table]
+    each = max(2 * ce, -(-(ce + 4) // 8) * 8)
+    late_memory, late_got, _ = lax.optimization_barrier((memory, got, nb_reply))
+    late_slots = late_got[:, : 2 * ce].reshape(n_side)
+    new_memory = late_memory.at[jnp.where(late_slots >= 0, late_slots, acc_rows)].set(
+        new_side, mode="drop"
+    )
+    late_code = late_got[:, 4 * ce :].reshape(n_nb)
+    table = jnp.maximum(late_code, 0) % events + jnp.arange(n_nb, dtype=I32) // cn * events
+    ge = grad_all[table]
+    nrow = (late_code // events).reshape(1, n_nb)
+    drow = jnp.concatenate(
+        [jnp.full((devices, each - ce), -1, I32), late_got[:, ce : 2 * ce]], axis=1
+    ).reshape(1, devices * each)
+    hots = hot(events, ce, cn, late_got, n_nb)
     nb_place = (no * cn + nrank).reshape(-1)
-    keys = back_nb[nb_place]
-    embedding, dq_out, scal, g_qkv = call(
-        functools.partial(attend_body, cn, devices),
-        [
-            ((events, m), BF16), ((n_dst, m), BF16), ((devices, 4 * cn), BF16),
-            ((3 * m, m), BF16),
-        ],
-        (keys, q_rows, q_proj, emb_grad, w_query, w_key, w_value, dplace, no, nrank),
+    back_nb, new_memory, ge, nrow, drow, hots, nb_place, q_rows = lax.optimization_barrier(
+        (back_nb, new_memory, ge, nrow, drow, hots, nb_place, q_rows)
+    )
+    keys = back_nb.reshape(n_nb, m)[nb_place]
+    dback = dplace // ce * each + (each - ce) + dplace % ce
+    embedding, reply, g_qkv = call(
+        functools.partial(attend_body, cn, devices, each),
+        [((events, m), BF16), ((devices * each, m), BF16), ((3 * m, m), BF16)],
+        (keys, q_rows, q_proj, emb_grad, w_query, w_key, w_value, dback, no, nrank),
         "attend",
         scratch=[pltpu.VMEM((events * neighbours, m), BF16)] * 4,
     )
-    scal_got = exchange(scal.reshape(devices, 4, cn))
-    dq_got = exchange(dq_out.reshape(devices, ce, m)).reshape(n_dst, m)
-    qe = proj_all[nb_table]
-    late = call(
-        back_body,
-        [((3 * width + 4 * m, m), BF16)],
-        (
-            scal_got.transpose(1, 0, 2).reshape(4, n_nb), nb_slots.reshape(1, n_nb), qe, ge,
-            dq_got, dst_slots.reshape(1, n_dst), side_slots.reshape(n_side, 1), fcol, fetched,
-            got_feats, code, pre, mean, div, upd, rst, cand, rstate, w_in, u_h, w_key, w_value,
-        ),
-        "back",
-        scratch=[pltpu.VMEM((n_side, 3 * m), BF16), pltpu.VMEM((n_side, width), BF16)],
-    )[0]
-    grads = jnp.concatenate([late, g_qkv], axis=0)
-    rows = grads.shape[0] // devices
-    shares = exchange(grads.reshape(devices, rows, m))
-    mine = jnp.sum(shares.astype(F32), axis=0).astype(BF16)
-    whole = exchange(jnp.broadcast_to(mine[None], (devices, rows, m)))
-    g_msg, g_in, g_zr, g_h, g_q, g_k, g_v = call(
+    back = exchange(reply.reshape(devices, each, m))
+    scal = back[:, :4, :cn].transpose(1, 0, 2).reshape(4, n_nb)
+    direct = cn % 16 != 0
+    index = lax.axis_index(AXES)
+    parity = (index % 2).astype(I32).reshape(1, 1)
+    total_rows = (w_msg.size + w_in.size + u_zr.size + u_h.size + 3 * w_query.size) // 128
+    half = total_rows // 2
+    args = (
+        scal, nrow, proj_all[table] if direct else proj_all, hots, ge,
+        back.reshape(devices * each, m), drow, scol, fcol, fetched,
+        got_feats, code, pre, mean, div, upd, rst, cand, rstate, w_in, u_h, w_key, w_value,
+        g_qkv, parity,
+    )
+    vm = pl.BlockSpec(memory_space=pltpu.VMEM)
+    sm = pl.BlockSpec(memory_space=pltpu.SMEM)
+    halves = pl.pallas_call(
+        functools.partial(back_body, direct),
+        out_shape=jax.ShapeDtypeStruct((2, half, 128), BF16),
+        in_specs=[vm] * (len(args) - 1) + [sm],
+        out_specs=vm,
+        scratch_shapes=[
+            pltpu.VMEM((n_side, 3 * m), BF16), pltpu.VMEM((n_side, width), BF16),
+            pltpu.VMEM((n_nb, m), BF16),
+        ],
+        compiler_params=pltpu.CompilerParams(vmem_limit_bytes=VMEM_LIMIT),
+        name="back",
+    )(*args)
+    pairs = [(i, i ^ 1) for i in range(devices)]
+    teams = [[i for i in range(devices) if i % 2 == p] for p in range(2)]
+    size = devices // 2
+    keep, send = halves[0], halves[1]
+    half_sum = (
+        keep.astype(F32) + lax.ppermute(send, AXES, pairs).astype(F32)
+    ).astype(BF16).reshape(size, half // size, 128)
+    shares = lax.all_to_all(
+        half_sum, AXES, split_axis=0, concat_axis=0, tiled=True, axis_index_groups=teams
+    )
+    spread = call(spread_body, [(shares.shape, BF16)], (shares,), "spread")[0]
+    mine = lax.all_to_all(
+        spread, AXES, split_axis=0, concat_axis=0, tiled=True, axis_index_groups=teams
+    ).reshape(half, 128)
+    other = lax.ppermute(mine, AXES, pairs)
+    outs = [
+        ((width, 3 * m), F32), ((m, 2 * m), F32), ((m, m), F32),
+        ((w_msg.shape[0], width), F32), ((m, m), F32), ((m, m), F32), ((m, m), F32),
+    ]
+    g_in, g_zr, g_h, g_msg, g_q, g_k, g_v = pl.pallas_call(
         unpack_body,
-        [
-            ((w_msg.shape[0], width), F32), ((width, 3 * m), F32), ((m, 2 * m), F32),
-            ((m, m), F32), ((m, m), F32), ((m, m), F32), ((m, m), F32),
-        ],
-        (whole.reshape(devices * rows, m),),
-        "unpack",
-    )
+        out_shape=[jax.ShapeDtypeStruct(a, d) for a, d in outs],
+        in_specs=[vm, vm, sm],
+        out_specs=[vm] * len(outs),
+        name="unpack",
+    )(mine, other, parity)
     return (new_memory, embedding, g_msg, g_in, g_zr, g_h, g_q, g_k, g_v)
 
 

time: 262 us -> 217 us (0.83)
  waiting for transfers between devices: 76.1 us -> 27.1 us
  Pallas kernels: 35 us -> 53.6 us
  local copies, waits for them, and re-layouts: 59.5 us -> 46.1 us
  blocking collectives: 50.5 us -> 54.7 us
  starting transfers between devices: 20.7 us -> 18 us
    all_to_all x6 -> x4, waiting for transfers between devices: 76.1 us -> 23.1 us  [exchange(): return lax.all_to_all(x, AXES, split_axis=0, concat_axis=0, tiled=True)]
    all_to_all x0 -> x2, blocking collectives: none -> 40.3 us  [the longest x1 20.7 us: body(): lax.all_to_all(half_sum, AXES, split_axis=0, concat_axis=0, tiled=True, a...]
    all_to_all x2 -> x1, blocking collectives: 50.5 us -> 14.4 us  [exchange(): return lax.all_to_all(x, AXES, split_axis=0, concat_axis=0, tiled=True)]
    pallas_call x1 -> x4, Pallas kernels: 5.63 us -> 31.6 us  [the longest x1 14.5 us: body(): pl.pallas_call(functools.partial(back_body, direct), out_shape=jax.ShapeD...]
    gather x5 -> x3, local copies, waits for them, and re-layouts: 36.4 us -> 28.3 us  [the longest x1 15 us: body(): fetched = memory[jnp.maximum(wanted, 0)]]
    pallas_call x6 -> x5, Pallas kernels: 29.3 us -> 22 us  [call(): pl.pallas_call(body, out_shape=[jax.ShapeDtypeStruct(s, d) for s, d in ou...]
    optimization_barrier x0 -> x1, local copies, waits for them, and re-layouts: none -> 4.48 us  [body(): late_memory, late_got, _ = lax.optimization_barrier((memory, got, nb_reply))]
    unnamed x16 -> x23, local copies, waits for them, and re-layouts: 7.05 us -> 2.77 us
  transfers between devices with their start and end apart: 8 -> 8, of which waited for: 5 -> 4; matrix products, arithmetic and copies ran while one was open for 21% -> 18% of each run, Pallas kernels for 9% -> 16%
where the time goes in v2:
time: 217 us; the launch traced here: 216 us
  blocking collectives  54.7 us (25%)
  Pallas kernels  53.6 us (25%)
  local copies, waits for them, and re-layouts  46.1 us (21%)
  waiting for transfers between devices  27.1 us (12%)
  starting transfers between devices  18 us (8%)
  between operations  14.3 us (7%)
  other arithmetic  2.6 us (1%)
    all_to_all x4, waiting for transfers between devices, exchange(): return lax.all_to_all(x, AXES, split_axis=0, concat_axis=0, tiled=True)  23.1 us
    pallas_call x5, Pallas kernels, call(): pl.pallas_call(body, out_shape=[jax.ShapeDtypeStruct(s, d) for s, d in ou...  22 us
    all_to_all x1, blocking collectives, body(): lax.all_to_all(half_sum, AXES, split_axis=0, concat_axis=0, tiled=True, a...  20.7 us
    all_to_all x1, blocking collectives, body(): lax.all_to_all(spread, AXES, split_axis=0, concat_axis=0, tiled=True, axi...  19.7 us
    all_to_all x4, starting transfers between devices, exchange(): return lax.all_to_all(x, AXES, split_axis=0, concat_axis=0, tiled=True)  17.9 us
    gather x1, local copies, waits for them, and re-layouts, body(): fetched = memory[jnp.maximum(wanted, 0)]  15 us
    pallas_call x1, Pallas kernels, body(): pl.pallas_call(functools.partial(back_body, direct), out_shape=jax.ShapeD...  14.5 us
    all_to_all x1, blocking collectives, exchange(): return lax.all_to_all(x, AXES, split_axis=0, concat_axis=0, tiled=True)  14.4 us
  transfers between devices with their start and end apart: 8, of which 4 were waited for; matrix products, arithmetic and copies ran while one was open for 18% of the time, Pallas kernels for 16%

profile of v2, /device:TPU:0, one launch (start us, length us, event | category | flops | bytes accessed | tf_op | source)
XLA Modules:
  0.0 216.3 jit_solution(4605208352980229794)
XLA Ops:
  7.2 0.0 all-gather.3.cloned.1.call-start
  7.2 4.5 %copy.38 = bf16[8192,256]{1,0:T(8,128)(2,1)} copy(bf16[8192,256]{1,0:T(8,128)(2,1)} %param.17) | data formatting | bytes 8388608 | tf_op jit(solution)/shard_map/optimization_barrier | solution.py:499
  11.7 0.6 copy.35
  12.3 4.0 %place.1 = (s32[32,112]{1,0:T(8,128)}, bf16[512,128]{1,0:T(8,128)(2,1)}, s32[1,128]{1,0:T(1,128)}, s32[10,128]{1,0:T(8,128)}) custom-call(s32[1,128]{1,0:T(1,128)} %bitcast.69, s32[1,128]{1,0:T(1,128)} %bitcast.70, s32[1,128]{1,0:T(1,128)} %bitcast.71, s32[1,128]{1,0:T(1,128)} %bitcast.72, s32[10,128]{1,0:T(8,128)} %bitcast.63, s32[10,128]{1,0:T(8,128)} %bitcast.68, ...), custom_call_target="tpu_custom_call" | custom-call | tf_op jit(solution)/shard_map/place/pallas_call | solution.py:61
  16.4 14.4 %all_to_all.37 = s32[32,1,112]{2,1,0:T(1,128)S(1)} all-to-all(s32[32,1,112]{2,1,0:T(1,128)} %bitcast.66), channel_id=1, replica_groups=mesh['acct'=8,'rep'=4] {'acct','rep'}, dimensions={0} | all-to-all | bytes 28672 | tf_op jit(solution)/shard_map/all_to_all | solution.py:432
  30.7 2.6 %all-to-all-start.1 = ((bf16[32,16,128]{2,1,0:T(8,128)(2,1)}), bf16[32,16,128]{2,1,0:T(8,128)(2,1)S(1)}, u32[]{:S(2)}, u32[]{:S(2)}) async-start(bf16[32,16,128]{2,1,0:T(8,128)(2,1)} %bitcast.61), calls=%async_computation.1 | async-start | bytes 262144 | tf_op jit(solution)/shard_map/all_to_all | solution.py:432
  33.3 0.1 slice.39
  33.4 0.1 reshape.314
  33.5 0.1 concatenate.17
  33.6 15.0 %gather_fusion = bf16[3072,256]{1,0:T(8,128)(2,1)} fusion(bf16[8192,256]{1,0:T(8,128)(2,1)} %copy.38, s32[3072]{0:T(1024)S(1)} %broadcast_clamp_fusion), kind=kCustom, calls=%fused_computation | custom fusion | bytes 3158016 | tf_op jit(solution)/shard_map/gather | solution.py:472
  48.6 0.7 copy-done.4
  49.3 8.1 %owner.1 = (bf16[512,256]{1,0:T(8,128)(2,1)}, bf16[256,256]{1,0:T(8,128)(2,1)}, s32[1,512]{1,0:T(1,128)}, s32[512,1]{1,0:T(8,128)}, f32[512,1]{1,0:T(8,128)}, /*...) custom-call(bf16[3072,256]{1,0:T(8,128)(2,1)} %gather_fusion, ...), custom_call_target="tpu_custom_call" | custom-call | tf_op jit(solution)/shard_map/owner/pallas_call | solution.py:61
  57.4 5.8 %all-to-all-start.3 = ((bf16[32,8,256]{2,1,0:T(8,128)(2,1)}), bf16[32,8,256]{2,1,0:T(8,128)(2,1)S(1)}, u32[]{:S(2)}, u32[]{:S(2)}) async-start(bf16[32,8,256]{2,1,0:T(8,128)(2,1)} %bitcast.62), calls=%async_computation.3 | async-start | bytes 262144 | tf_op jit(solution)/shard_map/all_to_all | solution.py:432
  63.2 0.0 all-gather.5.cloned.1.call-start
  63.2 9.3 %patch.1 = bf16[2560,256]{1,0:T(8,128)(2,1)} custom-call(bf16[3072,256]{1,0:T(8,128)(2,1)} %gather_fusion, s32[32,112]{1,0:T(8,128)} %bitcast.51, s32[1,512]{1,0:T(1,128)} %get-tuple-element.51.sfirst, bf16[512,256]{1,0:T(8,128)(2,1)} %get-tuple-element.52.new), custom_call_target="tpu_custom_call" | custom-call | tf_op jit(solution)/shard_map/patch/pallas_call | solution.py:191
  72.6 0.6 copy-done.7
  73.2 1.9 query.1
  75.2 5.9 %all-to-all-start.2 = ((bf16[32,80,256]{2,1,0:T(8,128)(2,1)}), bf16[32,80,256]{2,1,0:T(8,128)(2,1)S(1)}, u32[]{:S(2)}, u32[]{:S(2)}) async-start(bf16[32,80,256]{2,1,0:T(8,128)(2,1)} %bitcast.44), calls=%async_computation.2 | async-start | bytes 2621440 | tf_op jit(solution)/shard_map/all_to_all | solution.py:432
  81.1 0.6 fusion.6.dback
  81.6 4.9 %hot.1.hots = bf16[2560,128]{1,0:T(8,128)(2,1)} custom-call(s32[32,112]{1,0:T(8,128)} %bitcast.52), custom_call_target="tpu_custom_call" | custom-call | tf_op jit(solution)/shard_map/hot/pallas_call | solution.py:215
  86.6 0.1 slice.28
  86.6 0.1 reshape.318
  86.7 0.1 fusion.7
  86.8 0.1 rem.107
  86.9 0.1 reshape.319
  87.0 0.1 concatenate.20
  87.0 0.7 reshape.320.drow
  87.7 0.1 fusion.4
  87.8 0.6 and_select_fusion.nrow
  88.5 7.4 %scatter_fusion = bf16[8192,256]{1,0:T(8,128)(2,1)} fusion(bf16[8192,256]{1,0:T(8,128)(2,1)} %copy.38, s32[512]{0:T(512)S(1)} %bitcast.67, bf16[512,256]{1,0:T(8,128)(2,1)S(1)} %copy-done.5), kind=kCustom, calls=%fused_computation.3 | custom fusion | bytes 788480 | tf_op jit(solution)/shard_map/scatter | solution.py:501
  95.8 8.7 %gather_fusion.1 = bf16[2560,256]{1,0:T(8,128)(2,1)} fusion(bf16[4096,256]{1,0:T(8,128)(2,1)} %all-gather.3.cloned.1.call-done, s32[3072]{0:T(1024)S(1)} %pad_clamp_fusion), kind=kCustom, calls=%fused_computation.1 | custom fusion | bytes 2631680 | tf_op jit(solution)/shard_map/gather | solution.py:506
  104.5 12.6 %all-to-all-done.2 = bf16[32,80,256]{2,1,0:T(8,128)(2,1)S(1)} async-done(((bf16[32,80,256]{2,1,0:T(8,128)(2,1)}), bf16[32,80,256]{2,1,0:T(8,128)(2,1)S(1)}, u32[]{:S(2)}, u32[]{:S(2)}) %all-to-all-start.2) | async-done | bytes 1310752 | tf_op jit(solution)/shard_map/all_to_all | solution.py:432
  117.1 4.7 %gather_fusion.2 = bf16[1280,256]{1,0:T(8,128)(2,1)} fusion(bf16[2560,256]{1,0:T(8,128)(2,1)S(1)} %bitcast.43, s32[2048]{0:T(1024)S(1)} %pad_clamp_fusion.1), kind=kCustom, calls=%fused_computation.2 | custom fusion | bytes 1315840 | tf_op jit(solution)/shard_map/gather | solution.py:516
  121.7 6.0 %attend.1 = (bf16[128,256]{1,0:T(8,128)(2,1)}, bf16[512,256]{1,0:T(8,128)(2,1)}, bf16[768,256]{1,0:T(8,128)(2,1)}) custom-call(bf16[1280,256]{1,0:T(8,128)(2,1)} %gather_fusion.2, bf16[128,256]{1,0:T(8,128)(2,1)} %get-tuple-element.63.q_rows, bf16[128,256]{1,0:T(8,128)(2,1)} %get-tuple-element.64.q_proj, bf16[128,256]{1,0:T(8,128)(2,1)} %grad.1, ...), custom_call_target="tpu_custom_call" | custom-call | tf_op jit(solution)/shard_map/attend/pallas_call | solution.py:61
  127.7 3.6 %all-to-all-start.4 = ((bf16[32,16,256]{2,1,0:T(8,128)(2,1)}), bf16[32,16,256]{2,1,0:T(8,128)(2,1)S(1)}, u32[]{:S(2)}, u32[]{:S(2)}) async-start(bf16[32,16,256]{2,1,0:T(8,128)(2,1)} %bitcast.60), calls=%async_computation.4 | async-start | bytes 524288 | tf_op jit(solution)/shard_map/all_to_all | solution.py:432
  131.4 10.6 %all-to-all-done.4 = bf16[32,16,256]{2,1,0:T(8,128)(2,1)S(1)} async-done(((bf16[32,16,256]{2,1,0:T(8,128)(2,1)}), bf16[32,16,256]{2,1,0:T(8,128)(2,1)S(1)}, u32[]{:S(2)}, u32[]{:S(2)}) %all-to-all-start.4) | async-done | bytes 262176 | tf_op jit(solution)/shard_map/all_to_all | solution.py:432
  142.0 0.7 reshape.326.scal
  142.7 14.5 %back.1 = bf16[2,2176,128]{2,1,0:T(8,128)(2,1)} custom-call(bf16[4,2560]{1,0:T(4,128)(2,1)} %reshape.326.scal, s32[1,2560]{1,0:T(1,128)} %and_select_fusion.nrow, bf16[4096,256]{1,0:T(8,128)(2,1)} %all-gather.5.cloned.1.call-done.qsrc, bf16[2560,128]{1,0:T(8,128)(2,1)} %hot.1.hots, bf16[2560,256]{1,0:T(8,128)(2,1)} %gather_fusion.1, ...), custom_call_target="tpu_custom_call" | custom-call | tf_op jit(solution)/shard_map/back/pallas_call | solution.py:540
  157.2 1.1 slice_bitcast_fusion
  158.3 0.1 collective-permute-start
  158.4 1.9 collective-permute-done
  160.4 1.2 fusion
  161.6 20.7 %all_to_all.35.x = bf16[16,136,128]{2,1,0:T(8,128)(2,1)} all-to-all(bf16[16,136,128]{2,1,0:T(8,128)(2,1)S(1)} %bitcast.45), channel_id=1, replica_groups={{0,2,4,6,8,10,12,14,16,18,20,22,24,26,28,30},{1,3,5,7,9,11,13,15,17,19,..., dimensions={0} | all-to-all | bytes 1114112 | tf_op jit(solution)/shard_map/all_to_all | solution.py:559
  182.2 2.0 spread.1
  184.2 19.7 %all_to_all.36 = bf16[16,136,128]{2,1,0:T(8,128)(2,1)S(1)} all-to-all(bf16[16,136,128]{2,1,0:T(8,128)(2,1)} %spread.1), channel_id=1, replica_groups={{0,2,4,6,8,10,12,14,16,18,20,22,24,26,28,30},{1,3,5,7,9,11,13,15,17,19,..., dimensions={0} | all-to-all | bytes 1114112 | tf_op jit(solution)/shard_map/all_to_all | solution.py:563
  203.9 2.0 collective-permute-done.1.other
  205.8 0.8 copy-done.6
  206.7 2.8 %unpack.1 = (f32[128,768]{1,0:T(8,128)}, f32[256,512]{1,0:T(8,128)}, f32[256,256]{1,0:T(8,128)}, f32[512,128]{1,0:T(8,128)}, f32[256,256]{1,0:T(8,128)}, /*index=5*/f32[256,256]{1,0:T(8,128)}, f32[256,256]{1,0:T(8,128)}) custom-call(bf16[2176,128]{1,0:T(8,128)(2,1)} %bitcast.47, bf16[2176,128]{1,0:T(8,128)(2,1)} %copy-done.6, s32[1,1]{1,0:T(1,128)} %bitcast.22.parity), custom_call_target="tpu_custom_call" | custom-call | tf_op jit(solution)/shard_map/unpack/pallas_call | solution.py:571
  (37 shorter events, 0.2 us)
Async XLA Ops:
  7.2 88.7 %all-gather.3.cloned.1.call-start = ((), (), s32[]{:S(2)}) async-start(), calls=%async_computation.7 | async-start | bytes 2162688 | tf_op jit(solution)/shard_map/all_gather | solution.py:450
  7.2 4.5 %copy-start.9 = (s32[128,10,1]{0,2,1:T(1,128)S(1)}, s32[128,10,1]{0,2,1:T(1,128)}, u32[]{:S(2)}) copy-start(s32[128,10,1]{0,2,1:T(1,128)} %param.24) | copy-start | bytes 15364
  30.7 17.9 %copy-start.1 = (s32[32,1,112]{2,1,0:T(1,128)}, s32[32,1,112]{2,1,0:T(1,128)S(1)}, u32[]{:S(2)}) copy-start(s32[32,1,112]{2,1,0:T(1,128)S(1)} %all_to_all.37) | copy-start | bytes 43012
  30.7 17.9 %all-to-all-start.1 = ((bf16[32,16,128]{2,1,0:T(8,128)(2,1)}), bf16[32,16,128]{2,1,0:T(8,128)(2,1)S(1)}, u32[]{:S(2)}, u32[]{:S(2)}) async-start(bf16[32,16,128]{2,1,0:T(8,128)(2,1)} %bitcast.61), calls=%async_computation.1 | async-start | bytes 262144 | tf_op jit(solution)/shard_map/all_to_all | solution.py:432
  48.6 0.7 copy-start.4
  57.4 15.2 %all-to-all-start.3 = ((bf16[32,8,256]{2,1,0:T(8,128)(2,1)}), bf16[32,8,256]{2,1,0:T(8,128)(2,1)S(1)}, u32[]{:S(2)}, u32[]{:S(2)}) async-start(bf16[32,8,256]{2,1,0:T(8,128)(2,1)} %bitcast.62), calls=%async_computation.3 | async-start | bytes 262144 | tf_op jit(solution)/shard_map/all_to_all | solution.py:432
  63.2 79.5 %all-gather.5.cloned.1.call-start = ((), (), s32[]{:S(2)}) async-start(), calls=%async_computation.8 | async-start | bytes 2162688 | tf_op jit(solution)/shard_map/all_gather | solution.py:497
  72.6 8.5 %copy-start.10 = (s32[1,128]{1,0:T(1,128)S(1)}, s32[1,128]{1,0:T(1,128)}, u32[]{:S(2)}) copy-start(s32[1,128]{1,0:T(1,128)} %get-tuple-element.58.dplace) | copy-start | bytes 1540
  72.6 9.1 %copy-start.8 = (s32[10,128]{1,0:T(8,128)S(1)}, s32[10,128]{1,0:T(8,128)}, u32[]{:S(2)}) copy-start(s32[10,128]{1,0:T(8,128)} %get-tuple-element.55.nrank) | copy-start | bytes 15364
  72.6 0.7 copy-start.7
  75.2 11.4 %copy-start.2 = (s32[32,1,112]{2,1,0:T(1,128)S(1)}, s32[32,1,112]{2,1,0:T(1,128)}, u32[]{:S(2)}) copy-start(s32[32,1,112]{2,1,0:T(1,128)} %copy-done.1) | copy-start | bytes 43012
  75.2 13.3 %copy-start.5 = (bf16[512,256]{1,0:T(8,128)(2,1)S(1)}, bf16[512,256]{1,0:T(8,128)(2,1)}, u32[]{:S(2)}) copy-start(bf16[512,256]{1,0:T(8,128)(2,1)} %get-tuple-element.52.new) | copy-start | bytes 786436
  75.2 41.9 %all-to-all-start.2 = ((bf16[32,80,256]{2,1,0:T(8,128)(2,1)}), bf16[32,80,256]{2,1,0:T(8,128)(2,1)S(1)}, u32[]{:S(2)}, u32[]{:S(2)}) async-start(bf16[32,80,256]{2,1,0:T(8,128)(2,1)} %bitcast.44), calls=%async_computation.2 | async-start | bytes 2621440 | tf_op jit(solution)/shard_map/all_to_all | solution.py:432
  127.7 14.2 %all-to-all-start.4 = ((bf16[32,16,256]{2,1,0:T(8,128)(2,1)}), bf16[32,16,256]{2,1,0:T(8,128)(2,1)S(1)}, u32[]{:S(2)}, u32[]{:S(2)}) async-start(bf16[32,16,256]{2,1,0:T(8,128)(2,1)} %bitcast.60), calls=%async_computation.4 | async-start | bytes 524288 | tf_op jit(solution)/shard_map/all_to_all | solution.py:432
  142.0 0.8 copy-start.3
  158.3 2.0 collective-permute-start
  203.9 2.0 copy-start
  203.9 2.0 collective-permute-start.1
  205.8 0.8 copy-start.6
Sparse Core Ops, SparseCore 0:
  11.9 59.8 all-gather.2
  75.3 61.8 all-gather.4

commit v3 on v2

--- a/solution.py
+++ b/solution.py
@@ -108,19 +108,45 @@
     req[:, 4 * ce : 4 * ce + cn] = total.astype(I32) - 1
 
 
+def widen_rows(source, target):
+    step = 256
+
+    def run(i, carry):
+        b = pl.ds(pl.multiple_of(i * step, step), step)
+        target[b, :] = source[b, :].astype(F32)
+        return carry
+
+    lax.fori_loop(0, source.shape[0] // step, run, 0)
+
+
 def owner_body(
-    ce, rows, feats, got, w_msg, w_in, u_zr, u_h,
-    new, dst_new, sfirst, scol, fcol, code, pre, mean, div, upd, rst, cand, rstate, msg, bcol,
+    ce, cn, shift, memory, feats, got, slots_s, w_msg, w_in, u_zr, u_h,
+    new, dst_new, reply, rows, sfirst, scol, fcol, code, pre, mean, div, upd, rst, cand, rstate,
+    msg, bcol, table, wide, copied,
 ):
     n, f = feats.shape
-    m = rows.shape[1]
+    acc_rows, m = memory.shape
+    devices = got.shape[0]
     t = w_msg.shape[0] - m - f
     step = 128
+    widen_rows(memory, table)
+    group = math.gcd(ce, 8)
+
+    def side_rows(i, carry):
+        d, g = i // (2 * ce // group), i % (2 * ce // group)
+        base = pl.multiple_of(i * group, group)
+        for p in range(group):
+            slot = jnp.maximum(slots_s[d, g * group + p], 0)
+            wide[pl.ds(base + p, 1), :] = table[pl.ds(slot, 1), :]
+        return carry
+
+    lax.fori_loop(0, n // group, side_rows, 0, unroll=2)
     frequency = jnp.exp(iota((1, t), 1).astype(F32) * (-11.5 / t))
-    table = got[:, : 4 * ce].astype(F32)
-    scol[...] = to_col(table, n, 2 * ce, 0).astype(I32)
-    bcol[...] = to_col(table, n, 2 * ce, 2 * ce)
-    slots = to_row(table, n, 2 * ce, 0).astype(I32)
+    numbers = got[:, : 4 * ce].astype(F32)
+    scol[...] = to_col(numbers, n, 2 * ce, 0).astype(I32)
+    bcol[...] = to_col(numbers, n, 2 * ce, 2 * ce)
+    slots = to_row(numbers, n, 2 * ce, 0).astype(I32)
+    rows[...] = jnp.where(scol[...] >= 0, wide[...], 0.0).astype(BF16)
 
     def messages(i, carry):
         b = pl.ds(pl.multiple_of(i * step, step), step)
@@ -161,7 +187,9 @@
         rst[b, :] = reset
         cand[b, :] = candidate
         rstate[b, :] = reset_state
-        new[b, :] = ((1.0 - update) * state_wide + update * candidate).astype(BF16)
+        fresh = ((1.0 - update) * state_wide + update * candidate).astype(BF16)
+        new[b, :] = fresh
+        wide[b, :] = fresh.astype(F32)
         return early
 
     early = lax.fori_loop(0, n // step, gru, jnp.zeros((1, n), F32))
@@ -171,11 +199,38 @@
     pick = (iota((half, n), 1) == r + (r // ce + 1) * ce).astype(F32).astype(BF16)
     dst_new[...] = dot(pick, new[...]).astype(BF16)
 
-
-def patch_body(events, ce, cn, block, old, got, sfirst, new, out):
-    table = got[:, 4 * ce :].astype(F32)
-    code = to_col(table, block, cn, 0, pl.program_id(0) * block).astype(I32)
-    hit = (code // events == sfirst[...]).astype(F32).astype(BF16)
+    def store_rows(i, carry):
+        d, g = i // (2 * ce // group), i % (2 * ce // group)
+        base = pl.multiple_of(i * group, group)
+        for p in range(group):
+            slot = slots_s[d, g * group + p]
+            slot = jnp.where(slot >= 0, slot, acc_rows)
+            table[pl.ds(slot, 1), :] = wide[pl.ds(base + p, 1), :]
+        return carry
+
+    lax.fori_loop(0, n // group, store_rows, 0, unroll=2)
+    bunch = math.gcd(cn, 8)
+
+    def nb_rows(i, carry):
+        d, g = i // (cn // bunch), i % (cn // bunch)
+        lane = 4 * ce + g * bunch
+
+        @pl.when(slots_s[d, lane] >= 0)
+        def _():
+            base = pl.multiple_of(i * bunch, bunch)
+            for p in range(bunch):
+                slot = jnp.maximum(slots_s[d, lane + p], 0) >> shift
+                copied[pl.ds(base + p, 1), :] = table[pl.ds(slot, 1), :]
+
+        return carry
+
+    lax.fori_loop(0, devices * cn // bunch, nb_rows, 0)
+    reply[...] = copied[...].astype(BF16)
+
+
+def refresh_body(block, old, sfirst, new, out):
+    row = iota((block, 1), 0) + pl.program_id(0) * block
+    hit = (row == sfirst[...]).astype(F32).astype(BF16)
     rows = dot(hit, new[...])
     found = dot(hit, jnp.ones((new.shape[0], 128), BF16)) > 0.5
     for h in range(rows.shape[1] // 128):
@@ -183,24 +238,22 @@
         out[:, c] = jnp.where(found, rows[:, c], old[:, c].astype(F32)).astype(BF16)
 
 
-def patch(events, ce, cn, fetched, got, sfirst, new):
-    s, m = new.shape
-    n = fetched.shape[0] - s
+def refresh(memory, sfirst, new):
+    n, m = memory.shape
+    s = new.shape[0]
     block = 512
-    skip = s // block
     return pl.pallas_call(
-        functools.partial(patch_body, events, ce, cn, block),
+        functools.partial(refresh_body, block),
         grid=(n // block,),
         out_shape=jax.ShapeDtypeStruct((n, m), BF16),
         in_specs=[
-            pl.BlockSpec((block, m), lambda i: (i + skip, 0)),
-            pl.BlockSpec(got.shape, lambda i: (0, 0)),
+            pl.BlockSpec((block, m), lambda i: (i, 0)),
             pl.BlockSpec((1, s), lambda i: (0, 0)),
             pl.BlockSpec((s, m), lambda i: (0, 0)),
         ],
         out_specs=pl.BlockSpec((block, m), lambda i: (i, 0)),
-        name="patch",
-    )(fetched, got, sfirst, new)
+        name="refresh",
+    )(memory, sfirst, new)
 
 
 def hot_body(events, ce, cn, block, got, out):
@@ -466,28 +519,35 @@
     )
     got = exchange(req.reshape(devices, 1, 4 * ce + cn)).reshape(devices, 4 * ce + cn)
     got_feats = exchange(side_feats.reshape(devices, 2 * ce, feat)).reshape(n_side, feat)
-    side_slots = got[:, : 2 * ce].reshape(n_side)
-    nb_code = got[:, 4 * ce :].reshape(n_nb)
-    wanted = jnp.concatenate([side_slots, nb_code // events])
-    fetched = memory[jnp.maximum(wanted, 0)]
+    vm = pl.BlockSpec(memory_space=pltpu.VMEM)
+    sm = pl.BlockSpec(memory_space=pltpu.SMEM)
+    shift = events.bit_length() - 1
+    assert 1 << shift == events
+    owner_outs = [
+        ((n_side, m), BF16), ((n_dst, m), BF16), ((n_nb, m), BF16), ((n_side, m), BF16),
+        ((1, n_side), I32), ((n_side, 1), I32), ((n_side, 1), F32),
+        ((n_side, w_msg.shape[0] - m - feat), BF16),
+        ((n_side, width), F32), ((n_side, width), BF16), ((n_side, width), F32),
+        ((n_side, m), F32), ((n_side, m), F32), ((n_side, m), F32), ((n_side, m), BF16),
+    ]
     (
-        new_side, dst_new, sfirst, scol, fcol, code, pre, mean, div, upd, rst, cand, rstate,
-    ) = call(
-        functools.partial(owner_body, ce),
-        [
-            ((n_side, m), BF16), ((n_dst, m), BF16), ((1, n_side), I32), ((n_side, 1), I32),
-            ((n_side, 1), F32), ((n_side, w_msg.shape[0] - m - feat), BF16),
-            ((n_side, width), F32), ((n_side, width), BF16), ((n_side, width), F32),
-            ((n_side, m), F32), ((n_side, m), F32), ((n_side, m), F32), ((n_side, m), BF16),
+        new_side, dst_new, nb_reply, fetched, sfirst, scol, fcol, code, pre, mean, div,
+        upd, rst, cand, rstate,
+    ) = pl.pallas_call(
+        functools.partial(owner_body, ce, cn, shift),
+        out_shape=[jax.ShapeDtypeStruct(a, d) for a, d in owner_outs],
+        in_specs=[vm, vm, vm, sm, vm, vm, vm, vm],
+        out_specs=[vm] * len(owner_outs),
+        scratch_shapes=[
+            pltpu.VMEM((n_side, width), BF16), pltpu.VMEM((n_side, 1), F32),
+            pltpu.VMEM((acc_rows + 8, m), F32), pltpu.VMEM((n_side, m), F32),
+            pltpu.VMEM((n_nb, m), F32),
         ],
-        (fetched, got_feats, got, w_msg, w_in, u_zr, u_h),
-        "owner",
-        scratch=[pltpu.VMEM((n_side, width), BF16), pltpu.VMEM((n_side, 1), F32)],
-    )
+        compiler_params=pltpu.CompilerParams(vmem_limit_bytes=VMEM_LIMIT),
+        name="owner",
+    )(memory, got_feats, got, got, w_msg, w_in, u_zr, u_h)
     back_dst = exchange(dst_new.reshape(devices, ce, m)).reshape(n_dst, m)
-    nb_reply = patch(events, ce, cn, fetched, got, sfirst, new_side)
     back_nb = exchange(nb_reply.reshape(devices, cn, m))
-    back_dst, nb_reply = lax.optimization_barrier((back_dst, nb_reply))
     q_rows, q_proj = call(
         query_body,
         [((events, m), BF16), ((events, m), BF16)],
@@ -496,11 +556,8 @@
     )
     proj_all = lax.all_gather(q_proj, AXES, axis=0, tiled=True)
     each = max(2 * ce, -(-(ce + 4) // 8) * 8)
-    late_memory, late_got, _ = lax.optimization_barrier((memory, got, nb_reply))
-    late_slots = late_got[:, : 2 * ce].reshape(n_side)
-    new_memory = late_memory.at[jnp.where(late_slots >= 0, late_slots, acc_rows)].set(
-        new_side, mode="drop"
-    )
+    late_got, _ = lax.optimization_barrier((got, nb_reply))
+    new_memory = refresh(memory, sfirst, new_side)
     late_code = late_got[:, 4 * ce :].reshape(n_nb)
     table = jnp.maximum(late_code, 0) % events + jnp.arange(n_nb, dtype=I32) // cn * events
     ge = grad_all[table]
@@ -535,8 +592,6 @@
         got_feats, code, pre, mean, div, upd, rst, cand, rstate, w_in, u_h, w_key, w_value,
         g_qkv, parity,
     )
-    vm = pl.BlockSpec(memory_space=pltpu.VMEM)
-    sm = pl.BlockSpec(memory_space=pltpu.SMEM)
     halves = pl.pallas_call(
         functools.partial(back_body, direct),
         out_shape=jax.ShapeDtypeStruct((2, half, 128), BF16),

time: 217 us -> 228 us (1.051)
  Pallas kernels: 53.6 us -> 87.1 us
  local copies, waits for them, and re-layouts: 46.1 us -> 18.5 us
  blocking collectives: 54.7 us -> 77.7 us
  starting transfers between devices: 18 us -> 6.8 us
  waiting for transfers between devices: 27.1 us -> 21.5 us
    pallas_call x1 -> x2, Pallas kernels: 9.32 us -> 51.3 us  [the longest x1 37.9 us: body(): pl.pallas_call(functools.partial(owner_body, ce, cn, shift), out_shape=[j...]
    all_to_all x1 -> x3, blocking collectives: 14.4 us -> 37.3 us  [exchange(): return lax.all_to_all(x, AXES, split_axis=0, concat_axis=0, tiled=True)]
    gather x1 -> x0, local copies, waits for them, and re-layouts: 15 us -> none  [body(): fetched = memory[jnp.maximum(wanted, 0)]]
    all_to_all x4 -> x2, starting transfers between devices: 17.9 us -> 6.65 us  [exchange(): return lax.all_to_all(x, AXES, split_axis=0, concat_axis=0, tiled=True)]
    pallas_call x5 -> x4, Pallas kernels: 22 us -> 13.9 us  [call(): pl.pallas_call(body, out_shape=[jax.ShapeDtypeStruct(s, d) for s, d in ou...]
    scatter x1 -> x0, local copies, waits for them, and re-layouts: 7.37 us -> none  [body(): late_memory.at[jnp.where(late_slots >= 0, late_slots, acc_rows)]]
    all_to_all x4 -> x2, waiting for transfers between devices: 23.1 us -> 16.9 us  [exchange(): return lax.all_to_all(x, AXES, split_axis=0, concat_axis=0, tiled=True)]
    optimization_barrier x1 -> x0, local copies, waits for them, and re-layouts: 4.48 us -> none  [body(): late_memory, late_got, _ = lax.optimization_barrier((memory, got, nb_reply))]
  transfers between devices with their start and end apart: 8 -> 6, of which waited for: 4 -> 4; matrix products, arithmetic and copies ran while one was open for 18% -> 8% of each run, Pallas kernels for 16% -> 30%
where the time goes in v3:
time: 228 us; the launch traced here: 227 us
  Pallas kernels  87.1 us (38%)
  blocking collectives  77.7 us (34%)
  waiting for transfers between devices  21.5 us (9%)
  local copies, waits for them, and re-layouts  18.5 us (8%)
  between operations  14.2 us (6%)
  starting transfers between devices  6.8 us (3%)
    pallas_call x1, Pallas kernels, body(): pl.pallas_call(functools.partial(owner_body, ce, cn, shift), out_shape=[j...  37.9 us
    all_to_all x3, blocking collectives, exchange(): return lax.all_to_all(x, AXES, split_axis=0, concat_axis=0, tiled=True)  37.3 us
    all_to_all x1, blocking collectives, body(): lax.all_to_all(half_sum, AXES, split_axis=0, concat_axis=0, tiled=True, a...  20.7 us
    all_to_all x1, blocking collectives, body(): lax.all_to_all(spread, AXES, split_axis=0, concat_axis=0, tiled=True, axi...  19.7 us
    all_to_all x2, waiting for transfers between devices, exchange(): return lax.all_to_all(x, AXES, split_axis=0, concat_axis=0, tiled=True)  16.9 us
    pallas_call x1, Pallas kernels, body(): pl.pallas_call(functools.partial(back_body, direct), out_shape=jax.ShapeD...  14.2 us
    pallas_call x4, Pallas kernels, call(): pl.pallas_call(body, out_shape=[jax.ShapeDtypeStruct(s, d) for s, d in ou...  13.9 us
    pallas_call x1, Pallas kernels, refresh(): pl.pallas_call(functools.partial(refresh_body, block), grid=(n // block,)...  13.4 us
  transfers between devices with their start and end apart: 6, of which 4 were waited for; matrix products, arithmetic and copies ran while one was open for 8% of the time, Pallas kernels for 30%

profile of v3, /device:TPU:0, one launch (start us, length us, event | category | flops | bytes accessed | tf_op | source)
XLA Modules:
  0.0 227.3 jit_solution(18238959990511093701)
XLA Ops:
  7.2 0.0 all-gather.3.cloned.1.call-start
  7.2 0.7 all-gather.3.cloned.1.call-update
  7.9 0.0 all-gather.5.cloned.1.call-start
  8.0 1.3 copy.34
  9.2 4.0 %place.1 = (s32[32,112]{1,0:T(8,128)}, bf16[512,128]{1,0:T(8,128)(2,1)}, s32[1,128]{1,0:T(1,128)}, s32[10,128]{1,0:T(8,128)}) custom-call(s32[1,128]{1,0:T(1,128)} %bitcast.60, s32[1,128]{1,0:T(1,128)} %bitcast.61, s32[1,128]{1,0:T(1,128)} %bitcast.62, s32[1,128]{1,0:T(1,128)} %bitcast.63, s32[10,128]{1,0:T(8,128)} %bitcast.56, s32[10,128]{1,0:T(8,128)} %bitcast.59, ...), custom_call_target="tpu_custom_call" | custom-call | tf_op jit(solution)/shard_map/place/pallas_call | solution.py:61
  13.3 14.3 %all_to_all.35 = s32[32,1,112]{2,1,0:T(1,128)} all-to-all(s32[32,1,112]{2,1,0:T(1,128)} %bitcast.58), channel_id=1, replica_groups=mesh['acct'=8,'rep'=4] {'acct','rep'}, dimensions={0} | all-to-all | bytes 28672 | tf_op jit(solution)/shard_map/all_to_all | solution.py:485
  27.6 11.5 %all_to_all.36 = bf16[32,16,128]{2,1,0:T(8,128)(2,1)} all-to-all(bf16[32,16,128]{2,1,0:T(8,128)(2,1)} %bitcast.55), channel_id=1, replica_groups=mesh['acct'=8,'rep'=4] {'acct','rep'}, dimensions={0} | all-to-all | bytes 262144 | tf_op jit(solution)/shard_map/all_to_all | solution.py:485
  39.1 37.9 %owner.1 = (bf16[512,256]{1,0:T(8,128)(2,1)}, bf16[256,256]{1,0:T(8,128)(2,1)}, bf16[2560,256]{1,0:T(8,128)(2,1)}, bf16[512,256]{1,0:T(8,128)(2,1)}, s32[1,512]{...) custom-call(bf16[8192,256]{1,0:T(8,128)(2,1)} %old.1, ...), custom_call_target="tpu_custom_call" | custom-call | tf_op jit(solution)/shard_map/owner/pallas_call | solution.py:536
  76.9 11.5 %all_to_all.37 = bf16[32,8,256]{2,1,0:T(8,128)(2,1)} all-to-all(bf16[32,8,256]{2,1,0:T(8,128)(2,1)} %bitcast.54), channel_id=1, replica_groups=mesh['acct'=8,'rep'=4] {'acct','rep'}, dimensions={0} | all-to-all | bytes 262144 | tf_op jit(solution)/shard_map/all_to_all | solution.py:485
  88.5 1.9 query.1
  90.4 0.0 all-gather.5.cloned.1.call-update
  90.4 0.0 copy-start.8
  90.4 0.0 copy-start.6
  90.4 0.0 copy-start.7
  90.5 0.0 copy-start.3
  90.5 0.0 copy-start.4
  90.5 2.8 %all-to-all-start.2 = ((bf16[32,80,256]{2,1,0:T(8,128)(2,1)}), bf16[32,80,256]{2,1,0:T(8,128)(2,1)S(1)}, u32[]{:S(2)}, u32[]{:S(2)}) async-start(bf16[32,80,256]{2,1,0:T(8,128)(2,1)} %bitcast.43), calls=%async_computation.2 | async-start | bytes 2621440 | tf_op jit(solution)/shard_map/all_to_all | solution.py:485
  93.3 0.6 fusion.4.dback
  93.9 0.1 slice.16
  94.0 4.9 %hot.1.hots = bf16[2560,128]{1,0:T(8,128)(2,1)} custom-call(s32[32,112]{1,0:T(8,128)} %bitcast.49), custom_call_target="tpu_custom_call" | custom-call | tf_op jit(solution)/shard_map/hot/pallas_call | solution.py:268
  98.9 0.1 fusion.5
  99.0 0.1 rem.84
  99.1 0.1 reshape.252
  99.2 0.1 concatenate.3
  99.2 0.7 reshape.253.drow
  99.9 13.4 %refresh.1 = bf16[8192,256]{1,0:T(8,128)(2,1)} custom-call(bf16[8192,256]{1,0:T(8,128)(2,1)} %old.1, s32[1,512]{1,0:T(1,128)} %get-tuple-element.52.sfirst, bf16[512,256]{1,0:T(8,128)(2,1)} %get-tuple-element.53.new), custom_call_target="tpu_custom_call" | custom-call | tf_op jit(solution)/shard_map/refresh/pallas_call | solution.py:245
  113.4 0.1 fusion.2
  113.4 0.6 and_select_fusion.nrow
  114.1 8.7 %gather_fusion = bf16[2560,256]{1,0:T(8,128)(2,1)} fusion(bf16[4096,256]{1,0:T(8,128)(2,1)} %all-gather.3.cloned.1.call-done, s32[3072]{0:T(1024)S(1)} %pad_clamp_fusion), kind=kCustom, calls=%fused_computation | custom fusion | bytes 2631680 | tf_op jit(solution)/shard_map/gather | solution.py:563
  122.8 6.5 %all-to-all-done.2 = bf16[32,80,256]{2,1,0:T(8,128)(2,1)S(1)} async-done(((bf16[32,80,256]{2,1,0:T(8,128)(2,1)}), bf16[32,80,256]{2,1,0:T(8,128)(2,1)S(1)}, u32[]{:S(2)}, u32[]{:S(2)}) %all-to-all-start.2) | async-done | bytes 1310752 | tf_op jit(solution)/shard_map/all_to_all | solution.py:485
  129.3 4.7 %gather_fusion.1 = bf16[1280,256]{1,0:T(8,128)(2,1)} fusion(bf16[2560,256]{1,0:T(8,128)(2,1)S(1)} %bitcast.39, s32[2048]{0:T(1024)S(1)} %pad_clamp_fusion.1), kind=kCustom, calls=%fused_computation.1 | custom fusion | bytes 1315840 | tf_op jit(solution)/shard_map/gather | solution.py:573
  134.0 6.0 %attend.1 = (bf16[128,256]{1,0:T(8,128)(2,1)}, bf16[512,256]{1,0:T(8,128)(2,1)}, bf16[768,256]{1,0:T(8,128)(2,1)}) custom-call(bf16[1280,256]{1,0:T(8,128)(2,1)} %gather_fusion.1, bf16[128,256]{1,0:T(8,128)(2,1)} %get-tuple-element.62.q_rows, bf16[128,256]{1,0:T(8,128)(2,1)} %get-tuple-element.63.q_proj, bf16[128,256]{1,0:T(8,128)(2,1)} %grad.1, ...), custom_call_target="tpu_custom_call" | custom-call | tf_op jit(solution)/shard_map/attend/pallas_call | solution.py:61
  140.0 3.8 %all-to-all-start.4 = ((bf16[32,16,256]{2,1,0:T(8,128)(2,1)}), bf16[32,16,256]{2,1,0:T(8,128)(2,1)S(1)}, u32[]{:S(2)}, u32[]{:S(2)}) async-start(bf16[32,16,256]{2,1,0:T(8,128)(2,1)} %bitcast.53), calls=%async_computation.4 | async-start | bytes 524288 | tf_op jit(solution)/shard_map/all_to_all | solution.py:485
  143.8 10.4 %all-to-all-done.4 = bf16[32,16,256]{2,1,0:T(8,128)(2,1)S(1)} async-done(((bf16[32,16,256]{2,1,0:T(8,128)(2,1)}), bf16[32,16,256]{2,1,0:T(8,128)(2,1)S(1)}, u32[]{:S(2)}, u32[]{:S(2)}) %all-to-all-start.4) | async-done | bytes 262176 | tf_op jit(solution)/shard_map/all_to_all | solution.py:485
  154.3 0.7 reshape.259.scal
  155.0 14.2 %back.1 = bf16[2,2176,128]{2,1,0:T(8,128)(2,1)} custom-call(bf16[4,2560]{1,0:T(4,128)(2,1)} %reshape.259.scal, s32[1,2560]{1,0:T(1,128)} %and_select_fusion.nrow, bf16[4096,256]{1,0:T(8,128)(2,1)} %all-gather.5.cloned.1.call-done.qsrc, bf16[2560,128]{1,0:T(8,128)(2,1)} %hot.1.hots, bf16[2560,256]{1,0:T(8,128)(2,1)} %gather_fusion, ...), custom_call_target="tpu_custom_call" | custom-call | tf_op jit(solution)/shard_map/back/pallas_call | solution.py:595
  169.1 1.2 slice_bitcast_fusion
  170.3 0.1 collective-permute-start
  170.4 1.9 collective-permute-done
  172.4 0.1 fusion
  172.5 20.7 %all_to_all.38.x = bf16[16,136,128]{2,1,0:T(8,128)(2,1)} all-to-all(bf16[16,136,128]{2,1,0:T(8,128)(2,1)S(1)} %bitcast.40), channel_id=1, replica_groups={{0,2,4,6,8,10,12,14,16,18,20,22,24,26,28,30},{1,3,5,7,9,11,13,15,17,19,..., dimensions={0} | all-to-all | bytes 1114112 | tf_op jit(solution)/shard_map/all_to_all | solution.py:614
  193.2 2.0 spread.1
  195.2 19.7 %all_to_all.39 = bf16[16,136,128]{2,1,0:T(8,128)(2,1)S(1)} all-to-all(bf16[16,136,128]{2,1,0:T(8,128)(2,1)} %spread.1), channel_id=1, replica_groups={{0,2,4,6,8,10,12,14,16,18,20,22,24,26,28,30},{1,3,5,7,9,11,13,15,17,19,..., dimensions={0} | all-to-all | bytes 1114112 | tf_op jit(solution)/shard_map/all_to_all | solution.py:618
  214.9 0.0 collective-permute-start.1
  214.9 2.0 collective-permute-done.1.other
  216.8 0.0 copy-done.1
  216.8 0.8 copy-done.5
  217.7 2.8 %unpack.1 = (f32[128,768]{1,0:T(8,128)}, f32[256,512]{1,0:T(8,128)}, f32[256,256]{1,0:T(8,128)}, f32[512,128]{1,0:T(8,128)}, f32[256,256]{1,0:T(8,128)}, /*index=5*/f32[256,256]{1,0:T(8,128)}, f32[256,256]{1,0:T(8,128)}) custom-call(bf16[2176,128]{1,0:T(8,128)(2,1)} %bitcast.42, bf16[2176,128]{1,0:T(8,128)(2,1)} %copy-done.5, s32[1,1]{1,0:T(1,128)} %bitcast.20.parity), custom_call_target="tpu_custom_call" | custom-call | tf_op jit(solution)/shard_map/unpack/pallas_call | solution.py:626
  (19 shorter events, 0.1 us)
Async XLA Ops:
  7.2 106.9 %all-gather.3.cloned.1.call-start = ((), (), s32[]{:S(2)}) async-start(), calls=%async_computation.7 | async-start | bytes 2162688 | tf_op jit(solution)/shard_map/all_gather | solution.py:503
  7.9 147.1 %all-gather.5.cloned.1.call-start = ((), (), s32[]{:S(2)}) async-start(), calls=%async_computation.8 | async-start | bytes 2162688 | tf_op jit(solution)/shard_map/all_gather | solution.py:557
  90.4 2.9 %copy-start.8 = (s32[1,128]{1,0:T(1,128)S(1)}, s32[1,128]{1,0:T(1,128)}, u32[]{:S(2)}) copy-start(s32[1,128]{1,0:T(1,128)} %get-tuple-element.57.dplace) | copy-start | bytes 1540
  90.4 3.5 %copy-start.6 = (s32[10,128]{1,0:T(8,128)S(1)}, s32[10,128]{1,0:T(8,128)}, u32[]{:S(2)}) copy-start(s32[10,128]{1,0:T(8,128)} %get-tuple-element.55.nrank) | copy-start | bytes 15364
  90.4 3.5 %copy-start.7 = (s32[128,10,1]{0,2,1:T(1,128)S(1)}, s32[128,10,1]{0,2,1:T(1,128)}, u32[]{:S(2)}) copy-start(s32[128,10,1]{0,2,1:T(1,128)} %param.24) | copy-start | bytes 15364
  90.5 3.5 %copy-start.3 = (s32[32,1,112]{2,1,0:T(1,128)S(1)}, s32[32,1,112]{2,1,0:T(1,128)}, u32[]{:S(2)}) copy-start(s32[32,1,112]{2,1,0:T(1,128)} %all_to_all.35) | copy-start | bytes 43012
  90.5 8.4 %copy-start.4 = (s32[32,1,112]{2,1,0:T(1,128)S(1)}, s32[32,1,112]{2,1,0:T(1,128)}, u32[]{:S(2)}) copy-start(s32[32,1,112]{2,1,0:T(1,128)} %all_to_all.35) | copy-start | bytes 43012
  90.5 38.8 %all-to-all-start.2 = ((bf16[32,80,256]{2,1,0:T(8,128)(2,1)}), bf16[32,80,256]{2,1,0:T(8,128)(2,1)S(1)}, u32[]{:S(2)}, u32[]{:S(2)}) async-start(bf16[32,80,256]{2,1,0:T(8,128)(2,1)} %bitcast.43), calls=%async_computation.2 | async-start | bytes 2621440 | tf_op jit(solution)/shard_map/all_to_all | solution.py:485
  140.0 14.3 %all-to-all-start.4 = ((bf16[32,16,256]{2,1,0:T(8,128)(2,1)}), bf16[32,16,256]{2,1,0:T(8,128)(2,1)S(1)}, u32[]{:S(2)}, u32[]{:S(2)}) async-start(bf16[32,16,256]{2,1,0:T(8,128)(2,1)} %bitcast.53), calls=%async_computation.4 | async-start | bytes 524288 | tf_op jit(solution)/shard_map/all_to_all | solution.py:485
  154.2 0.8 copy-start.2
  169.1 3.2 %copy-start = (bf16[2,2176,128]{2,1,0:T(8,128)(2,1)S(1)}, bf16[2,2176,128]{2,1,0:T(8,128)(2,1)}, u32[]{:S(2)}) copy-start(bf16[2,2176,128]{2,1,0:T(8,128)(2,1)} %back.1) | copy-start | bytes 3342340
  170.3 2.0 collective-permute-start
  214.9 2.0 copy-start.1
  214.9 2.0 collective-permute-start.1
  216.8 0.8 copy-start.5
Sparse Core Ops, SparseCore 0:
  10.9 59.1 all-gather.2
  90.5 58.1 all-gather.4

commit v4 on v3

--- a/solution.py
+++ b/solution.py
@@ -15,7 +15,9 @@
 BF16 = jnp.bfloat16
 I32 = jnp.int32
 EXACT = lax.Precision.HIGHEST
-VMEM_LIMIT = 56 * 1024 * 1024
+
+def room(mib):
+    return pltpu.CompilerParams(vmem_limit_bytes=mib * 1024 * 1024)
 
 
 def dot(a, b, **kw):
@@ -56,7 +58,7 @@
     return 1.0 / (1.0 + jnp.exp(-v))
 
 
-def call(body, outs, args, name, scratch=(), cost=None):
+def call(body, outs, args, name, mib, scratch=()):
     vm = pl.BlockSpec(memory_space=pltpu.VMEM)
     return pl.pallas_call(
         body,
@@ -64,8 +66,7 @@
         in_specs=[vm] * len(args),
         out_specs=[vm] * len(outs),
         scratch_shapes=list(scratch),
-        compiler_params=pltpu.CompilerParams(vmem_limit_bytes=VMEM_LIMIT),
-        cost_estimate=cost,
+        compiler_params=room(mib),
         name=name,
     )(*args)
 
@@ -119,34 +120,67 @@
     lax.fori_loop(0, source.shape[0] // step, run, 0)
 
 
+def pick_rows(table, target, slots_s, first, count, read):
+    rows = math.lcm(count, 8)
+    sources = rows // count
+
+    def block(i, carry):
+        for g in range(rows // 8):
+            found = []
+            for r in range(g * 8, g * 8 + 8):
+                where = read(slots_s[i * sources + r // count, first + r % count])
+                found.append(table[pl.ds(where, 1), :])
+            base = pl.multiple_of(i * rows + g * 8, 8)
+            target[pl.ds(base, 8), :] = jnp.concatenate(found, axis=0)
+        return carry
+
+    lax.fori_loop(0, slots_s.shape[0] // sources, block, 0)
+
+
+def sides_body(ce, memory, slots_s, rows, table, wide):
+    widen_rows(memory, table)
+    pick_rows(table, wide, slots_s, 0, 2 * ce, lambda v: jnp.maximum(v, 0))
+    rows[...] = wide[...].astype(BF16)
+
+
+def answer_body(ce, cn, shift, memory, new, slots_s, reply, table, wide, copied):
+    acc_rows = memory.shape[0]
+    widen_rows(memory, table)
+    wide[...] = new[...].astype(F32)
+
+    each = 2 * ce
+    rows = math.lcm(each, 8)
+    sources = rows // each
+
+    def store(i, carry):
+        fresh = wide[pl.ds(pl.multiple_of(i * rows, rows), rows), :]
+        for r in range(rows):
+            slot = slots_s[i * sources + r // each, r % each]
+            slot = jnp.where(slot >= 0, slot, acc_rows)
+            table[pl.ds(slot, 1), :] = fresh[r : r + 1, :]
+        return carry
+
+    lax.fori_loop(0, slots_s.shape[0] // sources, store, 0)
+    pick_rows(
+        table, copied, slots_s, 4 * ce, cn,
+        lambda v: lax.shift_right_logical(jnp.maximum(v, 0), shift),
+    )
+    reply[...] = copied[...].astype(BF16)
+
+
 def owner_body(
-    ce, cn, shift, memory, feats, got, slots_s, w_msg, w_in, u_zr, u_h,
-    new, dst_new, reply, rows, sfirst, scol, fcol, code, pre, mean, div, upd, rst, cand, rstate,
-    msg, bcol, table, wide, copied,
+    ce, rows, feats, got, w_msg, w_in, u_zr, u_h,
+    new, dst_new, sfirst, scol, fcol, code, pre, mean, div, upd, rst, cand, rstate, msg, bcol,
 ):
     n, f = feats.shape
-    acc_rows, m = memory.shape
-    devices = got.shape[0]
+    m = rows.shape[1]
     t = w_msg.shape[0] - m - f
     step = 128
-    widen_rows(memory, table)
-    group = math.gcd(ce, 8)
-
-    def side_rows(i, carry):
-        d, g = i // (2 * ce // group), i % (2 * ce // group)
-        base = pl.multiple_of(i * group, group)
-        for p in range(group):
-            slot = jnp.maximum(slots_s[d, g * group + p], 0)
-            wide[pl.ds(base + p, 1), :] = table[pl.ds(slot, 1), :]
-        return carry
-
-    lax.fori_loop(0, n // group, side_rows, 0, unroll=2)
     frequency = jnp.exp(iota((1, t), 1).astype(F32) * (-11.5 / t))
     numbers = got[:, : 4 * ce].astype(F32)
     scol[...] = to_col(numbers, n, 2 * ce, 0).astype(I32)
     bcol[...] = to_col(numbers, n, 2 * ce, 2 * ce)
     slots = to_row(numbers, n, 2 * ce, 0).astype(I32)
-    rows[...] = jnp.where(scol[...] >= 0, wide[...], 0.0).astype(BF16)
 
     def messages(i, carry):
         b = pl.ds(pl.multiple_of(i * step, step), step)
@@ -187,9 +221,7 @@
         rst[b, :] = reset
         cand[b, :] = candidate
         rstate[b, :] = reset_state
-        fresh = ((1.0 - update) * state_wide + update * candidate).astype(BF16)
-        new[b, :] = fresh
-        wide[b, :] = fresh.astype(F32)
+        new[b, :] = ((1.0 - update) * state_wide + update * candidate).astype(BF16)
         return early
 
     early = lax.fori_loop(0, n // step, gru, jnp.zeros((1, n), F32))
@@ -198,34 +230,6 @@
     r = iota((half, n), 0)
     pick = (iota((half, n), 1) == r + (r // ce + 1) * ce).astype(F32).astype(BF16)
     dst_new[...] = dot(pick, new[...]).astype(BF16)
-
-    def store_rows(i, carry):
-        d, g = i // (2 * ce // group), i % (2 * ce // group)
-        base = pl.multiple_of(i * group, group)
-        for p in range(group):
-            slot = slots_s[d, g * group + p]
-            slot = jnp.where(slot >= 0, slot, acc_rows)
-            table[pl.ds(slot, 1), :] = wide[pl.ds(base + p, 1), :]
-        return carry
-
-    lax.fori_loop(0, n // group, store_rows, 0, unroll=2)
-    bunch = math.gcd(cn, 8)
-
-    def nb_rows(i, carry):
-        d, g = i // (cn // bunch), i % (cn // bunch)
-        lane = 4 * ce + g * bunch
-
-        @pl.when(slots_s[d, lane] >= 0)
-        def _():
-            base = pl.multiple_of(i * bunch, bunch)
-            for p in range(bunch):
-                slot = jnp.maximum(slots_s[d, lane + p], 0) >> shift
-                copied[pl.ds(base + p, 1), :] = table[pl.ds(slot, 1), :]
-
-        return carry
-
-    lax.fori_loop(0, devices * cn // bunch, nb_rows, 0)
-    reply[...] = copied[...].astype(BF16)
 
 
 def refresh_body(block, old, sfirst, new, out):
@@ -252,6 +256,7 @@
             pl.BlockSpec((s, m), lambda i: (0, 0)),
         ],
         out_specs=pl.BlockSpec((block, m), lambda i: (i, 0)),
+        compiler_params=room(8),
         name="refresh",
     )(memory, sfirst, new)
 
@@ -271,6 +276,7 @@
         out_shape=jax.ShapeDtypeStruct((n, events), BF16),
         in_specs=[pl.BlockSpec(got.shape, lambda i: (0, 0))],
         out_specs=pl.BlockSpec((block, events), lambda i: (i, 0)),
+        compiler_params=room(6),
         name="hot",
     )(got)
 
@@ -366,30 +372,27 @@
     reply[...] = sent.astype(BF16)
 
 
+def expand_body(cn, source, hots, out):
+    events = hots.shape[1]
+
+    def run(d, carry):
+        b = pl.ds(pl.multiple_of(d * cn, cn), cn)
+        e = pl.ds(pl.multiple_of(d * events, events), events)
+        out[b, :] = dot(hots[b, :], source[e, :]).astype(BF16)
+        return carry
+
+    lax.fori_loop(0, hots.shape[0] // cn, run, 0, unroll=4)
+
+
 def back_body(
-    direct, scal, nrow, qsrc, hots, ge, dq, drow, scol, fcol, rows, feats, code, pre, mean, div,
-    upd, rst, cand, rstate, w_in, u_h, w_key, w_value, g_qkv, parity, out, gates, dpre, qe,
+    scal, nrow, qe, ge, dq, drow, scol, fcol, rows, feats, code, pre, mean, div,
+    upd, rst, cand, rstate, w_in, u_h, w_key, w_value, g_qkv, parity, keep, send, gates, dpre,
 ):
     n, m = mean.shape[0], rows.shape[1]
     f = feats.shape[1]
     hs = m // HEADS
     step = 256
     s = mean.shape[1]
-    if direct:
-        qe = qsrc
-    else:
-        events = hots.shape[1]
-        devices = qsrc.shape[0] // events
-        cn = hots.shape[0] // devices
-
-        def expand(d, carry):
-            b = pl.ds(pl.multiple_of(d * cn, cn), cn)
-            e = pl.ds(pl.multiple_of(d * events, events), events)
-            qe[b, :] = dot(hots[b, :], qsrc[e, :]).astype(BF16)
-            return carry
-
-        lax.fori_loop(0, devices, expand, 0)
-
     def block(i, carry):
         b = pl.ds(pl.multiple_of(i * step, step), step)
         mine = scol[b, :]
@@ -421,17 +424,27 @@
         return carry
 
     lax.fori_loop(0, n // step, block, 0)
-    half = out.shape[1]
-    me = parity[0, 0]
+    half = keep.shape[0]
+    even = parity[0, 0] == 0
     at = [0]
 
     def put(value):
         start, size = at[0], value.shape[0]
         low = max(0, min(size, half - start))
-        if low:
-            out[me, start : start + low, :] = value[:low, :].astype(BF16)
-        if low < size:
-            out[1 - me, start + low - half : start + size - half, :] = value[low:, :].astype(BF16)
+        pieces = ((value[:low, :], True, start), (value[low:, :], False, start + low - half))
+        for part, first, r in pieces:
+            if part.shape[0]:
+                part = part.astype(BF16)
+                b = slice(r, r + part.shape[0])
+
+                @pl.when(even == first)
+                def _():
+                    keep[b, :] = part
+
+                @pl.when(even != first)
+                def _():
+                    send[b, :] = part
+
         at[0] = start + size
 
     def put_cols(value):
@@ -516,6 +529,7 @@
             no, nb_slot.T, buckets.reshape(1, events), features,
         ),
         "place",
+        56,
     )
     got = exchange(req.reshape(devices, 1, 4 * ce + cn)).reshape(devices, 4 * ce + cn)
     got_feats = exchange(side_feats.reshape(devices, 2 * ce, feat)).reshape(n_side, feat)
@@ -524,35 +538,52 @@
     shift = events.bit_length() - 1
     assert 1 << shift == events
     owner_outs = [
-        ((n_side, m), BF16), ((n_dst, m), BF16), ((n_nb, m), BF16), ((n_side, m), BF16),
+        ((n_side, m), BF16), ((n_dst, m), BF16),
         ((1, n_side), I32), ((n_side, 1), I32), ((n_side, 1), F32),
         ((n_side, w_msg.shape[0] - m - feat), BF16),
         ((n_side, width), F32), ((n_side, width), BF16), ((n_side, width), F32),
         ((n_side, m), F32), ((n_side, m), F32), ((n_side, m), F32), ((n_side, m), BF16),
     ]
+    fetched = pl.pallas_call(
+        functools.partial(sides_body, ce),
+        out_shape=jax.ShapeDtypeStruct((n_side, m), BF16),
+        in_specs=[vm, sm],
+        out_specs=vm,
+        scratch_shapes=[pltpu.VMEM((acc_rows, m), F32), pltpu.VMEM((n_side, m), F32)],
+        compiler_params=room(56),
+        name="sides",
+    )(memory, got)
     (
-        new_side, dst_new, nb_reply, fetched, sfirst, scol, fcol, code, pre, mean, div,
-        upd, rst, cand, rstate,
-    ) = pl.pallas_call(
-        functools.partial(owner_body, ce, cn, shift),
-        out_shape=[jax.ShapeDtypeStruct(a, d) for a, d in owner_outs],
-        in_specs=[vm, vm, vm, sm, vm, vm, vm, vm],
-        out_specs=[vm] * len(owner_outs),
+        new_side, dst_new, sfirst, scol, fcol, code, pre, mean, div, upd, rst, cand, rstate,
+    ) = call(
+        functools.partial(owner_body, ce),
+        owner_outs,
+        (fetched, got_feats, got, w_msg, w_in, u_zr, u_h),
+        "owner",
+        56,
+        scratch=[pltpu.VMEM((n_side, width), BF16), pltpu.VMEM((n_side, 1), F32)],
+    )
+    nb_reply = pl.pallas_call(
+        functools.partial(answer_body, ce, cn, shift),
+        out_shape=jax.ShapeDtypeStruct((n_nb, m), BF16),
+        in_specs=[vm, vm, sm],
+        out_specs=vm,
         scratch_shapes=[
-            pltpu.VMEM((n_side, width), BF16), pltpu.VMEM((n_side, 1), F32),
             pltpu.VMEM((acc_rows + 8, m), F32), pltpu.VMEM((n_side, m), F32),
             pltpu.VMEM((n_nb, m), F32),
         ],
-        compiler_params=pltpu.CompilerParams(vmem_limit_bytes=VMEM_LIMIT),
-        name="owner",
-    )(memory, got_feats, got, got, w_msg, w_in, u_zr, u_h)
+        compiler_params=room(56),
+        name="answer",
+    )(memory, new_side, got)
     back_dst = exchange(dst_new.reshape(devices, ce, m)).reshape(n_dst, m)
     back_nb = exchange(nb_reply.reshape(devices, cn, m))
+    back_dst, nb_reply = lax.optimization_barrier((back_dst, nb_reply))
     q_rows, q_proj = call(
         query_body,
         [((events, m), BF16), ((events, m), BF16)],
         (back_dst, dplace, w_query),
         "query",
+        4,
     )
     proj_all = lax.all_gather(q_proj, AXES, axis=0, tiled=True)
     each = max(2 * ce, -(-(ce + 4) // 8) * 8)
@@ -577,44 +608,51 @@
         [((events, m), BF16), ((devices * each, m), BF16), ((3 * m, m), BF16)],
         (keys, q_rows, q_proj, emb_grad, w_query, w_key, w_value, dback, no, nrank),
         "attend",
+        14,
         scratch=[pltpu.VMEM((events * neighbours, m), BF16)] * 4,
     )
     back = exchange(reply.reshape(devices, each, m))
+    if cn % 16:
+        qe = proj_all[table]
+    else:
+        qe = pl.pallas_call(
+            functools.partial(expand_body, cn),
+            out_shape=jax.ShapeDtypeStruct((n_nb, m), BF16),
+            in_specs=[vm, vm],
+            out_specs=vm,
+            compiler_params=room(8),
+            name="expand",
+        )(proj_all, hots)
+    back, qe = lax.optimization_barrier((back, qe))
     scal = back[:, :4, :cn].transpose(1, 0, 2).reshape(4, n_nb)
-    direct = cn % 16 != 0
     index = lax.axis_index(AXES)
     parity = (index % 2).astype(I32).reshape(1, 1)
     total_rows = (w_msg.size + w_in.size + u_zr.size + u_h.size + 3 * w_query.size) // 128
     half = total_rows // 2
     args = (
-        scal, nrow, proj_all[table] if direct else proj_all, hots, ge,
-        back.reshape(devices * each, m), drow, scol, fcol, fetched,
+        scal, nrow, qe, ge, back.reshape(devices * each, m), drow, scol, fcol, fetched,
         got_feats, code, pre, mean, div, upd, rst, cand, rstate, w_in, u_h, w_key, w_value,
         g_qkv, parity,
     )
-    halves = pl.pallas_call(
-        functools.partial(back_body, direct),
-        out_shape=jax.ShapeDtypeStruct((2, half, 128), BF16),
+    keep, send = pl.pallas_call(
+        back_body,
+        out_shape=[jax.ShapeDtypeStruct((half, 128), BF16)] * 2,
         in_specs=[vm] * (len(args) - 1) + [sm],
-        out_specs=vm,
-        scratch_shapes=[
-            pltpu.VMEM((n_side, 3 * m), BF16), pltpu.VMEM((n_side, width), BF16),
-            pltpu.VMEM((n_nb, m), BF16),
-        ],
-        compiler_params=pltpu.CompilerParams(vmem_limit_bytes=VMEM_LIMIT),
+        out_specs=[vm] * 2,
+        scratch_shapes=[pltpu.VMEM((n_side, 3 * m), BF16), pltpu.VMEM((n_side, width), BF16)],
+        compiler_params=room(56),
         name="back",
     )(*args)
     pairs = [(i, i ^ 1) for i in range(devices)]
     teams = [[i for i in range(devices) if i % 2 == p] for p in range(2)]
     size = devices // 2
-    keep, send = halves[0], halves[1]
     half_sum = (
         keep.astype(F32) + lax.ppermute(send, AXES, pairs).astype(F32)
     ).astype(BF16).reshape(size, half // size, 128)
     shares = lax.all_to_all(
         half_sum, AXES, split_axis=0, concat_axis=0, tiled=True, axis_index_groups=teams
     )
-    spread = call(spread_body, [(shares.shape, BF16)], (shares,), "spread")[0]
+    spread = call(spread_body, [(shares.shape, BF16)], (shares,), "spread", 6)[0]
     mine = lax.all_to_all(
         spread, AXES, split_axis=0, concat_axis=0, tiled=True, axis_index_groups=teams
     ).reshape(half, 128)
@@ -628,6 +666,7 @@
         out_shape=[jax.ShapeDtypeStruct(a, d) for a, d in outs],
         in_specs=[vm, vm, sm],
         out_specs=[vm] * len(outs),
+        compiler_params=room(8),
         name="unpack",
     )(mine, other, parity)
     return (new_memory, embedding, g_msg, g_in, g_zr, g_h, g_q, g_k, g_v)

time: 228 us -> 202 us (0.89)
  Pallas kernels: 87.1 us -> 62.6 us
  blocking collectives: 77.7 us -> 55.2 us
  starting transfers between devices: 6.8 us -> 15.3 us
  waiting for transfers between devices: 21.5 us -> 29.8 us
  local copies, waits for them, and re-layouts: 18.5 us -> 22.1 us
    all_to_all x3 -> x1, blocking collectives: 37.3 us -> 14.5 us  [exchange(): return lax.all_to_all(x, AXES, split_axis=0, concat_axis=0, tiled=True)]
    pallas_call x2 -> x4, Pallas kernels: 52 us -> 29.7 us  [the longest x1 12.8 us: body(): pl.pallas_call(functools.partial(answer_body, ce, cn, shift), out_shape=j...]
    all_gather x1, waiting for transfers between devices: 0.01 us -> 13.6 us  [body(): proj_all = lax.all_gather(q_proj, AXES, axis=0, tiled=True)]
    all_to_all x2 -> x4, starting transfers between devices: 6.65 us -> 15 us  [exchange(): return lax.all_to_all(x, AXES, split_axis=0, concat_axis=0, tiled=True)]
    unnamed x19 -> x35, local copies, waits for them, and re-layouts: 2.16 us -> 7.59 us
    all_to_all x2 -> x4, waiting for transfers between devices: 16.9 us -> 11.7 us  [exchange(): return lax.all_to_all(x, AXES, split_axis=0, concat_axis=0, tiled=True)]
    pallas_call x4 -> x5, Pallas kernels: 13.9 us -> 18.2 us  [call(): pl.pallas_call(body, out_shape=[jax.ShapeDtypeStruct(s, d) for s, d in ou...]
    pallas_call x1, Pallas kernels: 13.4 us -> 9.59 us  [refresh(): pl.pallas_call(functools.partial(refresh_body, block), grid=(n // block,)...]
  transfers between devices with their start and end apart: 6 -> 8, of which waited for: 4 -> 5; matrix products, arithmetic and copies ran while one was open for 8% -> 8% of each run, Pallas kernels for 30% -> 25%
where the time goes in v4:
time: 202 us; the launch traced here: 201 us
  Pallas kernels  62.6 us (31%)
  blocking collectives  55.2 us (27%)
  waiting for transfers between devices  29.8 us (15%)
  local copies, waits for them, and re-layouts  22.1 us (11%)
  starting transfers between devices  15.3 us (8%)
  between operations  14.3 us (7%)
  other arithmetic  2.02 us (1%)
    all_to_all x1, blocking collectives, body(): lax.all_to_all(half_sum, AXES, split_axis=0, concat_axis=0, tiled=True, a...  21.4 us
    all_to_all x1, blocking collectives, body(): lax.all_to_all(spread, AXES, split_axis=0, concat_axis=0, tiled=True, axi...  19.3 us
    pallas_call x5, Pallas kernels, call(): pl.pallas_call(body, out_shape=[jax.ShapeDtypeStruct(s, d) for s, d in ou...  18.2 us
    all_to_all x4, starting transfers between devices, exchange(): return lax.all_to_all(x, AXES, split_axis=0, concat_axis=0, tiled=True)  15 us
    all_to_all x1, blocking collectives, exchange(): return lax.all_to_all(x, AXES, split_axis=0, concat_axis=0, tiled=True)  14.5 us
    all_gather x1, waiting for transfers between devices, body(): proj_all = lax.all_gather(q_proj, AXES, axis=0, tiled=True)  13.6 us
    pallas_call x1, Pallas kernels, body(): pl.pallas_call(functools.partial(answer_body, ce, cn, shift), out_shape=j...  12.8 us
    all_to_all x4, waiting for transfers between devices, exchange(): return lax.all_to_all(x, AXES, split_axis=0, concat_axis=0, tiled=True)  11.7 us
  transfers between devices with their start and end apart: 8, of which 5 were waited for; matrix products, arithmetic and copies ran while one was open for 8% of the time, Pallas kernels for 25%

profile of v4, /device:TPU:0, one launch (start us, length us, event | category | flops | bytes accessed | tf_op | source)
XLA Modules:
  0.0 201.4 jit_solution(10075317888839288404)
XLA Ops:
  7.2 0.0 all-gather.3.cloned.1.call-start
  7.2 0.7 all-gather.3.cloned.1.call-update
  7.9 1.3 copy.34
  9.2 4.0 %place.1 = (s32[32,112]{1,0:T(8,128)}, bf16[512,128]{1,0:T(8,128)(2,1)}, s32[1,128]{1,0:T(1,128)}, s32[10,128]{1,0:T(8,128)}) custom-call(s32[1,128]{1,0:T(1,128)} %bitcast.53, s32[1,128]{1,0:T(1,128)} %bitcast.54, s32[1,128]{1,0:T(1,128)} %bitcast.55, s32[1,128]{1,0:T(1,128)} %bitcast.56, s32[10,128]{1,0:T(8,128)} %bitcast.41, s32[10,128]{1,0:T(8,128)} %bitcast.52, ...), custom_call_target="tpu_custom_call" | custom-call | tf_op jit(solution)/shard_map/place/pallas_call | solution.py:63
  13.2 14.5 %all_to_all.35 = s32[32,1,112]{2,1,0:T(1,128)} all-to-all(s32[32,1,112]{2,1,0:T(1,128)} %bitcast.51), channel_id=1, replica_groups=mesh['acct'=8,'rep'=4] {'acct','rep'}, dimensions={0} | all-to-all | bytes 28672 | tf_op jit(solution)/shard_map/all_to_all | solution.py:498
  27.7 2.6 %all-to-all-start.1 = ((bf16[32,16,128]{2,1,0:T(8,128)(2,1)}), bf16[32,16,128]{2,1,0:T(8,128)(2,1)S(1)}, u32[]{:S(2)}, u32[]{:S(2)}) async-start(bf16[32,16,128]{2,1,0:T(8,128)(2,1)} %bitcast.50), calls=%async_computation.1 | async-start | bytes 262144 | tf_op jit(solution)/shard_map/all_to_all | solution.py:498
  30.3 5.0 %sides.1.rows = bf16[512,256]{1,0:T(8,128)(2,1)} custom-call(bf16[8192,256]{1,0:T(8,128)(2,1)} %old.1, s32[32,112]{1,0:T(8,128)} %bitcast.34), custom_call_target="tpu_custom_call" | custom-call | tf_op jit(solution)/shard_map/sides/pallas_call | solution.py:547
  35.3 3.2 %all-to-all-done.1 = bf16[32,16,128]{2,1,0:T(8,128)(2,1)S(1)} async-done(((bf16[32,16,128]{2,1,0:T(8,128)(2,1)}), bf16[32,16,128]{2,1,0:T(8,128)(2,1)S(1)}, u32[]{:S(2)}, u32[]{:S(2)}) %all-to-all-start.1) | async-done | bytes 131104 | tf_op jit(solution)/shard_map/all_to_all | solution.py:498
  38.5 0.6 copy-done.15
  39.2 7.7 %owner.1 = (bf16[512,256]{1,0:T(8,128)(2,1)}, bf16[256,256]{1,0:T(8,128)(2,1)}, s32[1,512]{1,0:T(1,128)}, s32[512,1]{1,0:T(8,128)}, f32[512,1]{1,0:T(8,128)}, /*...) custom-call(bf16[512,256]{1,0:T(8,128)(2,1)} %sides.1.rows, ...), custom_call_target="tpu_custom_call" | custom-call | tf_op jit(solution)/shard_map/owner/pallas_call | solution.py:63
  46.8 2.6 %all-to-all-start.3 = ((bf16[32,8,256]{2,1,0:T(8,128)(2,1)}), bf16[32,8,256]{2,1,0:T(8,128)(2,1)S(1)}, u32[]{:S(2)}, u32[]{:S(2)}) async-start(bf16[32,8,256]{2,1,0:T(8,128)(2,1)} %bitcast.49), calls=%async_computation.3 | async-start | bytes 262144 | tf_op jit(solution)/shard_map/all_to_all | solution.py:498
  49.5 0.0 all-gather.5.cloned.1.call-start
  49.5 0.0 copy-start.7
  49.6 12.8 %answer.1 = bf16[2560,256]{1,0:T(8,128)(2,1)} custom-call(bf16[8192,256]{1,0:T(8,128)(2,1)} %old.1, bf16[512,256]{1,0:T(8,128)(2,1)} %get-tuple-element.53.new, s32[32,112]{1,0:T(8,128)} %bitcast.36), custom_call_target="tpu_custom_call" | custom-call | tf_op jit(solution)/shard_map/answer/pallas_call | solution.py:566
  62.3 0.9 query.1
  63.3 0.0 all-gather.5.cloned.1.call-update
  63.4 5.8 %all-to-all-start.2 = ((bf16[32,80,256]{2,1,0:T(8,128)(2,1)}), bf16[32,80,256]{2,1,0:T(8,128)(2,1)S(1)}, u32[]{:S(2)}, u32[]{:S(2)}) async-start(bf16[32,80,256]{2,1,0:T(8,128)(2,1)} %bitcast.44), calls=%async_computation.2 | async-start | bytes 2621440 | tf_op jit(solution)/shard_map/all_to_all | solution.py:498
  69.3 0.1 slice.17
  69.3 3.5 %hot.1.hots = bf16[2560,128]{1,0:T(8,128)(2,1)S(1)} custom-call(s32[32,112]{1,0:T(8,128)S(1)} %bitcast.38), custom_call_target="tpu_custom_call" | custom-call | tf_op jit(solution)/shard_map/hot/pallas_call | solution.py:273
  72.9 0.1 fusion.4
  73.0 0.1 rem.84
  73.1 0.1 reshape.250
  73.1 0.1 concatenate.3
  73.2 0.7 reshape.251.drow
  73.9 0.1 fusion.1
  74.0 0.6 and_select_fusion.nrow
  74.6 2.2 %copy-done = bf16[8192,256]{1,0:T(8,128)(2,1)S(1)} copy-done((bf16[8192,256]{1,0:T(8,128)(2,1)S(1)}, bf16[8192,256]{1,0:T(8,128)(2,1)}, u32[]{:S(2)}) %copy-start) | copy-done | bytes 4194328
  76.8 9.6 %refresh.1 = bf16[8192,256]{1,0:T(8,128)(2,1)} custom-call(bf16[8192,256]{1,0:T(8,128)(2,1)S(1)} %copy-done, s32[1,512]{1,0:T(1,128)S(1)} %copy-done.12, bf16[512,256]{1,0:T(8,128)(2,1)S(1)} %copy-done.3), custom_call_target="tpu_custom_call" | custom-call | tf_op jit(solution)/shard_map/refresh/pallas_call | solution.py:249
  86.4 8.7 %gather_fusion = bf16[2560,256]{1,0:T(8,128)(2,1)} fusion(bf16[4096,256]{1,0:T(8,128)(2,1)} %all-gather.3.cloned.1.call-done, s32[3072]{0:T(1024)S(1)} %pad_clamp_fusion), kind=kCustom, calls=%fused_computation | custom fusion | bytes 2631680 | tf_op jit(solution)/shard_map/gather | solution.py:594
  95.1 8.5 %all-to-all-done.2 = bf16[32,80,256]{2,1,0:T(8,128)(2,1)S(1)} async-done(((bf16[32,80,256]{2,1,0:T(8,128)(2,1)}), bf16[32,80,256]{2,1,0:T(8,128)(2,1)S(1)}, u32[]{:S(2)}, u32[]{:S(2)}) %all-to-all-start.2) | async-done | bytes 1310752 | tf_op jit(solution)/shard_map/all_to_all | solution.py:498
  103.6 4.1 %gather_fusion.1 = bf16[1280,256]{1,0:T(8,128)(2,1)S(1)} fusion(bf16[2560,256]{1,0:T(8,128)(2,1)S(1)} %bitcast.43, s32[2048]{0:T(1024)S(1)} %pad_clamp_fusion.1), kind=kCustom, calls=%fused_computation.1 | custom fusion | bytes 1315840 | tf_op jit(solution)/shard_map/gather | solution.py:604
  107.7 5.5 %attend.1 = (bf16[128,256]{1,0:T(8,128)(2,1)}, bf16[512,256]{1,0:T(8,128)(2,1)}, bf16[768,256]{1,0:T(8,128)(2,1)S(1)}) custom-call(bf16[1280,256]{1,0:T(8,128)(2,1)S(1)} %gather_fusion.1, bf16[128,256]{1,0:T(8,128)(2,1)S(1)} %get-tuple-element.63.q_rows, bf16[128,256]{1,0:T(8,128)(2,1)} %get-tuple-element.64.q_proj, bf16[128,256]{1,0:T(8,128)(2,1)S(1)} %copy-done.9, ...), custom_call_target="tpu_custom_call" | custom-call | tf_op jit(solution)/shard_map/attend/pallas_call | solution.py:63
  113.2 0.7 copy-done.8
  113.9 3.9 %all-to-all-start.4 = ((bf16[32,16,256]{2,1,0:T(8,128)(2,1)}), bf16[32,16,256]{2,1,0:T(8,128)(2,1)S(1)}, u32[]{:S(2)}, u32[]{:S(2)}) async-start(bf16[32,16,256]{2,1,0:T(8,128)(2,1)} %bitcast.17), calls=%async_computation.4 | async-start | bytes 524288 | tf_op jit(solution)/shard_map/all_to_all | solution.py:498
  117.9 13.6 %all-gather.5.cloned.1.call-done.source = bf16[4096,256]{1,0:T(8,128)(2,1)} async-done(((bf16[128,256]{1,0:T(8,128)(2,1)}), bf16[4096,256]{1,0:T(8,128)(2,1)}) %all-gather.5.cloned.1.call-update) | async-done | bytes 2097168 | tf_op jit(solution)/shard_map/all_gather | solution.py:588
  131.4 1.6 copy-done.2
  133.0 1.6 expand.1.qe
  134.6 1.1 copy-done.1
  135.7 0.7 reshape.257.scal
  136.4 10.4 %back.1 = (bf16[2176,128]{1,0:T(8,128)(2,1)}, bf16[2176,128]{1,0:T(8,128)(2,1)}) custom-call(bf16[4,2560]{1,0:T(4,128)(2,1)} %reshape.257.scal, s32[1,2560]{1,0:T(1,128)} %and_select_fusion.nrow, bf16[2560,256]{1,0:T(8,128)(2,1)} %copy-done.1, bf16[2560,256]{1,0:T(8,128)(2,1)} %gather_fusion, bf16[512,256]{1,0:T(8,128)(2,1)} %bitcast.46, ...), custom_call_target="tpu_custom_call" | custom-call | tf_op jit(solution)/shard_map/back/pallas_call | solution.py:637
  146.8 0.3 collective-permute-start
  147.0 1.9 collective-permute-done
  149.0 1.2 add_convert_fusion
  150.2 21.4 %all_to_all.36.x = bf16[16,136,128]{2,1,0:T(8,128)(2,1)S(1)} all-to-all(bf16[16,136,128]{2,1,0:T(8,128)(2,1)S(1)} %bitcast.45), channel_id=1, replica_groups={{0,2,4,6,8,10,12,14,16,18,20,22,24,26,28,30},{1,3,5,7,9,11,13,15,17,19,..., dimensions={0} | all-to-all | bytes 1114112 | tf_op jit(solution)/shard_map/all_to_all | solution.py:652
  171.6 0.1 spread.1
  171.7 19.3 %all_to_all.37 = bf16[16,136,128]{2,1,0:T(8,128)(2,1)S(1)} all-to-all(bf16[16,136,128]{2,1,0:T(8,128)(2,1)S(1)} %spread.1), channel_id=1, replica_groups={{0,2,4,6,8,10,12,14,16,18,20,22,24,26,28,30},{1,3,5,7,9,11,13,15,17,19,..., dimensions={0} | all-to-all | bytes 1114112 | tf_op jit(solution)/shard_map/all_to_all | solution.py:656
  191.0 2.0 collective-permute-done.1.other
  193.0 1.6 unpack.1
  (39 shorter events, 0.1 us)
Async XLA Ops:
  7.2 79.2 %all-gather.3.cloned.1.call-start = ((), (), s32[]{:S(2)}) async-start(), calls=%async_computation.7 | async-start | bytes 2162688 | tf_op jit(solution)/shard_map/all_gather | solution.py:516
  27.7 10.8 %all-to-all-start.1 = ((bf16[32,16,128]{2,1,0:T(8,128)(2,1)}), bf16[32,16,128]{2,1,0:T(8,128)(2,1)S(1)}, u32[]{:S(2)}, u32[]{:S(2)}) async-start(bf16[32,16,128]{2,1,0:T(8,128)(2,1)} %bitcast.50), calls=%async_computation.1 | async-start | bytes 262144 | tf_op jit(solution)/shard_map/all_to_all | solution.py:498
  38.5 0.6 copy-start.15
  46.8 15.5 %all-to-all-start.3 = ((bf16[32,8,256]{2,1,0:T(8,128)(2,1)}), bf16[32,8,256]{2,1,0:T(8,128)(2,1)S(1)}, u32[]{:S(2)}, u32[]{:S(2)}) async-start(bf16[32,8,256]{2,1,0:T(8,128)(2,1)} %bitcast.49), calls=%async_computation.3 | async-start | bytes 262144 | tf_op jit(solution)/shard_map/all_to_all | solution.py:498
  49.5 81.9 %all-gather.5.cloned.1.call-start = ((), (), s32[]{:S(2)}) async-start(), calls=%async_computation.8 | async-start | bytes 2162688 | tf_op jit(solution)/shard_map/all_gather | solution.py:588
  49.5 12.8 %copy-start.7 = (bf16[256,256]{1,0:T(8,128)(2,1)S(1)}, bf16[256,256]{1,0:T(8,128)(2,1)}, u32[]{:S(2)}) copy-start(bf16[256,256]{1,0:T(8,128)(2,1)} %w_query.3) | copy-start | bytes 393220
  49.6 12.8 %copy-start.13 = (s32[1,128]{1,0:T(1,128)S(1)}, s32[1,128]{1,0:T(1,128)}, u32[]{:S(2)}) copy-start(s32[1,128]{1,0:T(1,128)} %get-tuple-element.58.dplace) | copy-start | bytes 1540
  63.3 5.9 %copy-start.11 = (s32[10,128]{1,0:T(8,128)S(1)}, s32[10,128]{1,0:T(8,128)}, u32[]{:S(2)}) copy-start(s32[10,128]{1,0:T(8,128)} %get-tuple-element.55.nrank) | copy-start | bytes 15364
  63.3 5.9 %copy-start.16 = (s32[128,10,1]{0,2,1:T(1,128)S(1)}, s32[128,10,1]{0,2,1:T(1,128)}, u32[]{:S(2)}) copy-start(s32[128,10,1]{0,2,1:T(1,128)} %param.24) | copy-start | bytes 15364
  63.3 5.9 %copy-start.4 = (s32[32,1,112]{2,1,0:T(1,128)S(1)}, s32[32,1,112]{2,1,0:T(1,128)}, u32[]{:S(2)}) copy-start(s32[32,1,112]{2,1,0:T(1,128)} %all_to_all.35) | copy-start | bytes 43012
  63.3 11.3 %copy-start.3 = (bf16[512,256]{1,0:T(8,128)(2,1)S(1)}, bf16[512,256]{1,0:T(8,128)(2,1)}, u32[]{:S(2)}) copy-start(bf16[512,256]{1,0:T(8,128)(2,1)} %get-tuple-element.53.new) | copy-start | bytes 786436
  63.3 11.3 %copy-start.12 = (s32[1,512]{1,0:T(1,128)S(1)}, s32[1,512]{1,0:T(1,128)}, u32[]{:S(2)}) copy-start(s32[1,512]{1,0:T(1,128)} %get-tuple-element.54.sfirst) | copy-start | bytes 6148
  63.4 40.2 %all-to-all-start.2 = ((bf16[32,80,256]{2,1,0:T(8,128)(2,1)}), bf16[32,80,256]{2,1,0:T(8,128)(2,1)S(1)}, u32[]{:S(2)}, u32[]{:S(2)}) async-start(bf16[32,80,256]{2,1,0:T(8,128)(2,1)} %bitcast.44), calls=%async_computation.2 | async-start | bytes 2621440 | tf_op jit(solution)/shard_map/all_to_all | solution.py:498
  74.6 2.2 %copy-start = (bf16[8192,256]{1,0:T(8,128)(2,1)S(1)}, bf16[8192,256]{1,0:T(8,128)(2,1)}, u32[]{:S(2)}) copy-start(bf16[8192,256]{1,0:T(8,128)(2,1)} %old.1) | copy-start | bytes 12582916
  103.6 4.1 %copy-start.5 = (bf16[256,256]{1,0:T(8,128)(2,1)S(1)}, bf16[256,256]{1,0:T(8,128)(2,1)}, u32[]{:S(2)}) copy-start(bf16[256,256]{1,0:T(8,128)(2,1)} %w_key.3) | copy-start | bytes 393220
  103.6 4.1 %copy-start.6 = (bf16[256,256]{1,0:T(8,128)(2,1)S(1)}, bf16[256,256]{1,0:T(8,128)(2,1)}, u32[]{:S(2)}) copy-start(bf16[256,256]{1,0:T(8,128)(2,1)} %w_value.3) | copy-start | bytes 393220
  103.6 4.1 %copy-start.9 = (bf16[128,256]{1,0:T(8,128)(2,1)S(1)}, bf16[128,256]{1,0:T(8,128)(2,1)}, u32[]{:S(2)}) copy-start(bf16[128,256]{1,0:T(8,128)(2,1)} %grad.1) | copy-start | bytes 196612
  103.6 4.1 %copy-start.10 = (s32[128,10,1]{0,1,2:T(8,128)S(1)}, s32[128,10,1]{0,1,2:T(8,128)}, u32[]{:S(2)}) copy-start(s32[128,10,1]{0,1,2:T(8,128)} %copy.34) | copy-start | bytes 15364
  113.2 0.7 copy-start.8
  113.9 21.7 %all-to-all-start.4 = ((bf16[32,16,256]{2,1,0:T(8,128)(2,1)}), bf16[32,16,256]{2,1,0:T(8,128)(2,1)S(1)}, u32[]{:S(2)}, u32[]{:S(2)}) async-start(bf16[32,16,256]{2,1,0:T(8,128)(2,1)} %bitcast.17), calls=%async_computation.4 | async-start | bytes 524288 | tf_op jit(solution)/shard_map/all_to_all | solution.py:498
  131.4 1.6 copy-start.2
  134.6 1.1 copy-start.1
  135.7 0.7 copy-start.14
  146.8 2.2 %collective-permute-start = (bf16[2176,128]{1,0:T(8,128)(2,1)}, bf16[2176,128]{1,0:T(8,128)(2,1)S(1)}, u32[]{:S(2)}, u32[]{:S(2)}) collective-permute-start(bf16[2176,128]{1,0:T(8,128)(2,1)} %get-tuple-element.85), channel_id=1, source_target_pairs={{0,1},{1,0},{2,3},{3,2},{4,5},{5,4},{6,7},{7,6},{8,9},{9,8},{10,11... | collective-permute-start | bytes 1671176 | tf_op jit(solution)/shard_map/ppermute | solution.py:650
  191.0 2.0 collective-permute-start.1
Sparse Core Ops, SparseCore 0:
  10.9 59.1 all-gather.2
  72.9 58.4 all-gather.4

commit v5 on v4

--- a/solution.py
+++ b/solution.py
@@ -58,12 +58,13 @@
     return 1.0 / (1.0 + jnp.exp(-v))
 
 
-def call(body, outs, args, name, mib, scratch=()):
+def call(body, outs, args, name, mib, scratch=(), scalars=0):
     vm = pl.BlockSpec(memory_space=pltpu.VMEM)
+    sm = pl.BlockSpec(memory_space=pltpu.SMEM)
     return pl.pallas_call(
         body,
         out_shape=[jax.ShapeDtypeStruct(s, d) for s, d in outs],
-        in_specs=[vm] * len(args),
+        in_specs=[vm] * (len(args) - scalars) + [sm] * scalars,
         out_specs=[vm] * len(outs),
         scratch_shapes=list(scratch),
         compiler_params=room(mib),
@@ -80,7 +81,10 @@
 
     def fill(onehot, rank, value, cap):
         hits = (iota((cap, events), 0) == rank).astype(F32)
-        return dot_nt(onehot, hits * value.astype(F32), precision=EXACT)
+        owner_b = onehot.astype(BF16)
+        high = dot_nt(owner_b, (hits * (value >> 7).astype(F32)).astype(BF16))
+        low = dot_nt(owner_b, (hits * (value & 127).astype(F32)).astype(BF16))
+        return high * 128.0 + low
 
     chosen = jnp.zeros((2 * devices * ce, events), F32)
     for side, (o_ref, s_ref) in enumerate(((so, ss), (do, ds))):
@@ -97,7 +101,8 @@
             dplace[...] = owner * ce + rank
     feats[...] = dot(chosen.astype(BF16), feat[...]).astype(BF16)
     base = jnp.zeros((devices, 1), F32)
-    total = jnp.zeros((devices, cn), F32)
+    slots = jnp.zeros((devices, cn), F32)
+    which = jnp.zeros((devices, cn), F32)
     event = iota((1, events), 1)
     for k in range(neighbours):
         onehot = (own == no[k : k + 1, :]).astype(F32)
@@ -105,8 +110,10 @@
         rank = jnp.sum(onehot * before, axis=0, keepdims=True).astype(I32)
         nrank[k : k + 1, :] = rank
         base = base + jnp.sum(onehot, axis=1, keepdims=True)
-        total = total + fill(onehot, rank, ns[k : k + 1, :] * events + event + 1, cn)
-    req[:, 4 * ce : 4 * ce + cn] = total.astype(I32) - 1
+        slots = slots + fill(onehot, rank, ns[k : k + 1, :], cn)
+        which = which + fill(onehot, rank, event + 1, cn)
+    req[:, 4 * ce : 4 * ce + cn] = slots.astype(I32)
+    req[:, 4 * ce + cn :] = which.astype(I32) - 1
 
 
 def widen_rows(source, target):
@@ -114,10 +121,16 @@
 
     def run(i, carry):
         b = pl.ds(pl.multiple_of(i * step, step), step)
-        target[b, :] = source[b, :].astype(F32)
+        for h in range(target.shape[0]):
+            target[h, b, :] = source[b, h * 128 : (h + 1) * 128].astype(F32)
         return carry
 
     lax.fori_loop(0, source.shape[0] // step, run, 0)
+
+
+def narrow_rows(source, target):
+    for h in range(source.shape[0]):
+        target[:, h * 128 : (h + 1) * 128] = source[h].astype(BF16)
 
 
 def pick_rows(table, target, slots_s, first, count, read):
@@ -126,12 +139,14 @@
 
     def block(i, carry):
         for g in range(rows // 8):
-            found = []
-            for r in range(g * 8, g * 8 + 8):
-                where = read(slots_s[i * sources + r // count, first + r % count])
-                found.append(table[pl.ds(where, 1), :])
+            where = [
+                read(slots_s[i * sources + r // count, first + r % count])
+                for r in range(g * 8, g * 8 + 8)
+            ]
             base = pl.multiple_of(i * rows + g * 8, 8)
-            target[pl.ds(base, 8), :] = jnp.concatenate(found, axis=0)
+            for h in range(table.shape[0]):
+                found = [table[h, pl.ds(w, 1), :] for w in where]
+                target[h, pl.ds(base, 8), :] = jnp.concatenate(found, axis=0)
         return carry
 
     lax.fori_loop(0, slots_s.shape[0] // sources, block, 0)
@@ -140,32 +155,32 @@
 def sides_body(ce, memory, slots_s, rows, table, wide):
     widen_rows(memory, table)
     pick_rows(table, wide, slots_s, 0, 2 * ce, lambda v: jnp.maximum(v, 0))
-    rows[...] = wide[...].astype(BF16)
-
-
-def answer_body(ce, cn, shift, memory, new, slots_s, reply, table, wide, copied):
+    narrow_rows(wide, rows)
+
+
+def answer_body(ce, cn, memory, new, slots_s, reply, table, wide, copied):
     acc_rows = memory.shape[0]
     widen_rows(memory, table)
-    wide[...] = new[...].astype(F32)
+    widen_rows(new, wide)
 
     each = 2 * ce
     rows = math.lcm(each, 8)
     sources = rows // each
 
     def store(i, carry):
-        fresh = wide[pl.ds(pl.multiple_of(i * rows, rows), rows), :]
+        fresh = [
+            wide[h, pl.ds(pl.multiple_of(i * rows, rows), rows), :] for h in range(wide.shape[0])
+        ]
         for r in range(rows):
             slot = slots_s[i * sources + r // each, r % each]
             slot = jnp.where(slot >= 0, slot, acc_rows)
-            table[pl.ds(slot, 1), :] = fresh[r : r + 1, :]
+            for h in range(wide.shape[0]):
+                table[h, pl.ds(slot, 1), :] = fresh[h][r : r + 1, :]
         return carry
 
     lax.fori_loop(0, slots_s.shape[0] // sources, store, 0)
-    pick_rows(
-        table, copied, slots_s, 4 * ce, cn,
-        lambda v: lax.shift_right_logical(jnp.maximum(v, 0), shift),
-    )
-    reply[...] = copied[...].astype(BF16)
+    pick_rows(table, copied, slots_s, 4 * ce, cn, lambda v: v)
+    narrow_rows(copied, reply)
 
 
 def owner_body(
@@ -262,9 +277,8 @@
 
 
 def hot_body(events, ce, cn, block, got, out):
-    table = got[:, 4 * ce :].astype(F32)
-    code = to_col(table, block, cn, 0, pl.program_id(0) * block).astype(I32)
-    event = jnp.where(code >= 0, code % events, -1)
+    table = got[:, 4 * ce + cn :].astype(F32)
+    event = to_col(table, block, cn, 0, pl.program_id(0) * block).astype(I32)
     out[...] = (iota((block, events), 1) == event).astype(F32).astype(BF16)
 
 
@@ -291,13 +305,16 @@
 
 
 def attend_body(
-    cn, devices, each, keys, q_rows, q_proj, grad, w_query, w_key, w_value, dback, no, nrank,
-    emb, reply, g_qkv, kp, vp, dk, dv,
+    cn, devices, each, back, q_rows, q_proj, grad, w_query, w_key, w_value, dback, no, nrank, places,
+    emb, reply, g_qkv, kp, vp, dk, dv, keys, wide, picked,
 ):
     events, m = q_rows.shape
     neighbours = no.shape[0]
     hs = m // HEADS
     scaling = 1.0 / math.sqrt(hs)
+    widen_rows(back, wide)
+    pick_rows(wide, picked, places, 0, events, lambda v: v)
+    narrow_rows(picked, keys)
     qf = q_proj[...].astype(F32)
     gf = grad[...].astype(F32)
     lane = iota((events, 128), 1)
@@ -513,12 +530,13 @@
     n_dst = devices * ce
     n_side = 2 * n_dst
     n_nb = devices * cn
+    lanes = 4 * ce + 2 * cn
     grad_all = lax.all_gather(emb_grad, AXES, axis=0, tiled=True)
     no = nb_owner.reshape(events, neighbours).T
     req, side_feats, dplace, nrank = call(
         functools.partial(place_body, ce, cn, devices),
         [
-            ((devices, 4 * ce + cn), I32),
+            ((devices, lanes), I32),
             ((n_side, feat), BF16),
             ((1, events), I32),
             ((neighbours, events), I32),
@@ -531,12 +549,10 @@
         "place",
         56,
     )
-    got = exchange(req.reshape(devices, 1, 4 * ce + cn)).reshape(devices, 4 * ce + cn)
+    got = exchange(req.reshape(devices, 1, lanes)).reshape(devices, lanes)
     got_feats = exchange(side_feats.reshape(devices, 2 * ce, feat)).reshape(n_side, feat)
     vm = pl.BlockSpec(memory_space=pltpu.VMEM)
     sm = pl.BlockSpec(memory_space=pltpu.SMEM)
-    shift = events.bit_length() - 1
-    assert 1 << shift == events
     owner_outs = [
         ((n_side, m), BF16), ((n_dst, m), BF16),
         ((1, n_side), I32), ((n_side, 1), I32), ((n_side, 1), F32),
@@ -549,7 +565,9 @@
         out_shape=jax.ShapeDtypeStruct((n_side, m), BF16),
         in_specs=[vm, sm],
         out_specs=vm,
-        scratch_shapes=[pltpu.VMEM((acc_rows, m), F32), pltpu.VMEM((n_side, m), F32)],
+        scratch_shapes=[
+            pltpu.VMEM((m // 128, acc_rows, 128), F32), pltpu.VMEM((m // 128, n_side, 128), F32),
+        ],
         compiler_params=room(56),
         name="sides",
     )(memory, got)
@@ -564,13 +582,13 @@
         scratch=[pltpu.VMEM((n_side, width), BF16), pltpu.VMEM((n_side, 1), F32)],
     )
     nb_reply = pl.pallas_call(
-        functools.partial(answer_body, ce, cn, shift),
+        functools.partial(answer_body, ce, cn),
         out_shape=jax.ShapeDtypeStruct((n_nb, m), BF16),
         in_specs=[vm, vm, sm],
         out_specs=vm,
         scratch_shapes=[
-            pltpu.VMEM((acc_rows + 8, m), F32), pltpu.VMEM((n_side, m), F32),
-            pltpu.VMEM((n_nb, m), F32),
+            pltpu.VMEM((m // 128, acc_rows + 8, 128), F32),
+            pltpu.VMEM((m // 128, n_side, 128), F32), pltpu.VMEM((m // 128, n_nb, 128), F32),
         ],
         compiler_params=room(56),
         name="answer",
@@ -589,27 +607,35 @@
     each = max(2 * ce, -(-(ce + 4) // 8) * 8)
     late_got, _ = lax.optimization_barrier((got, nb_reply))
     new_memory = refresh(memory, sfirst, new_side)
-    late_code = late_got[:, 4 * ce :].reshape(n_nb)
-    table = jnp.maximum(late_code, 0) % events + jnp.arange(n_nb, dtype=I32) // cn * events
+    late_event = late_got[:, 4 * ce + cn :].reshape(n_nb)
+    table = jnp.maximum(late_event, 0) + jnp.arange(n_nb, dtype=I32) // cn * events
     ge = grad_all[table]
-    nrow = (late_code // events).reshape(1, n_nb)
+    late_slots = late_got[:, 4 * ce : 4 * ce + cn].reshape(n_nb)
+    nrow = jnp.where(late_event >= 0, late_slots, -1).reshape(1, n_nb)
     drow = jnp.concatenate(
         [jnp.full((devices, each - ce), -1, I32), late_got[:, ce : 2 * ce]], axis=1
     ).reshape(1, devices * each)
     hots = hot(events, ce, cn, late_got, n_nb)
-    nb_place = (no * cn + nrank).reshape(-1)
+    nb_place = no * cn + nrank
     back_nb, new_memory, ge, nrow, drow, hots, nb_place, q_rows = lax.optimization_barrier(
         (back_nb, new_memory, ge, nrow, drow, hots, nb_place, q_rows)
     )
-    keys = back_nb.reshape(n_nb, m)[nb_place]
     dback = dplace // ce * each + (each - ce) + dplace % ce
     embedding, reply, g_qkv = call(
         functools.partial(attend_body, cn, devices, each),
         [((events, m), BF16), ((devices * each, m), BF16), ((3 * m, m), BF16)],
-        (keys, q_rows, q_proj, emb_grad, w_query, w_key, w_value, dback, no, nrank),
+        (
+            back_nb.reshape(n_nb, m), q_rows, q_proj, emb_grad, w_query, w_key, w_value, dback, no,
+            nrank, nb_place,
+        ),
         "attend",
-        14,
-        scratch=[pltpu.VMEM((events * neighbours, m), BF16)] * 4,
+        20,
+        scratch=[pltpu.VMEM((events * neighbours, m), BF16)] * 5
+        + [
+            pltpu.VMEM((m // 128, n_nb, 128), F32),
+            pltpu.VMEM((m // 128, events * neighbours, 128), F32),
+        ],
+        scalars=1,
     )
     back = exchange(reply.reshape(devices, each, m))
     if cn % 16:

time: 202 us -> 202 us (level)
  waiting for transfers between devices: 29.8 us -> 35 us
  Pallas kernels: 62.6 us -> 59.2 us
  local copies, waits for them, and re-layouts: 22.1 us -> 20 us
    all_gather x1, waiting for transfers between devices: 13.6 us -> 19.7 us  [body(): proj_all = lax.all_gather(q_proj, AXES, axis=0, tiled=True)]
    pallas_call x1, Pallas kernels: 12.8 us -> 8.7 us  [body(): pl.pallas_call(functools.partial(answer_body, ce, cn), out_shape=jax.Shap...]
    gather x1 -> x0, local copies, waits for them, and re-layouts: 4.06 us -> none  [body(): keys = back_nb.reshape(n_nb, m)[nb_place]]
    unnamed x35 -> x36, local copies, waits for them, and re-layouts: 7.59 us -> 8.2 us
  transfers between devices with their start and end apart: 8 -> 8, of which waited for: 5 -> 5; matrix products, arithmetic and copies ran while one was open for 8% -> 7% of each run, Pallas kernels for 25% -> 23%
where the time goes in v5:
time: 202 us; the launch traced here: 201 us
  Pallas kernels  59.2 us (29%)
  blocking collectives  55.6 us (28%)
  waiting for transfers between devices  35 us (17%)
  local copies, waits for them, and re-layouts  20 us (10%)
  starting transfers between devices  15.6 us (8%)
  between operations  14.3 us (7%)
    all_to_all x1, blocking collectives, body(): lax.all_to_all(half_sum, AXES, split_axis=0, concat_axis=0, tiled=True, a...  21.9 us
    all_gather x1, waiting for transfers between devices, body(): proj_all = lax.all_gather(q_proj, AXES, axis=0, tiled=True)  19.7 us
    pallas_call x5, Pallas kernels, call(): pl.pallas_call(body, out_shape=[jax.ShapeDtypeStruct(s, d) for s, d in ou...  19.6 us
    all_to_all x1, blocking collectives, body(): lax.all_to_all(spread, AXES, split_axis=0, concat_axis=0, tiled=True, axi...  19.3 us
    all_to_all x4, starting transfers between devices, exchange(): return lax.all_to_all(x, AXES, split_axis=0, concat_axis=0, tiled=True)  15.2 us
    all_to_all x1, blocking collectives, exchange(): return lax.all_to_all(x, AXES, split_axis=0, concat_axis=0, tiled=True)  14.4 us
    all_to_all x4, waiting for transfers between devices, exchange(): return lax.all_to_all(x, AXES, split_axis=0, concat_axis=0, tiled=True)  10.8 us
    pallas_call x1, Pallas kernels, body(): pl.pallas_call(back_body, out_shape=[jax.ShapeDtypeStruct((half, 128), BF...  10.4 us
  transfers between devices with their start and end apart: 8, of which 5 were waited for; matrix products, arithmetic and copies ran while one was open for 7% of the time, Pallas kernels for 23%

profile of v5, /device:TPU:0, one launch (start us, length us, event | category | flops | bytes accessed | tf_op | source)
XLA Modules:
  0.0 201.1 jit_solution(14171479921454914076)
XLA Ops:
  7.2 0.0 all-gather.3.cloned.1.call-start
  7.2 0.7 all-gather.3.cloned.1.call-update
  7.9 1.3 copy.37
  9.2 3.9 %place.1 = (s32[32,192]{1,0:T(8,128)}, bf16[512,128]{1,0:T(8,128)(2,1)}, s32[1,128]{1,0:T(1,128)}, s32[10,128]{1,0:T(8,128)}) custom-call(s32[1,128]{1,0:T(1,128)} %bitcast.51, s32[1,128]{1,0:T(1,128)} %bitcast.52, s32[1,128]{1,0:T(1,128)} %bitcast.53, s32[1,128]{1,0:T(1,128)} %bitcast.54, s32[10,128]{1,0:T(8,128)} %bitcast.40, s32[10,128]{1,0:T(8,128)} %bitcast.50, ...), custom_call_target="tpu_custom_call" | custom-call | tf_op jit(solution)/shard_map/place/pallas_call | solution.py:64
  13.1 0.8 copy.28
  13.9 14.4 %all_to_all.35 = s32[32,1,192]{2,1,0:T(1,128)S(1)} all-to-all(s32[32,1,192]{2,1,0:T(1,128)S(1)} %copy.28), channel_id=1, replica_groups=mesh['acct'=8,'rep'=4] {'acct','rep'}, dimensions={0} | all-to-all | bytes 49152 | tf_op jit(solution)/shard_map/all_to_all | solution.py:515
  28.2 2.6 %all-to-all-start.1 = ((bf16[32,16,128]{2,1,0:T(8,128)(2,1)}), bf16[32,16,128]{2,1,0:T(8,128)(2,1)S(1)}, u32[]{:S(2)}, u32[]{:S(2)}) async-start(bf16[32,16,128]{2,1,0:T(8,128)(2,1)} %bitcast.48), calls=%async_computation.1 | async-start | bytes 262144 | tf_op jit(solution)/shard_map/all_to_all | solution.py:515
  30.8 0.6 copy.36
  31.4 4.7 %sides.1.rows = bf16[512,256]{1,0:T(8,128)(2,1)} custom-call(bf16[8192,256]{1,0:T(8,128)(2,1)} %old.1, s32[32,192]{1,0:T(8,128)} %bitcast.33), custom_call_target="tpu_custom_call" | custom-call | tf_op jit(solution)/shard_map/sides/pallas_call | solution.py:563
  36.1 2.9 %all-to-all-done.1 = bf16[32,16,128]{2,1,0:T(8,128)(2,1)S(1)} async-done(((bf16[32,16,128]{2,1,0:T(8,128)(2,1)}), bf16[32,16,128]{2,1,0:T(8,128)(2,1)S(1)}, u32[]{:S(2)}, u32[]{:S(2)}) %all-to-all-start.1) | async-done | bytes 131104 | tf_op jit(solution)/shard_map/all_to_all | solution.py:515
  39.0 0.6 copy-done.15
  39.7 7.6 %owner.1 = (bf16[512,256]{1,0:T(8,128)(2,1)}, bf16[256,256]{1,0:T(8,128)(2,1)}, s32[1,512]{1,0:T(1,128)}, s32[512,1]{1,0:T(8,128)}, f32[512,1]{1,0:T(8,128)}, /*...) custom-call(bf16[512,256]{1,0:T(8,128)(2,1)} %sides.1.rows, ...), custom_call_target="tpu_custom_call" | custom-call | tf_op jit(solution)/shard_map/owner/pallas_call | solution.py:64
  47.3 2.9 %all-to-all-start.3 = ((bf16[32,8,256]{2,1,0:T(8,128)(2,1)}), bf16[32,8,256]{2,1,0:T(8,128)(2,1)S(1)}, u32[]{:S(2)}, u32[]{:S(2)}) async-start(bf16[32,8,256]{2,1,0:T(8,128)(2,1)} %bitcast.47), calls=%async_computation.3 | async-start | bytes 262144 | tf_op jit(solution)/shard_map/all_to_all | solution.py:515
  50.2 0.0 all-gather.5.cloned.1.call-start
  50.3 8.7 %answer.1 = bf16[2560,256]{1,0:T(8,128)(2,1)} custom-call(bf16[8192,256]{1,0:T(8,128)(2,1)} %old.1, bf16[512,256]{1,0:T(8,128)(2,1)} %get-tuple-element.53.new, s32[32,192]{1,0:T(8,128)} %bitcast.35), custom_call_target="tpu_custom_call" | custom-call | tf_op jit(solution)/shard_map/answer/pallas_call | solution.py:584
  59.0 0.9 query.1
  60.0 0.0 all-gather.5.cloned.1.call-update
  60.0 5.8 %all-to-all-start.2 = ((bf16[32,80,256]{2,1,0:T(8,128)(2,1)}), bf16[32,80,256]{2,1,0:T(8,128)(2,1)S(1)}, u32[]{:S(2)}, u32[]{:S(2)}) async-start(bf16[32,80,256]{2,1,0:T(8,128)(2,1)} %bitcast.42), calls=%async_computation.2 | async-start | bytes 2621440 | tf_op jit(solution)/shard_map/all_to_all | solution.py:515
  66.0 0.1 slice.20
  66.0 3.1 %hot.1.hots = bf16[2560,128]{1,0:T(8,128)(2,1)S(1)} custom-call(s32[32,192]{1,0:T(8,128)S(1)} %bitcast.37), custom_call_target="tpu_custom_call" | custom-call | tf_op jit(solution)/shard_map/hot/pallas_call | solution.py:287
  69.2 0.1 slice_select_fusion
  69.2 0.1 max.14
  69.3 0.7 select_n.57.nrow
  70.0 0.1 concatenate.3
  70.1 0.7 reshape.180.drow
  70.8 0.1 fusion
  70.9 2.2 %copy-done = bf16[8192,256]{1,0:T(8,128)(2,1)S(1)} copy-done((bf16[8192,256]{1,0:T(8,128)(2,1)S(1)}, bf16[8192,256]{1,0:T(8,128)(2,1)}, u32[]{:S(2)}) %copy-start) | copy-done | bytes 4194328
  73.1 9.6 %refresh.1 = bf16[8192,256]{1,0:T(8,128)(2,1)} custom-call(bf16[8192,256]{1,0:T(8,128)(2,1)S(1)} %copy-done, s32[1,512]{1,0:T(1,128)S(1)} %copy-done.12, bf16[512,256]{1,0:T(8,128)(2,1)S(1)} %copy-done.4), custom_call_target="tpu_custom_call" | custom-call | tf_op jit(solution)/shard_map/refresh/pallas_call | solution.py:264
  82.7 0.0 all-gather.3.cloned.1.call-done
  82.7 8.7 %gather_fusion = bf16[2560,256]{1,0:T(8,128)(2,1)} fusion(bf16[4096,256]{1,0:T(8,128)(2,1)} %all-gather.3.cloned.1.call-done, s32[3072]{0:T(1024)S(1)} %pad_clamp_fusion), kind=kCustom, calls=%fused_computation | custom fusion | bytes 2631680 | tf_op jit(solution)/shard_map/gather | solution.py:612
  91.4 7.9 %all-to-all-done.2 = bf16[32,80,256]{2,1,0:T(8,128)(2,1)S(1)} async-done(((bf16[32,80,256]{2,1,0:T(8,128)(2,1)}), bf16[32,80,256]{2,1,0:T(8,128)(2,1)S(1)}, u32[]{:S(2)}, u32[]{:S(2)}) %all-to-all-start.2) | async-done | bytes 1310752 | tf_op jit(solution)/shard_map/all_to_all | solution.py:515
  99.3 7.1 %attend.1 = (bf16[128,256]{1,0:T(8,128)(2,1)}, bf16[512,256]{1,0:T(8,128)(2,1)}, bf16[768,256]{1,0:T(8,128)(2,1)S(1)}) custom-call(bf16[2560,256]{1,0:T(8,128)(2,1)S(1)} %bitcast.30, bf16[128,256]{1,0:T(8,128)(2,1)S(1)} %get-tuple-element.62.q_rows, bf16[128,256]{1,0:T(8,128)(2,1)} %get-tuple-element.63.q_proj, bf16[128,256]{1,0:T(8,128)(2,1)S(1)} %copy-done.9, ...), custom_call_target="tpu_custom_call" | custom-call | tf_op jit(solution)/shard_map/attend/pallas_call | solution.py:64
  106.4 0.7 copy-done.8
  107.1 3.9 %all-to-all-start.4 = ((bf16[32,16,256]{2,1,0:T(8,128)(2,1)}), bf16[32,16,256]{2,1,0:T(8,128)(2,1)S(1)}, u32[]{:S(2)}, u32[]{:S(2)}) async-start(bf16[32,16,256]{2,1,0:T(8,128)(2,1)} %bitcast.14), calls=%async_computation.4 | async-start | bytes 524288 | tf_op jit(solution)/shard_map/all_to_all | solution.py:515
  111.0 19.7 %all-gather.5.cloned.1.call-done.source = bf16[4096,256]{1,0:T(8,128)(2,1)} async-done(((bf16[128,256]{1,0:T(8,128)(2,1)}), bf16[4096,256]{1,0:T(8,128)(2,1)}) %all-gather.5.cloned.1.call-update) | async-done | bytes 2097168 | tf_op jit(solution)/shard_map/all_gather | solution.py:606
  130.7 1.6 copy-done.2
  132.3 1.6 expand.1.qe
  133.8 1.1 copy-done.1
  134.9 0.7 reshape.185.scal
  135.7 10.4 %back.1 = (bf16[2176,128]{1,0:T(8,128)(2,1)}, bf16[2176,128]{1,0:T(8,128)(2,1)}) custom-call(bf16[4,2560]{1,0:T(4,128)(2,1)} %reshape.185.scal, s32[1,2560]{1,0:T(1,128)} %select_n.57.nrow, bf16[2560,256]{1,0:T(8,128)(2,1)} %copy-done.1, bf16[2560,256]{1,0:T(8,128)(2,1)} %gather_fusion, bf16[512,256]{1,0:T(8,128)(2,1)} %bitcast.44, s32[1,512]{1,0:T(1,128)} %reshape.180.drow, ...), custom_call_target="tpu_custom_call" | custom-call | tf_op jit(solution)/shard_map/back/pallas_call | solution.py:663
  146.0 0.3 collective-permute-start
  146.3 1.9 collective-permute-done
  148.2 1.2 add_convert_fusion
  149.4 21.9 %all_to_all.36.x = bf16[16,136,128]{2,1,0:T(8,128)(2,1)S(1)} all-to-all(bf16[16,136,128]{2,1,0:T(8,128)(2,1)S(1)} %bitcast.43), channel_id=1, replica_groups={{0,2,4,6,8,10,12,14,16,18,20,22,24,26,28,30},{1,3,5,7,9,11,13,15,17,19,..., dimensions={0} | all-to-all | bytes 1114112 | tf_op jit(solution)/shard_map/all_to_all | solution.py:678
  171.3 0.1 spread.1
  171.4 19.3 %all_to_all.37 = bf16[16,136,128]{2,1,0:T(8,128)(2,1)S(1)} all-to-all(bf16[16,136,128]{2,1,0:T(8,128)(2,1)S(1)} %spread.1), channel_id=1, replica_groups={{0,2,4,6,8,10,12,14,16,18,20,22,24,26,28,30},{1,3,5,7,9,11,13,15,17,19,..., dimensions={0} | all-to-all | bytes 1114112 | tf_op jit(solution)/shard_map/all_to_all | solution.py:682
  190.7 2.0 collective-permute-done.1.other
  192.7 1.6 unpack.1
  (37 shorter events, 0.1 us)
Async XLA Ops:
  7.2 75.5 %all-gather.3.cloned.1.call-start = ((), (), s32[]{:S(2)}) async-start(), calls=%async_computation.7 | async-start | bytes 2162688 | tf_op jit(solution)/shard_map/all_gather | solution.py:534
  28.2 10.8 %all-to-all-start.1 = ((bf16[32,16,128]{2,1,0:T(8,128)(2,1)}), bf16[32,16,128]{2,1,0:T(8,128)(2,1)S(1)}, u32[]{:S(2)}, u32[]{:S(2)}) async-start(bf16[32,16,128]{2,1,0:T(8,128)(2,1)} %bitcast.48), calls=%async_computation.1 | async-start | bytes 262144 | tf_op jit(solution)/shard_map/all_to_all | solution.py:515
  39.0 0.6 copy-start.15
  47.3 11.7 %all-to-all-start.3 = ((bf16[32,8,256]{2,1,0:T(8,128)(2,1)}), bf16[32,8,256]{2,1,0:T(8,128)(2,1)S(1)}, u32[]{:S(2)}, u32[]{:S(2)}) async-start(bf16[32,8,256]{2,1,0:T(8,128)(2,1)} %bitcast.47), calls=%async_computation.3 | async-start | bytes 262144 | tf_op jit(solution)/shard_map/all_to_all | solution.py:515
  50.2 80.4 %all-gather.5.cloned.1.call-start = ((), (), s32[]{:S(2)}) async-start(), calls=%async_computation.8 | async-start | bytes 2162688 | tf_op jit(solution)/shard_map/all_gather | solution.py:606
  50.3 8.7 %copy-start.7 = (bf16[256,256]{1,0:T(8,128)(2,1)S(1)}, bf16[256,256]{1,0:T(8,128)(2,1)}, u32[]{:S(2)}) copy-start(bf16[256,256]{1,0:T(8,128)(2,1)} %w_query.3) | copy-start | bytes 393220
  50.3 8.7 %copy-start.13 = (s32[1,128]{1,0:T(1,128)S(1)}, s32[1,128]{1,0:T(1,128)}, u32[]{:S(2)}) copy-start(s32[1,128]{1,0:T(1,128)} %get-tuple-element.58.dplace) | copy-start | bytes 1540
  60.0 5.9 %copy-start.11 = (s32[10,128]{1,0:T(8,128)S(1)}, s32[10,128]{1,0:T(8,128)}, u32[]{:S(2)}) copy-start(s32[10,128]{1,0:T(8,128)} %get-tuple-element.55.nrank) | copy-start | bytes 15364
  60.0 5.9 %copy-start.16 = (s32[128,10,1]{0,2,1:T(1,128)S(1)}, s32[128,10,1]{0,2,1:T(1,128)}, u32[]{:S(2)}) copy-start(s32[128,10,1]{0,2,1:T(1,128)} %param.24) | copy-start | bytes 15364
  60.0 5.9 %copy-start.3 = (s32[32,1,192]{2,0,1:T(8,128)S(1)}, s32[32,1,192]{2,0,1:T(8,128)}, u32[]{:S(2)}) copy-start(s32[32,1,192]{2,0,1:T(8,128)} %copy.36) | copy-start | bytes 73732
  60.0 10.8 %copy-start.4 = (bf16[512,256]{1,0:T(8,128)(2,1)S(1)}, bf16[512,256]{1,0:T(8,128)(2,1)}, u32[]{:S(2)}) copy-start(bf16[512,256]{1,0:T(8,128)(2,1)} %get-tuple-element.53.new) | copy-start | bytes 786436
  60.0 10.8 %copy-start.12 = (s32[1,512]{1,0:T(1,128)S(1)}, s32[1,512]{1,0:T(1,128)}, u32[]{:S(2)}) copy-start(s32[1,512]{1,0:T(1,128)} %get-tuple-element.54.sfirst) | copy-start | bytes 6148
  60.0 39.2 %all-to-all-start.2 = ((bf16[32,80,256]{2,1,0:T(8,128)(2,1)}), bf16[32,80,256]{2,1,0:T(8,128)(2,1)S(1)}, u32[]{:S(2)}, u32[]{:S(2)}) async-start(bf16[32,80,256]{2,1,0:T(8,128)(2,1)} %bitcast.42), calls=%async_computation.2 | async-start | bytes 2621440 | tf_op jit(solution)/shard_map/all_to_all | solution.py:515
  70.9 2.2 %copy-start = (bf16[8192,256]{1,0:T(8,128)(2,1)S(1)}, bf16[8192,256]{1,0:T(8,128)(2,1)}, u32[]{:S(2)}) copy-start(bf16[8192,256]{1,0:T(8,128)(2,1)} %old.1) | copy-start | bytes 12582916
  82.6 16.6 %copy-start.5 = (bf16[256,256]{1,0:T(8,128)(2,1)S(1)}, bf16[256,256]{1,0:T(8,128)(2,1)}, u32[]{:S(2)}) copy-start(bf16[256,256]{1,0:T(8,128)(2,1)} %w_key.3) | copy-start | bytes 393220
  82.6 16.6 %copy-start.6 = (bf16[256,256]{1,0:T(8,128)(2,1)S(1)}, bf16[256,256]{1,0:T(8,128)(2,1)}, u32[]{:S(2)}) copy-start(bf16[256,256]{1,0:T(8,128)(2,1)} %w_value.3) | copy-start | bytes 393220
  82.6 16.6 %copy-start.9 = (bf16[128,256]{1,0:T(8,128)(2,1)S(1)}, bf16[128,256]{1,0:T(8,128)(2,1)}, u32[]{:S(2)}) copy-start(bf16[128,256]{1,0:T(8,128)(2,1)} %grad.1) | copy-start | bytes 196612
  82.7 16.6 %copy-start.10 = (s32[128,10,1]{0,1,2:T(8,128)S(1)}, s32[128,10,1]{0,1,2:T(8,128)}, u32[]{:S(2)}) copy-start(s32[128,10,1]{0,1,2:T(8,128)} %copy.37) | copy-start | bytes 15364
  106.4 0.7 copy-start.8
  107.1 27.8 %all-to-all-start.4 = ((bf16[32,16,256]{2,1,0:T(8,128)(2,1)}), bf16[32,16,256]{2,1,0:T(8,128)(2,1)S(1)}, u32[]{:S(2)}, u32[]{:S(2)}) async-start(bf16[32,16,256]{2,1,0:T(8,128)(2,1)} %bitcast.14), calls=%async_computation.4 | async-start | bytes 524288 | tf_op jit(solution)/shard_map/all_to_all | solution.py:515
  130.7 1.6 copy-start.2
  133.8 1.1 copy-start.1
  134.9 0.7 copy-start.14
  146.0 2.2 %collective-permute-start = (bf16[2176,128]{1,0:T(8,128)(2,1)}, bf16[2176,128]{1,0:T(8,128)(2,1)S(1)}, u32[]{:S(2)}, u32[]{:S(2)}) collective-permute-start(bf16[2176,128]{1,0:T(8,128)(2,1)} %get-tuple-element.85), channel_id=1, source_target_pairs={{0,1},{1,0},{2,3},{3,2},{4,5},{5,4},{6,7},{7,6},{8,9},{9,8},{10,11... | collective-permute-start | bytes 1671176 | tf_op jit(solution)/shard_map/ppermute | solution.py:676
  190.7 2.0 collective-permute-start.1
Sparse Core Ops, SparseCore 0:
  10.9 59.2 all-gather.2
  73.0 57.6 all-gather.4

commit v6 on v5

--- a/solution.py
+++ b/solution.py
@@ -401,9 +401,31 @@
     lax.fori_loop(0, hots.shape[0] // cn, run, 0, unroll=4)
 
 
+def early_body(scal, nrow, ge, dq, drow, scol, w_value, out):
+    n, m = out.shape
+    hs = m // HEADS
+    step = 256
+
+    def block(i, carry):
+        b = pl.ds(pl.multiple_of(i * step, step), step)
+        mine = scol[b, :]
+        mine = jnp.where(mine >= 0, mine, -7)
+        hit = mine == nrow[...]
+        parts = []
+        for h in range(HEADS):
+            a = jnp.where(hit, scal[2 + h : 3 + h, :].astype(F32), 0.0).astype(BF16)
+            parts.append(dot(a, ge[:, h * hs : (h + 1) * hs]).astype(BF16))
+        here = (mine == drow[...]).astype(F32).astype(BF16)
+        dval = jnp.concatenate(parts, axis=1)
+        out[b, :] = dot(here, dq[...]) + dot_nt(dval, w_value[...])
+        return carry
+
+    lax.fori_loop(0, n // step, block, 0)
+
+
 def back_body(
-    scal, nrow, qe, ge, dq, drow, scol, fcol, rows, feats, code, pre, mean, div,
-    upd, rst, cand, rstate, w_in, u_h, w_key, w_value, g_qkv, parity, keep, send, gates, dpre,
+    scal, nrow, qe, partial, scol, fcol, rows, feats, code, pre, mean, div,
+    upd, rst, cand, rstate, w_in, u_h, w_key, g_qkv, parity, keep, send, gates, dpre,
 ):
     n, m = mean.shape[0], rows.shape[1]
     f = feats.shape[1]
@@ -416,15 +438,10 @@
         mine = jnp.where(mine >= 0, mine, -7)
         hit = mine == nrow[...]
         parts = []
-        for j in range(4):
-            src = qe if j < 2 else ge
-            h = j % 2
-            a = jnp.where(hit, scal[j : j + 1, :].astype(F32), 0.0).astype(BF16)
-            parts.append(dot(a, src[:, h * hs : (h + 1) * hs]).astype(BF16))
-        dkey = jnp.concatenate(parts[:2], axis=1)
-        dval = jnp.concatenate(parts[2:], axis=1)
-        here = (mine == drow[...]).astype(F32).astype(BF16)
-        du = dot(here, dq[...]) + dot_nt(dkey, w_key[...]) + dot_nt(dval, w_value[...])
+        for h in range(HEADS):
+            a = jnp.where(hit, scal[h : h + 1, :].astype(F32), 0.0).astype(BF16)
+            parts.append(dot(a, qe[:, h * hs : (h + 1) * hs]).astype(BF16))
+        du = partial[b, :] + dot_nt(jnp.concatenate(parts, axis=1), w_key[...])
         state = rows[b, :].astype(F32)
         update = upd[b, :]
         reset = rst[b, :]
@@ -649,15 +666,22 @@
             compiler_params=room(8),
             name="expand",
         )(proj_all, hots)
-    back, qe = lax.optimization_barrier((back, qe))
     scal = back[:, :4, :cn].transpose(1, 0, 2).reshape(4, n_nb)
+    partial = call(
+        early_body,
+        [((n_side, m), F32)],
+        (scal, nrow, ge, back.reshape(devices * each, m), drow, scol, w_value),
+        "early",
+        56,
+    )[0]
+    qe, partial = lax.optimization_barrier((qe, partial))
     index = lax.axis_index(AXES)
     parity = (index % 2).astype(I32).reshape(1, 1)
     total_rows = (w_msg.size + w_in.size + u_zr.size + u_h.size + 3 * w_query.size) // 128
     half = total_rows // 2
     args = (
-        scal, nrow, qe, ge, back.reshape(devices * each, m), drow, scol, fcol, fetched,
-        got_feats, code, pre, mean, div, upd, rst, cand, rstate, w_in, u_h, w_key, w_value,
+        scal, nrow, qe, partial, scol, fcol, fetched,
+        got_feats, code, pre, mean, div, upd, rst, cand, rstate, w_in, u_h, w_key,
         g_qkv, parity,
     )
     keep, send = pl.pallas_call(

time: 202 us -> 200 us (0.990)
  waiting for transfers between devices: 35 us -> 29.5 us
  Pallas kernels: 59.2 us -> 62.4 us
    all_gather x1, waiting for transfers between devices: 19.7 us -> 2.24 us  [body(): proj_all = lax.all_gather(q_proj, AXES, axis=0, tiled=True)]
    all_to_all x4, waiting for transfers between devices: 10.8 us -> 22.7 us  [exchange(): return lax.all_to_all(x, AXES, split_axis=0, concat_axis=0, tiled=True)]
    pallas_call x5 -> x6, Pallas kernels: 19.6 us -> 24.5 us  [call(): pl.pallas_call(body, out_shape=[jax.ShapeDtypeStruct(s, d) for s, d in ou...]
  transfers between devices with their start and end apart: 8 -> 8, of which waited for: 5 -> 6; matrix products, arithmetic and copies ran while one was open for 7% -> 7% of each run, Pallas kernels for 23% -> 25%
where the time goes in v6:
time: 200 us; the launch traced here: 199 us
  Pallas kernels  62.4 us (31%)
  blocking collectives  55.5 us (28%)
  waiting for transfers between devices  29.5 us (15%)
  local copies, waits for them, and re-layouts  20 us (10%)
  starting transfers between devices  15.6 us (8%)
  between operations  14.3 us (7%)
    pallas_call x6, Pallas kernels, call(): pl.pallas_call(body, out_shape=[jax.ShapeDtypeStruct(s, d) for s, d in ou...  24.5 us
    all_to_all x4, waiting for transfers between devices, exchange(): return lax.all_to_all(x, AXES, split_axis=0, concat_axis=0, tiled=True)  22.7 us
    all_to_all x1, blocking collectives, body(): lax.all_to_all(half_sum, AXES, split_axis=0, concat_axis=0, tiled=True, a...  21.8 us
    all_to_all x1, blocking collectives, body(): lax.all_to_all(spread, AXES, split_axis=0, concat_axis=0, tiled=True, axi...  19.3 us
    all_to_all x4, starting transfers between devices, exchange(): return lax.all_to_all(x, AXES, split_axis=0, concat_axis=0, tiled=True)  15.2 us
    all_to_all x1, blocking collectives, exchange(): return lax.all_to_all(x, AXES, split_axis=0, concat_axis=0, tiled=True)  14.4 us
    pallas_call x1, Pallas kernels, refresh(): pl.pallas_call(functools.partial(refresh_body, block), grid=(n // block,)...  9.6 us
    gather x1, local copies, waits for them, and re-layouts, body(): ge = grad_all[table]  8.72 us
  transfers between devices with their start and end apart: 8, of which 6 were waited for; matrix products, arithmetic and copies ran while one was open for 7% of the time, Pallas kernels for 25%

profile of v6, /device:TPU:0, one launch (start us, length us, event | category | flops | bytes accessed | tf_op | source)
XLA Modules:
  0.0 198.6 jit_solution(11879282395477071958)
XLA Ops:
  7.2 0.0 all-gather.3.cloned.1.call-start
  7.2 0.7 all-gather.3.cloned.1.call-update
  7.9 1.3 copy.39
  9.2 3.9 %place.1 = (s32[32,192]{1,0:T(8,128)}, bf16[512,128]{1,0:T(8,128)(2,1)}, s32[1,128]{1,0:T(1,128)}, s32[10,128]{1,0:T(8,128)}) custom-call(s32[1,128]{1,0:T(1,128)} %bitcast.51, s32[1,128]{1,0:T(1,128)} %bitcast.52, s32[1,128]{1,0:T(1,128)} %bitcast.53, s32[1,128]{1,0:T(1,128)} %bitcast.54, s32[10,128]{1,0:T(8,128)} %bitcast.40, s32[10,128]{1,0:T(8,128)} %bitcast.50, ...), custom_call_target="tpu_custom_call" | custom-call | tf_op jit(solution)/shard_map/place/pallas_call | solution.py:64
  13.1 0.8 copy.30
  13.9 14.4 %all_to_all.35 = s32[32,1,192]{2,1,0:T(1,128)S(1)} all-to-all(s32[32,1,192]{2,1,0:T(1,128)S(1)} %copy.30), channel_id=1, replica_groups=mesh['acct'=8,'rep'=4] {'acct','rep'}, dimensions={0} | all-to-all | bytes 49152 | tf_op jit(solution)/shard_map/all_to_all | solution.py:532
  28.2 2.6 %all-to-all-start.1 = ((bf16[32,16,128]{2,1,0:T(8,128)(2,1)}), bf16[32,16,128]{2,1,0:T(8,128)(2,1)S(1)}, u32[]{:S(2)}, u32[]{:S(2)}) async-start(bf16[32,16,128]{2,1,0:T(8,128)(2,1)} %bitcast.48), calls=%async_computation.1 | async-start | bytes 262144 | tf_op jit(solution)/shard_map/all_to_all | solution.py:532
  30.8 0.6 copy.38
  31.4 4.7 %sides.1.rows = bf16[512,256]{1,0:T(8,128)(2,1)} custom-call(bf16[8192,256]{1,0:T(8,128)(2,1)} %old.1, s32[32,192]{1,0:T(8,128)} %bitcast.33), custom_call_target="tpu_custom_call" | custom-call | tf_op jit(solution)/shard_map/sides/pallas_call | solution.py:580
  36.1 2.9 %all-to-all-done.1 = bf16[32,16,128]{2,1,0:T(8,128)(2,1)S(1)} async-done(((bf16[32,16,128]{2,1,0:T(8,128)(2,1)}), bf16[32,16,128]{2,1,0:T(8,128)(2,1)S(1)}, u32[]{:S(2)}, u32[]{:S(2)}) %all-to-all-start.1) | async-done | bytes 131104 | tf_op jit(solution)/shard_map/all_to_all | solution.py:532
  39.0 0.6 copy-done.15
  39.7 7.6 %owner.1 = (bf16[512,256]{1,0:T(8,128)(2,1)}, bf16[256,256]{1,0:T(8,128)(2,1)}, s32[1,512]{1,0:T(1,128)}, s32[512,1]{1,0:T(8,128)}, f32[512,1]{1,0:T(8,128)}, /*...) custom-call(bf16[512,256]{1,0:T(8,128)(2,1)} %sides.1.rows, ...), custom_call_target="tpu_custom_call" | custom-call | tf_op jit(solution)/shard_map/owner/pallas_call | solution.py:64
  47.3 2.9 %all-to-all-start.3 = ((bf16[32,8,256]{2,1,0:T(8,128)(2,1)}), bf16[32,8,256]{2,1,0:T(8,128)(2,1)S(1)}, u32[]{:S(2)}, u32[]{:S(2)}) async-start(bf16[32,8,256]{2,1,0:T(8,128)(2,1)} %bitcast.47), calls=%async_computation.3 | async-start | bytes 262144 | tf_op jit(solution)/shard_map/all_to_all | solution.py:532
  50.2 0.0 all-gather.5.cloned.1.call-start
  50.3 8.7 %answer.1 = bf16[2560,256]{1,0:T(8,128)(2,1)} custom-call(bf16[8192,256]{1,0:T(8,128)(2,1)} %old.1, bf16[512,256]{1,0:T(8,128)(2,1)} %get-tuple-element.53.new, s32[32,192]{1,0:T(8,128)} %bitcast.35), custom_call_target="tpu_custom_call" | custom-call | tf_op jit(solution)/shard_map/answer/pallas_call | solution.py:601
  59.0 0.9 query.1
  60.1 5.8 %all-to-all-start.2 = ((bf16[32,80,256]{2,1,0:T(8,128)(2,1)}), bf16[32,80,256]{2,1,0:T(8,128)(2,1)S(1)}, u32[]{:S(2)}, u32[]{:S(2)}) async-start(bf16[32,80,256]{2,1,0:T(8,128)(2,1)} %bitcast.42), calls=%async_computation.2 | async-start | bytes 2621440 | tf_op jit(solution)/shard_map/all_to_all | solution.py:532
  66.0 3.1 %hot.1.hots = bf16[2560,128]{1,0:T(8,128)(2,1)S(1)} custom-call(s32[32,192]{1,0:T(8,128)S(1)} %bitcast.36), custom_call_target="tpu_custom_call" | custom-call | tf_op jit(solution)/shard_map/hot/pallas_call | solution.py:287
  69.1 0.1 slice.20
  69.2 0.1 slice_select_fusion
  69.3 0.1 max.14
  69.4 0.7 select_n.57.nrow
  70.1 0.1 concatenate.3
  70.1 0.7 reshape.180.drow
  70.8 0.1 fusion
  70.9 2.2 %copy-done = bf16[8192,256]{1,0:T(8,128)(2,1)S(1)} copy-done((bf16[8192,256]{1,0:T(8,128)(2,1)S(1)}, bf16[8192,256]{1,0:T(8,128)(2,1)}, u32[]{:S(2)}) %copy-start) | copy-done | bytes 4194328
  73.1 9.6 %refresh.1 = bf16[8192,256]{1,0:T(8,128)(2,1)} custom-call(bf16[8192,256]{1,0:T(8,128)(2,1)S(1)} %copy-done, s32[1,512]{1,0:T(1,128)S(1)} %copy-done.12, bf16[512,256]{1,0:T(8,128)(2,1)S(1)} %copy-done.4), custom_call_target="tpu_custom_call" | custom-call | tf_op jit(solution)/shard_map/refresh/pallas_call | solution.py:264
  82.7 8.7 %gather_fusion = bf16[2560,256]{1,0:T(8,128)(2,1)} fusion(bf16[4096,256]{1,0:T(8,128)(2,1)} %all-gather.3.cloned.1.call-done, s32[3072]{0:T(1024)S(1)} %pad_clamp_fusion), kind=kCustom, calls=%fused_computation | custom fusion | bytes 2631680 | tf_op jit(solution)/shard_map/gather | solution.py:629
  91.5 7.9 %all-to-all-done.2 = bf16[32,80,256]{2,1,0:T(8,128)(2,1)S(1)} async-done(((bf16[32,80,256]{2,1,0:T(8,128)(2,1)}), bf16[32,80,256]{2,1,0:T(8,128)(2,1)S(1)}, u32[]{:S(2)}, u32[]{:S(2)}) %all-to-all-start.2) | async-done | bytes 1310752 | tf_op jit(solution)/shard_map/all_to_all | solution.py:532
  99.3 7.1 %attend.1 = (bf16[128,256]{1,0:T(8,128)(2,1)}, bf16[512,256]{1,0:T(8,128)(2,1)}, bf16[768,256]{1,0:T(8,128)(2,1)S(1)}) custom-call(bf16[2560,256]{1,0:T(8,128)(2,1)S(1)} %bitcast.30, bf16[128,256]{1,0:T(8,128)(2,1)S(1)} %get-tuple-element.62.q_rows, bf16[128,256]{1,0:T(8,128)(2,1)} %get-tuple-element.63.q_proj, bf16[128,256]{1,0:T(8,128)(2,1)S(1)} %copy-done.9, ...), custom_call_target="tpu_custom_call" | custom-call | tf_op jit(solution)/shard_map/attend/pallas_call | solution.py:64
  106.4 0.7 copy-done.8
  107.1 3.9 %all-to-all-start.4 = ((bf16[32,16,256]{2,1,0:T(8,128)(2,1)}), bf16[32,16,256]{2,1,0:T(8,128)(2,1)S(1)}, u32[]{:S(2)}, u32[]{:S(2)}) async-start(bf16[32,16,256]{2,1,0:T(8,128)(2,1)} %bitcast.14), calls=%async_computation.4 | async-start | bytes 524288 | tf_op jit(solution)/shard_map/all_to_all | solution.py:532
  111.0 11.9 %all-to-all-done.4 = bf16[32,16,256]{2,1,0:T(8,128)(2,1)S(1)} async-done(((bf16[32,16,256]{2,1,0:T(8,128)(2,1)}), bf16[32,16,256]{2,1,0:T(8,128)(2,1)S(1)}, u32[]{:S(2)}, u32[]{:S(2)}) %all-to-all-start.4) | async-done | bytes 262176 | tf_op jit(solution)/shard_map/all_to_all | solution.py:532
  123.0 0.7 reshape.185.scal
  123.7 4.9 %early.1.partial = f32[512,256]{1,0:T(8,128)} custom-call(bf16[4,2560]{1,0:T(4,128)(2,1)} %reshape.185.scal, s32[1,2560]{1,0:T(1,128)} %select_n.57.nrow, bf16[2560,256]{1,0:T(8,128)(2,1)} %gather_fusion, bf16[512,256]{1,0:T(8,128)(2,1)} %bitcast.44, s32[1,512]{1,0:T(1,128)} %reshape.180.drow, s32[512,1]{1,0:T(8,128)} %get-tuple-element.71.scol, ...), custom_call_target="tpu_custom_call" | custom-call | tf_op jit(solution)/shard_map/early/pallas_call | solution.py:64
  128.6 2.2 %all-gather.5.cloned.1.call-done.source = bf16[4096,256]{1,0:T(8,128)(2,1)} async-done(((bf16[128,256]{1,0:T(8,128)(2,1)}), bf16[4096,256]{1,0:T(8,128)(2,1)}) %all-gather.5.cloned.1.call-update) | async-done | bytes 2097168 | tf_op jit(solution)/shard_map/all_gather | solution.py:623
  130.8 1.6 copy-done.2
  132.4 1.6 expand.1.qe
  134.0 1.1 copy-done.1
  135.0 8.6 %back.1 = (bf16[2176,128]{1,0:T(8,128)(2,1)}, bf16[2176,128]{1,0:T(8,128)(2,1)}) custom-call(bf16[4,2560]{1,0:T(4,128)(2,1)} %reshape.185.scal, s32[1,2560]{1,0:T(1,128)} %select_n.57.nrow, bf16[2560,256]{1,0:T(8,128)(2,1)} %copy-done.1, f32[512,256]{1,0:T(8,128)} %early.1.partial, s32[512,1]{1,0:T(8,128)} %get-tuple-element.71.scol, ...), custom_call_target="tpu_custom_call" | custom-call | tf_op jit(solution)/shard_map/back/pallas_call | solution.py:687
  143.6 0.3 collective-permute-start
  143.9 1.9 collective-permute-done
  145.8 1.2 add_convert_fusion
  147.0 21.8 %all_to_all.36.x = bf16[16,136,128]{2,1,0:T(8,128)(2,1)S(1)} all-to-all(bf16[16,136,128]{2,1,0:T(8,128)(2,1)S(1)} %bitcast.43), channel_id=1, replica_groups={{0,2,4,6,8,10,12,14,16,18,20,22,24,26,28,30},{1,3,5,7,9,11,13,15,17,19,..., dimensions={0} | all-to-all | bytes 1114112 | tf_op jit(solution)/shard_map/all_to_all | solution.py:702
  168.8 0.1 spread.1
  168.9 19.3 %all_to_all.37 = bf16[16,136,128]{2,1,0:T(8,128)(2,1)S(1)} all-to-all(bf16[16,136,128]{2,1,0:T(8,128)(2,1)S(1)} %spread.1), channel_id=1, replica_groups={{0,2,4,6,8,10,12,14,16,18,20,22,24,26,28,30},{1,3,5,7,9,11,13,15,17,19,..., dimensions={0} | all-to-all | bytes 1114112 | tf_op jit(solution)/shard_map/all_to_all | solution.py:706
  188.2 2.0 collective-permute-done.1.other
  190.2 1.6 unpack.1
  (38 shorter events, 0.2 us)
Async XLA Ops:
  7.2 75.5 %all-gather.3.cloned.1.call-start = ((), (), s32[]{:S(2)}) async-start(), calls=%async_computation.7 | async-start | bytes 2162688 | tf_op jit(solution)/shard_map/all_gather | solution.py:551
  28.2 10.8 %all-to-all-start.1 = ((bf16[32,16,128]{2,1,0:T(8,128)(2,1)}), bf16[32,16,128]{2,1,0:T(8,128)(2,1)S(1)}, u32[]{:S(2)}, u32[]{:S(2)}) async-start(bf16[32,16,128]{2,1,0:T(8,128)(2,1)} %bitcast.48), calls=%async_computation.1 | async-start | bytes 262144 | tf_op jit(solution)/shard_map/all_to_all | solution.py:532
  39.0 0.6 copy-start.15
  47.3 11.7 %all-to-all-start.3 = ((bf16[32,8,256]{2,1,0:T(8,128)(2,1)}), bf16[32,8,256]{2,1,0:T(8,128)(2,1)S(1)}, u32[]{:S(2)}, u32[]{:S(2)}) async-start(bf16[32,8,256]{2,1,0:T(8,128)(2,1)} %bitcast.47), calls=%async_computation.3 | async-start | bytes 262144 | tf_op jit(solution)/shard_map/all_to_all | solution.py:532
  50.2 80.6 %all-gather.5.cloned.1.call-start = ((), (), s32[]{:S(2)}) async-start(), calls=%async_computation.8 | async-start | bytes 2162688 | tf_op jit(solution)/shard_map/all_gather | solution.py:623
  50.3 8.7 %copy-start.6 = (bf16[256,256]{1,0:T(8,128)(2,1)S(1)}, bf16[256,256]{1,0:T(8,128)(2,1)}, u32[]{:S(2)}) copy-start(bf16[256,256]{1,0:T(8,128)(2,1)} %w_query.3) | copy-start | bytes 393220
  50.3 8.7 %copy-start.13 = (s32[1,128]{1,0:T(1,128)S(1)}, s32[1,128]{1,0:T(1,128)}, u32[]{:S(2)}) copy-start(s32[1,128]{1,0:T(1,128)} %get-tuple-element.58.dplace) | copy-start | bytes 1540
  60.0 5.9 %copy-start.11 = (s32[10,128]{1,0:T(8,128)S(1)}, s32[10,128]{1,0:T(8,128)}, u32[]{:S(2)}) copy-start(s32[10,128]{1,0:T(8,128)} %get-tuple-element.55.nrank) | copy-start | bytes 15364
  60.0 5.9 %copy-start.16 = (s32[128,10,1]{0,2,1:T(1,128)S(1)}, s32[128,10,1]{0,2,1:T(1,128)}, u32[]{:S(2)}) copy-start(s32[128,10,1]{0,2,1:T(1,128)} %param.24) | copy-start | bytes 15364
  60.0 5.9 %copy-start.3 = (s32[32,1,192]{2,0,1:T(8,128)S(1)}, s32[32,1,192]{2,0,1:T(8,128)}, u32[]{:S(2)}) copy-start(s32[32,1,192]{2,0,1:T(8,128)} %copy.38) | copy-start | bytes 73732
  60.0 10.8 %copy-start.4 = (bf16[512,256]{1,0:T(8,128)(2,1)S(1)}, bf16[512,256]{1,0:T(8,128)(2,1)}, u32[]{:S(2)}) copy-start(bf16[512,256]{1,0:T(8,128)(2,1)} %get-tuple-element.53.new) | copy-start | bytes 786436
  60.1 10.8 %copy-start.12 = (s32[1,512]{1,0:T(1,128)S(1)}, s32[1,512]{1,0:T(1,128)}, u32[]{:S(2)}) copy-start(s32[1,512]{1,0:T(1,128)} %get-tuple-element.54.sfirst) | copy-start | bytes 6148
  60.1 39.2 %all-to-all-start.2 = ((bf16[32,80,256]{2,1,0:T(8,128)(2,1)}), bf16[32,80,256]{2,1,0:T(8,128)(2,1)S(1)}, u32[]{:S(2)}, u32[]{:S(2)}) async-start(bf16[32,80,256]{2,1,0:T(8,128)(2,1)} %bitcast.42), calls=%async_computation.2 | async-start | bytes 2621440 | tf_op jit(solution)/shard_map/all_to_all | solution.py:532
  70.9 2.2 %copy-start = (bf16[8192,256]{1,0:T(8,128)(2,1)S(1)}, bf16[8192,256]{1,0:T(8,128)(2,1)}, u32[]{:S(2)}) copy-start(bf16[8192,256]{1,0:T(8,128)(2,1)} %old.1) | copy-start | bytes 12582916
  82.7 16.6 %copy-start.5 = (bf16[256,256]{1,0:T(8,128)(2,1)S(1)}, bf16[256,256]{1,0:T(8,128)(2,1)}, u32[]{:S(2)}) copy-start(bf16[256,256]{1,0:T(8,128)(2,1)} %w_value.3) | copy-start | bytes 393220
  82.7 16.6 %copy-start.7 = (bf16[256,256]{1,0:T(8,128)(2,1)S(1)}, bf16[256,256]{1,0:T(8,128)(2,1)}, u32[]{:S(2)}) copy-start(bf16[256,256]{1,0:T(8,128)(2,1)} %w_key.3) | copy-start | bytes 393220
  82.7 16.6 %copy-start.9 = (bf16[128,256]{1,0:T(8,128)(2,1)S(1)}, bf16[128,256]{1,0:T(8,128)(2,1)}, u32[]{:S(2)}) copy-start(bf16[128,256]{1,0:T(8,128)(2,1)} %grad.1) | copy-start | bytes 196612
  82.7 16.6 %copy-start.10 = (s32[128,10,1]{0,1,2:T(8,128)S(1)}, s32[128,10,1]{0,1,2:T(8,128)}, u32[]{:S(2)}) copy-start(s32[128,10,1]{0,1,2:T(8,128)} %copy.39) | copy-start | bytes 15364
  106.4 0.7 copy-start.8
  107.1 15.8 %all-to-all-start.4 = ((bf16[32,16,256]{2,1,0:T(8,128)(2,1)}), bf16[32,16,256]{2,1,0:T(8,128)(2,1)S(1)}, u32[]{:S(2)}, u32[]{:S(2)}) async-start(bf16[32,16,256]{2,1,0:T(8,128)(2,1)} %bitcast.14), calls=%async_computation.4 | async-start | bytes 524288 | tf_op jit(solution)/shard_map/all_to_all | solution.py:532
  123.0 0.7 copy-start.14
  130.8 1.6 copy-start.2
  134.0 1.1 copy-start.1
  143.6 2.2 %collective-permute-start = (bf16[2176,128]{1,0:T(8,128)(2,1)}, bf16[2176,128]{1,0:T(8,128)(2,1)S(1)}, u32[]{:S(2)}, u32[]{:S(2)}) collective-permute-start(bf16[2176,128]{1,0:T(8,128)(2,1)} %get-tuple-element.85), channel_id=1, source_target_pairs={{0,1},{1,0},{2,3},{3,2},{4,5},{5,4},{6,7},{7,6},{8,9},{9,8},{10,11... | collective-permute-start | bytes 1671176 | tf_op jit(solution)/shard_map/ppermute | solution.py:700
  188.2 2.0 collective-permute-start.1
Sparse Core Ops, SparseCore 0:
  10.9 59.2 all-gather.2
  73.0 57.7 all-gather.4

commit v7 on v6

--- a/solution.py
+++ b/solution.py
@@ -424,14 +424,20 @@
 
 
 def back_body(
-    scal, nrow, qe, partial, scol, fcol, rows, feats, code, pre, mean, div,
-    upd, rst, cand, rstate, w_in, u_h, w_key, g_qkv, parity, keep, send, gates, dpre,
+    cn, scal, nrow, source, hots, partial, scol, fcol, rows, feats, code, pre, mean, div,
+    upd, rst, cand, rstate, w_in, u_h, w_key, g_qkv, parity, keep, send, gates, dpre, expanded,
 ):
     n, m = mean.shape[0], rows.shape[1]
     f = feats.shape[1]
     hs = m // HEADS
     step = 256
     s = mean.shape[1]
+    if cn % 16:
+        qe = source
+    else:
+        qe = expanded
+        expand_body(cn, source, hots, qe)
+
     def block(i, carry):
         b = pl.ds(pl.multiple_of(i * step, step), step)
         mine = scol[b, :]
@@ -655,17 +661,7 @@
         scalars=1,
     )
     back = exchange(reply.reshape(devices, each, m))
-    if cn % 16:
-        qe = proj_all[table]
-    else:
-        qe = pl.pallas_call(
-            functools.partial(expand_body, cn),
-            out_shape=jax.ShapeDtypeStruct((n_nb, m), BF16),
-            in_specs=[vm, vm],
-            out_specs=vm,
-            compiler_params=room(8),
-            name="expand",
-        )(proj_all, hots)
+    source = proj_all[table] if cn % 16 else proj_all
     scal = back[:, :4, :cn].transpose(1, 0, 2).reshape(4, n_nb)
     partial = call(
         early_body,
@@ -674,22 +670,25 @@
         "early",
         56,
     )[0]
-    qe, partial = lax.optimization_barrier((qe, partial))
+    source, partial = lax.optimization_barrier((source, partial))
     index = lax.axis_index(AXES)
     parity = (index % 2).astype(I32).reshape(1, 1)
     total_rows = (w_msg.size + w_in.size + u_zr.size + u_h.size + 3 * w_query.size) // 128
     half = total_rows // 2
     args = (
-        scal, nrow, qe, partial, scol, fcol, fetched,
+        scal, nrow, source, hots, partial, scol, fcol, fetched,
         got_feats, code, pre, mean, div, upd, rst, cand, rstate, w_in, u_h, w_key,
         g_qkv, parity,
     )
     keep, send = pl.pallas_call(
-        back_body,
+        functools.partial(back_body, cn),
         out_shape=[jax.ShapeDtypeStruct((half, 128), BF16)] * 2,
         in_specs=[vm] * (len(args) - 1) + [sm],
         out_specs=[vm] * 2,
-        scratch_shapes=[pltpu.VMEM((n_side, 3 * m), BF16), pltpu.VMEM((n_side, width), BF16)],
+        scratch_shapes=[
+            pltpu.VMEM((n_side, 3 * m), BF16), pltpu.VMEM((n_side, width), BF16),
+            pltpu.VMEM((n_nb, m), BF16),
+        ],
         compiler_params=room(56),
         name="back",
     )(*args)

time: 200 us -> 197 us (0.985)
    unnamed x36 -> x34, local copies, waits for them, and re-layouts: 8.2 us -> 6.37 us
    pallas_call x2 -> x1, Pallas kernels: 10.1 us -> 10.6 us  [body(): pl.pallas_call(functools.partial(back_body, cn), out_shape=[jax.ShapeDtyp...]
  transfers between devices with their start and end apart: 8 -> 8, of which waited for: 6 -> 6; matrix products, arithmetic and copies ran while one was open for 7% -> 7% of each run, Pallas kernels for 25% -> 26%
where the time goes in v7:
time: 197 us; the launch traced here: 196 us
  Pallas kernels  62.8 us (32%)
  blocking collectives  55.5 us (28%)
  waiting for transfers between devices  28.7 us (15%)
  local copies, waits for them, and re-layouts  18.2 us (9%)
  starting transfers between devices  15.5 us (8%)
  between operations  14.3 us (7%)
    pallas_call x6, Pallas kernels, call(): pl.pallas_call(body, out_shape=[jax.ShapeDtypeStruct(s, d) for s, d in ou...  24.4 us
    all_to_all x4, waiting for transfers between devices, exchange(): return lax.all_to_all(x, AXES, split_axis=0, concat_axis=0, tiled=True)  21.9 us
    all_to_all x1, blocking collectives, body(): lax.all_to_all(half_sum, AXES, split_axis=0, concat_axis=0, tiled=True, a...  21.8 us
    all_to_all x1, blocking collectives, body(): lax.all_to_all(spread, AXES, split_axis=0, concat_axis=0, tiled=True, axi...  19.3 us
    all_to_all x4, starting transfers between devices, exchange(): return lax.all_to_all(x, AXES, split_axis=0, concat_axis=0, tiled=True)  15.2 us
    all_to_all x1, blocking collectives, exchange(): return lax.all_to_all(x, AXES, split_axis=0, concat_axis=0, tiled=True)  14.4 us
    pallas_call x1, Pallas kernels, body(): pl.pallas_call(functools.partial(back_body, cn), out_shape=[jax.ShapeDtyp...  10.6 us
    pallas_call x1, Pallas kernels, refresh(): pl.pallas_call(functools.partial(refresh_body, block), grid=(n // block,)...  9.59 us
  transfers between devices with their start and end apart: 8, of which 6 were waited for; matrix products, arithmetic and copies ran while one was open for 7% of the time, Pallas kernels for 26%

profile of v7, /device:TPU:0, one launch (start us, length us, event | category | flops | bytes accessed | tf_op | source)
XLA Modules:
  0.0 196.4 jit_solution(6716093659329979872)
XLA Ops:
  7.2 0.0 all-gather.3.cloned.1.call-start
  7.2 0.7 all-gather.3.cloned.1.call-update
  7.9 1.3 copy.39
  9.2 3.9 %place.1 = (s32[32,192]{1,0:T(8,128)}, bf16[512,128]{1,0:T(8,128)(2,1)}, s32[1,128]{1,0:T(1,128)}, s32[10,128]{1,0:T(8,128)}) custom-call(s32[1,128]{1,0:T(1,128)} %bitcast.51, s32[1,128]{1,0:T(1,128)} %bitcast.52, s32[1,128]{1,0:T(1,128)} %bitcast.53, s32[1,128]{1,0:T(1,128)} %bitcast.54, s32[10,128]{1,0:T(8,128)} %bitcast.40, s32[10,128]{1,0:T(8,128)} %bitcast.50, ...), custom_call_target="tpu_custom_call" | custom-call | tf_op jit(solution)/shard_map/place/pallas_call | solution.py:64
  13.1 0.8 copy.30
  13.9 14.4 %all_to_all.35 = s32[32,1,192]{2,1,0:T(1,128)S(1)} all-to-all(s32[32,1,192]{2,1,0:T(1,128)S(1)} %copy.30), channel_id=1, replica_groups=mesh['acct'=8,'rep'=4] {'acct','rep'}, dimensions={0} | all-to-all | bytes 49152 | tf_op jit(solution)/shard_map/all_to_all | solution.py:538
  28.2 2.6 %all-to-all-start.1 = ((bf16[32,16,128]{2,1,0:T(8,128)(2,1)}), bf16[32,16,128]{2,1,0:T(8,128)(2,1)S(1)}, u32[]{:S(2)}, u32[]{:S(2)}) async-start(bf16[32,16,128]{2,1,0:T(8,128)(2,1)} %bitcast.48), calls=%async_computation.1 | async-start | bytes 262144 | tf_op jit(solution)/shard_map/all_to_all | solution.py:538
  30.8 0.6 copy.38
  31.4 4.7 %sides.1.rows = bf16[512,256]{1,0:T(8,128)(2,1)} custom-call(bf16[8192,256]{1,0:T(8,128)(2,1)} %old.1, s32[32,192]{1,0:T(8,128)} %bitcast.33), custom_call_target="tpu_custom_call" | custom-call | tf_op jit(solution)/shard_map/sides/pallas_call | solution.py:586
  36.1 2.9 %all-to-all-done.1 = bf16[32,16,128]{2,1,0:T(8,128)(2,1)S(1)} async-done(((bf16[32,16,128]{2,1,0:T(8,128)(2,1)}), bf16[32,16,128]{2,1,0:T(8,128)(2,1)S(1)}, u32[]{:S(2)}, u32[]{:S(2)}) %all-to-all-start.1) | async-done | bytes 131104 | tf_op jit(solution)/shard_map/all_to_all | solution.py:538
  39.0 0.7 copy-done.14
  39.7 7.6 %owner.1 = (bf16[512,256]{1,0:T(8,128)(2,1)}, bf16[256,256]{1,0:T(8,128)(2,1)}, s32[1,512]{1,0:T(1,128)}, s32[512,1]{1,0:T(8,128)}, f32[512,1]{1,0:T(8,128)}, /*...) custom-call(bf16[512,256]{1,0:T(8,128)(2,1)} %sides.1.rows, ...), custom_call_target="tpu_custom_call" | custom-call | tf_op jit(solution)/shard_map/owner/pallas_call | solution.py:64
  47.3 2.9 %all-to-all-start.3 = ((bf16[32,8,256]{2,1,0:T(8,128)(2,1)}), bf16[32,8,256]{2,1,0:T(8,128)(2,1)S(1)}, u32[]{:S(2)}, u32[]{:S(2)}) async-start(bf16[32,8,256]{2,1,0:T(8,128)(2,1)} %bitcast.47), calls=%async_computation.3 | async-start | bytes 262144 | tf_op jit(solution)/shard_map/all_to_all | solution.py:538
  50.2 0.0 all-gather.5.cloned.1.call-start
  50.3 8.7 %answer.1 = bf16[2560,256]{1,0:T(8,128)(2,1)} custom-call(bf16[8192,256]{1,0:T(8,128)(2,1)} %old.1, bf16[512,256]{1,0:T(8,128)(2,1)} %get-tuple-element.53.new, s32[32,192]{1,0:T(8,128)} %bitcast.35), custom_call_target="tpu_custom_call" | custom-call | tf_op jit(solution)/shard_map/answer/pallas_call | solution.py:607
  59.0 0.9 query.1
  60.0 0.0 all-gather.5.cloned.1.call-update
  60.1 5.8 %all-to-all-start.2 = ((bf16[32,80,256]{2,1,0:T(8,128)(2,1)}), bf16[32,80,256]{2,1,0:T(8,128)(2,1)S(1)}, u32[]{:S(2)}, u32[]{:S(2)}) async-start(bf16[32,80,256]{2,1,0:T(8,128)(2,1)} %bitcast.42), calls=%async_computation.2 | async-start | bytes 2621440 | tf_op jit(solution)/shard_map/all_to_all | solution.py:538
  66.0 3.1 %hot.1.hots = bf16[2560,128]{1,0:T(8,128)(2,1)S(1)} custom-call(s32[32,192]{1,0:T(8,128)S(1)} %bitcast.36), custom_call_target="tpu_custom_call" | custom-call | tf_op jit(solution)/shard_map/hot/pallas_call | solution.py:287
  69.1 0.8 copy-done.1
  70.0 0.1 slice.20
  70.0 0.1 slice_select_fusion
  70.1 0.1 max.14
  70.2 0.7 select_n.57.nrow
  70.9 0.1 concatenate.3
  71.0 0.6 reshape.180.drow
  71.6 0.1 fusion
  71.7 2.2 %copy-done = bf16[8192,256]{1,0:T(8,128)(2,1)S(1)} copy-done((bf16[8192,256]{1,0:T(8,128)(2,1)S(1)}, bf16[8192,256]{1,0:T(8,128)(2,1)}, u32[]{:S(2)}) %copy-start) | copy-done | bytes 4194328
  73.9 9.6 %refresh.1 = bf16[8192,256]{1,0:T(8,128)(2,1)} custom-call(bf16[8192,256]{1,0:T(8,128)(2,1)S(1)} %copy-done, s32[1,512]{1,0:T(1,128)S(1)} %copy-done.11, bf16[512,256]{1,0:T(8,128)(2,1)S(1)} %copy-done.3), custom_call_target="tpu_custom_call" | custom-call | tf_op jit(solution)/shard_map/refresh/pallas_call | solution.py:264
  83.5 0.0 all-gather.3.cloned.1.call-done
  83.5 8.8 %gather_fusion = bf16[2560,256]{1,0:T(8,128)(2,1)} fusion(bf16[4096,256]{1,0:T(8,128)(2,1)} %all-gather.3.cloned.1.call-done, s32[3072]{0:T(1024)S(1)} %pad_clamp_fusion), kind=kCustom, calls=%fused_computation | custom fusion | bytes 2631680 | tf_op jit(solution)/shard_map/gather | solution.py:635
  92.3 7.1 %all-to-all-done.2 = bf16[32,80,256]{2,1,0:T(8,128)(2,1)S(1)} async-done(((bf16[32,80,256]{2,1,0:T(8,128)(2,1)}), bf16[32,80,256]{2,1,0:T(8,128)(2,1)S(1)}, u32[]{:S(2)}, u32[]{:S(2)}) %all-to-all-start.2) | async-done | bytes 1310752 | tf_op jit(solution)/shard_map/all_to_all | solution.py:538
  99.4 7.1 %attend.1 = (bf16[128,256]{1,0:T(8,128)(2,1)}, bf16[512,256]{1,0:T(8,128)(2,1)}, bf16[768,256]{1,0:T(8,128)(2,1)S(1)}) custom-call(bf16[2560,256]{1,0:T(8,128)(2,1)S(1)} %bitcast.30, bf16[128,256]{1,0:T(8,128)(2,1)S(1)} %get-tuple-element.62.q_rows, bf16[128,256]{1,0:T(8,128)(2,1)} %get-tuple-element.63.q_proj, bf16[128,256]{1,0:T(8,128)(2,1)S(1)} %copy-done.8, ...), custom_call_target="tpu_custom_call" | custom-call | tf_op jit(solution)/shard_map/attend/pallas_call | solution.py:64
  106.4 0.7 copy-done.7
  107.2 3.9 %all-to-all-start.4 = ((bf16[32,16,256]{2,1,0:T(8,128)(2,1)}), bf16[32,16,256]{2,1,0:T(8,128)(2,1)S(1)}, u32[]{:S(2)}, u32[]{:S(2)}) async-start(bf16[32,16,256]{2,1,0:T(8,128)(2,1)} %bitcast.14), calls=%async_computation.4 | async-start | bytes 524288 | tf_op jit(solution)/shard_map/all_to_all | solution.py:538
  111.0 11.9 %all-to-all-done.4 = bf16[32,16,256]{2,1,0:T(8,128)(2,1)S(1)} async-done(((bf16[32,16,256]{2,1,0:T(8,128)(2,1)}), bf16[32,16,256]{2,1,0:T(8,128)(2,1)S(1)}, u32[]{:S(2)}, u32[]{:S(2)}) %all-to-all-start.4) | async-done | bytes 262176 | tf_op jit(solution)/shard_map/all_to_all | solution.py:538
  123.0 0.7 reshape.185.scal
  123.7 4.8 %early.1.partial = f32[512,256]{1,0:T(8,128)} custom-call(bf16[4,2560]{1,0:T(4,128)(2,1)} %reshape.185.scal, s32[1,2560]{1,0:T(1,128)} %select_n.57.nrow, bf16[2560,256]{1,0:T(8,128)(2,1)} %gather_fusion, bf16[512,256]{1,0:T(8,128)(2,1)} %bitcast.44, s32[1,512]{1,0:T(1,128)} %reshape.180.drow, s32[512,1]{1,0:T(8,128)} %get-tuple-element.70.scol, ...), custom_call_target="tpu_custom_call" | custom-call | tf_op jit(solution)/shard_map/early/pallas_call | solution.py:64
  128.6 2.3 %all-gather.5.cloned.1.call-done.source = bf16[4096,256]{1,0:T(8,128)(2,1)} async-done(((bf16[128,256]{1,0:T(8,128)(2,1)}), bf16[4096,256]{1,0:T(8,128)(2,1)}) %all-gather.5.cloned.1.call-update) | async-done | bytes 2097168 | tf_op jit(solution)/shard_map/all_gather | solution.py:629
  130.8 10.6 %back.1 = (bf16[2176,128]{1,0:T(8,128)(2,1)}, bf16[2176,128]{1,0:T(8,128)(2,1)}) custom-call(bf16[4,2560]{1,0:T(4,128)(2,1)} %reshape.185.scal, s32[1,2560]{1,0:T(1,128)} %select_n.57.nrow, bf16[4096,256]{1,0:T(8,128)(2,1)} %all-gather.5.cloned.1.call-done.source, bf16[2560,128]{1,0:T(8,128)(2,1)} %copy-done.1, f32[512,256]{1,0:T(8,128)} %early.1.partial, ...), custom_call_target="tpu_custom_call" | custom-call | tf_op jit(solution)/shard_map/back/pallas_call | solution.py:683
  141.4 0.3 collective-permute-start
  141.6 1.9 collective-permute-done
  143.5 1.2 add_convert_fusion
  144.8 21.8 %all_to_all.36.x = bf16[16,136,128]{2,1,0:T(8,128)(2,1)S(1)} all-to-all(bf16[16,136,128]{2,1,0:T(8,128)(2,1)S(1)} %bitcast.43), channel_id=1, replica_groups={{0,2,4,6,8,10,12,14,16,18,20,22,24,26,28,30},{1,3,5,7,9,11,13,15,17,19,..., dimensions={0} | all-to-all | bytes 1114112 | tf_op jit(solution)/shard_map/all_to_all | solution.py:701
  166.6 0.1 spread.1
  166.7 19.3 %all_to_all.37 = bf16[16,136,128]{2,1,0:T(8,128)(2,1)S(1)} all-to-all(bf16[16,136,128]{2,1,0:T(8,128)(2,1)S(1)} %spread.1), channel_id=1, replica_groups={{0,2,4,6,8,10,12,14,16,18,20,22,24,26,28,30},{1,3,5,7,9,11,13,15,17,19,..., dimensions={0} | all-to-all | bytes 1114112 | tf_op jit(solution)/shard_map/all_to_all | solution.py:705
  186.0 2.0 collective-permute-done.1.other
  187.9 1.6 unpack.1
  (35 shorter events, 0.1 us)
Async XLA Ops:
  7.2 76.3 %all-gather.3.cloned.1.call-start = ((), (), s32[]{:S(2)}) async-start(), calls=%async_computation.7 | async-start | bytes 2162688 | tf_op jit(solution)/shard_map/all_gather | solution.py:557
  28.2 10.8 %all-to-all-start.1 = ((bf16[32,16,128]{2,1,0:T(8,128)(2,1)}), bf16[32,16,128]{2,1,0:T(8,128)(2,1)S(1)}, u32[]{:S(2)}, u32[]{:S(2)}) async-start(bf16[32,16,128]{2,1,0:T(8,128)(2,1)} %bitcast.48), calls=%async_computation.1 | async-start | bytes 262144 | tf_op jit(solution)/shard_map/all_to_all | solution.py:538
  39.0 0.7 copy-start.14
  47.3 11.7 %all-to-all-start.3 = ((bf16[32,8,256]{2,1,0:T(8,128)(2,1)}), bf16[32,8,256]{2,1,0:T(8,128)(2,1)S(1)}, u32[]{:S(2)}, u32[]{:S(2)}) async-start(bf16[32,8,256]{2,1,0:T(8,128)(2,1)} %bitcast.47), calls=%async_computation.3 | async-start | bytes 262144 | tf_op jit(solution)/shard_map/all_to_all | solution.py:538
  50.2 80.6 %all-gather.5.cloned.1.call-start = ((), (), s32[]{:S(2)}) async-start(), calls=%async_computation.8 | async-start | bytes 2162688 | tf_op jit(solution)/shard_map/all_gather | solution.py:629
  50.3 8.8 %copy-start.6 = (bf16[256,256]{1,0:T(8,128)(2,1)S(1)}, bf16[256,256]{1,0:T(8,128)(2,1)}, u32[]{:S(2)}) copy-start(bf16[256,256]{1,0:T(8,128)(2,1)} %w_query.3) | copy-start | bytes 393220
  50.3 8.7 %copy-start.12 = (s32[1,128]{1,0:T(1,128)S(1)}, s32[1,128]{1,0:T(1,128)}, u32[]{:S(2)}) copy-start(s32[1,128]{1,0:T(1,128)} %get-tuple-element.58.dplace) | copy-start | bytes 1540
  60.0 5.9 %copy-start.10 = (s32[10,128]{1,0:T(8,128)S(1)}, s32[10,128]{1,0:T(8,128)}, u32[]{:S(2)}) copy-start(s32[10,128]{1,0:T(8,128)} %get-tuple-element.55.nrank) | copy-start | bytes 15364
  60.0 5.9 %copy-start.15 = (s32[128,10,1]{0,2,1:T(1,128)S(1)}, s32[128,10,1]{0,2,1:T(1,128)}, u32[]{:S(2)}) copy-start(s32[128,10,1]{0,2,1:T(1,128)} %param.24) | copy-start | bytes 15364
  60.0 5.9 %copy-start.2 = (s32[32,1,192]{2,0,1:T(8,128)S(1)}, s32[32,1,192]{2,0,1:T(8,128)}, u32[]{:S(2)}) copy-start(s32[32,1,192]{2,0,1:T(8,128)} %copy.38) | copy-start | bytes 73732
  60.1 11.6 %copy-start.3 = (bf16[512,256]{1,0:T(8,128)(2,1)S(1)}, bf16[512,256]{1,0:T(8,128)(2,1)}, u32[]{:S(2)}) copy-start(bf16[512,256]{1,0:T(8,128)(2,1)} %get-tuple-element.53.new) | copy-start | bytes 786436
  60.1 11.6 %copy-start.11 = (s32[1,512]{1,0:T(1,128)S(1)}, s32[1,512]{1,0:T(1,128)}, u32[]{:S(2)}) copy-start(s32[1,512]{1,0:T(1,128)} %get-tuple-element.54.sfirst) | copy-start | bytes 6148
  60.1 39.3 %all-to-all-start.2 = ((bf16[32,80,256]{2,1,0:T(8,128)(2,1)}), bf16[32,80,256]{2,1,0:T(8,128)(2,1)S(1)}, u32[]{:S(2)}, u32[]{:S(2)}) async-start(bf16[32,80,256]{2,1,0:T(8,128)(2,1)} %bitcast.42), calls=%async_computation.2 | async-start | bytes 2621440 | tf_op jit(solution)/shard_map/all_to_all | solution.py:538
  69.1 0.8 copy-start.1
  71.7 2.2 %copy-start = (bf16[8192,256]{1,0:T(8,128)(2,1)S(1)}, bf16[8192,256]{1,0:T(8,128)(2,1)}, u32[]{:S(2)}) copy-start(bf16[8192,256]{1,0:T(8,128)(2,1)} %old.1) | copy-start | bytes 12582916
  83.5 15.9 %copy-start.4 = (bf16[256,256]{1,0:T(8,128)(2,1)S(1)}, bf16[256,256]{1,0:T(8,128)(2,1)}, u32[]{:S(2)}) copy-start(bf16[256,256]{1,0:T(8,128)(2,1)} %w_key.3) | copy-start | bytes 393220
  83.5 15.9 %copy-start.5 = (bf16[256,256]{1,0:T(8,128)(2,1)S(1)}, bf16[256,256]{1,0:T(8,128)(2,1)}, u32[]{:S(2)}) copy-start(bf16[256,256]{1,0:T(8,128)(2,1)} %w_value.3) | copy-start | bytes 393220
  83.5 15.9 %copy-start.8 = (bf16[128,256]{1,0:T(8,128)(2,1)S(1)}, bf16[128,256]{1,0:T(8,128)(2,1)}, u32[]{:S(2)}) copy-start(bf16[128,256]{1,0:T(8,128)(2,1)} %grad.1) | copy-start | bytes 196612
  83.5 15.9 %copy-start.9 = (s32[128,10,1]{0,1,2:T(8,128)S(1)}, s32[128,10,1]{0,1,2:T(8,128)}, u32[]{:S(2)}) copy-start(s32[128,10,1]{0,1,2:T(8,128)} %copy.39) | copy-start | bytes 15364
  106.4 0.7 copy-start.7
  107.2 15.8 %all-to-all-start.4 = ((bf16[32,16,256]{2,1,0:T(8,128)(2,1)}), bf16[32,16,256]{2,1,0:T(8,128)(2,1)S(1)}, u32[]{:S(2)}, u32[]{:S(2)}) async-start(bf16[32,16,256]{2,1,0:T(8,128)(2,1)} %bitcast.14), calls=%async_computation.4 | async-start | bytes 524288 | tf_op jit(solution)/shard_map/all_to_all | solution.py:538
  123.0 0.7 copy-start.13
  141.4 2.2 %collective-permute-start = (bf16[2176,128]{1,0:T(8,128)(2,1)}, bf16[2176,128]{1,0:T(8,128)(2,1)S(1)}, u32[]{:S(2)}, u32[]{:S(2)}) collective-permute-start(bf16[2176,128]{1,0:T(8,128)(2,1)} %get-tuple-element.85), channel_id=1, source_target_pairs={{0,1},{1,0},{2,3},{3,2},{4,5},{5,4},{6,7},{7,6},{8,9},{9,8},{10,11... | collective-permute-start | bytes 1671176 | tf_op jit(solution)/shard_map/ppermute | solution.py:699
  186.0 2.0 collective-permute-start.1
Sparse Core Ops, SparseCore 0:
  10.9 59.3 all-gather.2
  73.1 57.6 all-gather.4

commit v8 on v7

--- a/solution.py
+++ b/solution.py
@@ -190,7 +190,7 @@
     n, f = feats.shape
     m = rows.shape[1]
     t = w_msg.shape[0] - m - f
-    step = 128
+    step = 256
     frequency = jnp.exp(iota((1, t), 1).astype(F32) * (-11.5 / t))
     numbers = got[:, : 4 * ce].astype(F32)
     scol[...] = to_col(numbers, n, 2 * ce, 0).astype(I32)

time: 197 us -> 196 us (level)
  transfers between devices with their start and end apart: 8 -> 8, of which waited for: 6 -> 6; matrix products, arithmetic and copies ran while one was open for 7% -> 7% of each run, Pallas kernels for 26% -> 25%
where the time goes in v8:
time: 196 us
  Pallas kernels  61.4 us (31%)
  blocking collectives  55.2 us (28%)
  waiting for transfers between devices  29.4 us (15%)
  local copies, waits for them, and re-layouts  18.2 us (9%)
  starting transfers between devices  15.6 us (8%)
  between operations  14.3 us (7%)
    pallas_call x6, Pallas kernels, call(): pl.pallas_call(body, out_shape=[jax.ShapeDtypeStruct(s, d) for s, d in ou...  23.1 us
    all_to_all x1, blocking collectives, body(): lax.all_to_all(half_sum, AXES, split_axis=0, concat_axis=0, tiled=True, a...  21.5 us
    all_to_all x4, waiting for transfers between devices, exchange(): return lax.all_to_all(x, AXES, split_axis=0, concat_axis=0, tiled=True)  21.1 us
    all_to_all x1, blocking collectives, body(): lax.all_to_all(spread, AXES, split_axis=0, concat_axis=0, tiled=True, axi...  19.3 us
    all_to_all x4, starting transfers between devices, exchange(): return lax.all_to_all(x, AXES, split_axis=0, concat_axis=0, tiled=True)  15.3 us
    all_to_all x1, blocking collectives, exchange(): return lax.all_to_all(x, AXES, split_axis=0, concat_axis=0, tiled=True)  14.4 us
    pallas_call x1, Pallas kernels, body(): pl.pallas_call(functools.partial(back_body, cn), out_shape=[jax.ShapeDtyp...  10.6 us
    pallas_call x1, Pallas kernels, refresh(): pl.pallas_call(functools.partial(refresh_body, block), grid=(n // block,)...  9.59 us
  transfers between devices with their start and end apart: 8, of which 6 were waited for; matrix products, arithmetic and copies ran while one was open for 7% of the time, Pallas kernels for 25%

profile of v8, /device:TPU:0, one launch (start us, length us, event | category | flops | bytes accessed | tf_op | source)
XLA Modules:
  0.0 195.6 jit_solution(15535680118030778552)
XLA Ops:
  7.2 0.0 all-gather.3.cloned.1.call-start
  7.2 0.7 all-gather.3.cloned.1.call-update
  7.9 1.3 copy.39
  9.2 3.9 %place.1 = (s32[32,192]{1,0:T(8,128)}, bf16[512,128]{1,0:T(8,128)(2,1)}, s32[1,128]{1,0:T(1,128)}, s32[10,128]{1,0:T(8,128)}) custom-call(s32[1,128]{1,0:T(1,128)} %bitcast.51, s32[1,128]{1,0:T(1,128)} %bitcast.52, s32[1,128]{1,0:T(1,128)} %bitcast.53, s32[1,128]{1,0:T(1,128)} %bitcast.54, s32[10,128]{1,0:T(8,128)} %bitcast.40, s32[10,128]{1,0:T(8,128)} %bitcast.50, ...), custom_call_target="tpu_custom_call" | custom-call | tf_op jit(solution)/shard_map/place/pallas_call | solution.py:64
  13.1 0.8 copy.30
  13.9 14.4 %all_to_all.35 = s32[32,1,192]{2,1,0:T(1,128)S(1)} all-to-all(s32[32,1,192]{2,1,0:T(1,128)S(1)} %copy.30), channel_id=1, replica_groups=mesh['acct'=8,'rep'=4] {'acct','rep'}, dimensions={0} | all-to-all | bytes 49152 | tf_op jit(solution)/shard_map/all_to_all | solution.py:538
  28.2 2.6 %all-to-all-start.1 = ((bf16[32,16,128]{2,1,0:T(8,128)(2,1)}), bf16[32,16,128]{2,1,0:T(8,128)(2,1)S(1)}, u32[]{:S(2)}, u32[]{:S(2)}) async-start(bf16[32,16,128]{2,1,0:T(8,128)(2,1)} %bitcast.48), calls=%async_computation.1 | async-start | bytes 262144 | tf_op jit(solution)/shard_map/all_to_all | solution.py:538
  30.8 0.6 copy.38
  31.4 4.7 %sides.1.rows = bf16[512,256]{1,0:T(8,128)(2,1)} custom-call(bf16[8192,256]{1,0:T(8,128)(2,1)} %old.1, s32[32,192]{1,0:T(8,128)} %bitcast.33), custom_call_target="tpu_custom_call" | custom-call | tf_op jit(solution)/shard_map/sides/pallas_call | solution.py:586
  36.1 2.9 %all-to-all-done.1 = bf16[32,16,128]{2,1,0:T(8,128)(2,1)S(1)} async-done(((bf16[32,16,128]{2,1,0:T(8,128)(2,1)}), bf16[32,16,128]{2,1,0:T(8,128)(2,1)S(1)}, u32[]{:S(2)}, u32[]{:S(2)}) %all-to-all-start.1) | async-done | bytes 131104 | tf_op jit(solution)/shard_map/all_to_all | solution.py:538
  39.0 0.7 copy-done.14
  39.7 6.3 %owner.1 = (bf16[512,256]{1,0:T(8,128)(2,1)}, bf16[256,256]{1,0:T(8,128)(2,1)}, s32[1,512]{1,0:T(1,128)}, s32[512,1]{1,0:T(8,128)}, f32[512,1]{1,0:T(8,128)}, /*...) custom-call(bf16[512,256]{1,0:T(8,128)(2,1)} %sides.1.rows, ...), custom_call_target="tpu_custom_call" | custom-call | tf_op jit(solution)/shard_map/owner/pallas_call | solution.py:64
  46.0 2.9 %all-to-all-start.3 = ((bf16[32,8,256]{2,1,0:T(8,128)(2,1)}), bf16[32,8,256]{2,1,0:T(8,128)(2,1)S(1)}, u32[]{:S(2)}, u32[]{:S(2)}) async-start(bf16[32,8,256]{2,1,0:T(8,128)(2,1)} %bitcast.47), calls=%async_computation.3 | async-start | bytes 262144 | tf_op jit(solution)/shard_map/all_to_all | solution.py:538
  48.9 0.0 all-gather.5.cloned.1.call-start
  49.0 8.7 %answer.1 = bf16[2560,256]{1,0:T(8,128)(2,1)} custom-call(bf16[8192,256]{1,0:T(8,128)(2,1)} %old.1, bf16[512,256]{1,0:T(8,128)(2,1)} %get-tuple-element.53.new, s32[32,192]{1,0:T(8,128)} %bitcast.35), custom_call_target="tpu_custom_call" | custom-call | tf_op jit(solution)/shard_map/answer/pallas_call | solution.py:607
  57.7 0.9 query.1
  58.7 0.0 all-gather.5.cloned.1.call-update
  58.8 5.8 %all-to-all-start.2 = ((bf16[32,80,256]{2,1,0:T(8,128)(2,1)}), bf16[32,80,256]{2,1,0:T(8,128)(2,1)S(1)}, u32[]{:S(2)}, u32[]{:S(2)}) async-start(bf16[32,80,256]{2,1,0:T(8,128)(2,1)} %bitcast.42), calls=%async_computation.2 | async-start | bytes 2621440 | tf_op jit(solution)/shard_map/all_to_all | solution.py:538
  64.7 3.1 %hot.1.hots = bf16[2560,128]{1,0:T(8,128)(2,1)S(1)} custom-call(s32[32,192]{1,0:T(8,128)S(1)} %bitcast.36), custom_call_target="tpu_custom_call" | custom-call | tf_op jit(solution)/shard_map/hot/pallas_call | solution.py:287
  67.8 0.8 copy-done.1
  68.7 0.1 slice.20
  68.7 0.1 slice_select_fusion
  68.8 0.1 max.14
  68.9 0.7 select_n.57.nrow
  69.6 0.1 concatenate.3
  69.6 0.6 reshape.180.drow
  70.3 0.1 fusion
  70.4 2.2 %copy-done = bf16[8192,256]{1,0:T(8,128)(2,1)S(1)} copy-done((bf16[8192,256]{1,0:T(8,128)(2,1)S(1)}, bf16[8192,256]{1,0:T(8,128)(2,1)}, u32[]{:S(2)}) %copy-start) | copy-done | bytes 4194328
  72.6 9.6 %refresh.1 = bf16[8192,256]{1,0:T(8,128)(2,1)} custom-call(bf16[8192,256]{1,0:T(8,128)(2,1)S(1)} %copy-done, s32[1,512]{1,0:T(1,128)S(1)} %copy-done.11, bf16[512,256]{1,0:T(8,128)(2,1)S(1)} %copy-done.3), custom_call_target="tpu_custom_call" | custom-call | tf_op jit(solution)/shard_map/refresh/pallas_call | solution.py:264
  82.2 0.0 all-gather.3.cloned.1.call-done
  82.2 8.8 %gather_fusion = bf16[2560,256]{1,0:T(8,128)(2,1)} fusion(bf16[4096,256]{1,0:T(8,128)(2,1)} %all-gather.3.cloned.1.call-done, s32[3072]{0:T(1024)S(1)} %pad_clamp_fusion), kind=kCustom, calls=%fused_computation | custom fusion | bytes 2631680 | tf_op jit(solution)/shard_map/gather | solution.py:635
  90.9 6.9 %all-to-all-done.2 = bf16[32,80,256]{2,1,0:T(8,128)(2,1)S(1)} async-done(((bf16[32,80,256]{2,1,0:T(8,128)(2,1)}), bf16[32,80,256]{2,1,0:T(8,128)(2,1)S(1)}, u32[]{:S(2)}, u32[]{:S(2)}) %all-to-all-start.2) | async-done | bytes 1310752 | tf_op jit(solution)/shard_map/all_to_all | solution.py:538
  97.9 7.1 %attend.1 = (bf16[128,256]{1,0:T(8,128)(2,1)}, bf16[512,256]{1,0:T(8,128)(2,1)}, bf16[768,256]{1,0:T(8,128)(2,1)S(1)}) custom-call(bf16[2560,256]{1,0:T(8,128)(2,1)S(1)} %bitcast.30, bf16[128,256]{1,0:T(8,128)(2,1)S(1)} %get-tuple-element.62.q_rows, bf16[128,256]{1,0:T(8,128)(2,1)} %get-tuple-element.63.q_proj, bf16[128,256]{1,0:T(8,128)(2,1)S(1)} %copy-done.8, ...), custom_call_target="tpu_custom_call" | custom-call | tf_op jit(solution)/shard_map/attend/pallas_call | solution.py:64
  105.0 0.7 copy-done.7
  105.7 4.0 %all-to-all-start.4 = ((bf16[32,16,256]{2,1,0:T(8,128)(2,1)}), bf16[32,16,256]{2,1,0:T(8,128)(2,1)S(1)}, u32[]{:S(2)}, u32[]{:S(2)}) async-start(bf16[32,16,256]{2,1,0:T(8,128)(2,1)} %bitcast.14), calls=%async_computation.4 | async-start | bytes 524288 | tf_op jit(solution)/shard_map/all_to_all | solution.py:538
  109.7 11.3 %all-to-all-done.4 = bf16[32,16,256]{2,1,0:T(8,128)(2,1)S(1)} async-done(((bf16[32,16,256]{2,1,0:T(8,128)(2,1)}), bf16[32,16,256]{2,1,0:T(8,128)(2,1)S(1)}, u32[]{:S(2)}, u32[]{:S(2)}) %all-to-all-start.4) | async-done | bytes 262176 | tf_op jit(solution)/shard_map/all_to_all | solution.py:538
  121.0 0.7 reshape.185.scal
  121.7 4.8 %early.1.partial = f32[512,256]{1,0:T(8,128)} custom-call(bf16[4,2560]{1,0:T(4,128)(2,1)} %reshape.185.scal, s32[1,2560]{1,0:T(1,128)} %select_n.57.nrow, bf16[2560,256]{1,0:T(8,128)(2,1)} %gather_fusion, bf16[512,256]{1,0:T(8,128)(2,1)} %bitcast.44, s32[1,512]{1,0:T(1,128)} %reshape.180.drow, s32[512,1]{1,0:T(8,128)} %get-tuple-element.70.scol, ...), custom_call_target="tpu_custom_call" | custom-call | tf_op jit(solution)/shard_map/early/pallas_call | solution.py:64
  126.6 3.7 %all-gather.5.cloned.1.call-done.source = bf16[4096,256]{1,0:T(8,128)(2,1)} async-done(((bf16[128,256]{1,0:T(8,128)(2,1)}), bf16[4096,256]{1,0:T(8,128)(2,1)}) %all-gather.5.cloned.1.call-update) | async-done | bytes 2097168 | tf_op jit(solution)/shard_map/all_gather | solution.py:629
  130.3 10.6 %back.1 = (bf16[2176,128]{1,0:T(8,128)(2,1)}, bf16[2176,128]{1,0:T(8,128)(2,1)}) custom-call(bf16[4,2560]{1,0:T(4,128)(2,1)} %reshape.185.scal, s32[1,2560]{1,0:T(1,128)} %select_n.57.nrow, bf16[4096,256]{1,0:T(8,128)(2,1)} %all-gather.5.cloned.1.call-done.source, bf16[2560,128]{1,0:T(8,128)(2,1)} %copy-done.1, f32[512,256]{1,0:T(8,128)} %early.1.partial, ...), custom_call_target="tpu_custom_call" | custom-call | tf_op jit(solution)/shard_map/back/pallas_call | solution.py:683
  140.8 0.3 collective-permute-start
  141.1 1.9 collective-permute-done
  143.0 1.2 add_convert_fusion
  144.2 21.5 %all_to_all.36.x = bf16[16,136,128]{2,1,0:T(8,128)(2,1)S(1)} all-to-all(bf16[16,136,128]{2,1,0:T(8,128)(2,1)S(1)} %bitcast.43), channel_id=1, replica_groups={{0,2,4,6,8,10,12,14,16,18,20,22,24,26,28,30},{1,3,5,7,9,11,13,15,17,19,..., dimensions={0} | all-to-all | bytes 1114112 | tf_op jit(solution)/shard_map/all_to_all | solution.py:701
  165.7 0.1 spread.1
  165.8 19.3 %all_to_all.37 = bf16[16,136,128]{2,1,0:T(8,128)(2,1)S(1)} all-to-all(bf16[16,136,128]{2,1,0:T(8,128)(2,1)S(1)} %spread.1), channel_id=1, replica_groups={{0,2,4,6,8,10,12,14,16,18,20,22,24,26,28,30},{1,3,5,7,9,11,13,15,17,19,..., dimensions={0} | all-to-all | bytes 1114112 | tf_op jit(solution)/shard_map/all_to_all | solution.py:705
  185.2 2.0 collective-permute-done.1.other
  187.1 1.6 unpack.1
  (35 shorter events, 0.1 us)
Async XLA Ops:
  7.2 75.0 %all-gather.3.cloned.1.call-start = ((), (), s32[]{:S(2)}) async-start(), calls=%async_computation.7 | async-start | bytes 2162688 | tf_op jit(solution)/shard_map/all_gather | solution.py:557
  28.2 10.8 %all-to-all-start.1 = ((bf16[32,16,128]{2,1,0:T(8,128)(2,1)}), bf16[32,16,128]{2,1,0:T(8,128)(2,1)S(1)}, u32[]{:S(2)}, u32[]{:S(2)}) async-start(bf16[32,16,128]{2,1,0:T(8,128)(2,1)} %bitcast.48), calls=%async_computation.1 | async-start | bytes 262144 | tf_op jit(solution)/shard_map/all_to_all | solution.py:538
  39.0 0.7 copy-start.14
  46.0 11.7 %all-to-all-start.3 = ((bf16[32,8,256]{2,1,0:T(8,128)(2,1)}), bf16[32,8,256]{2,1,0:T(8,128)(2,1)S(1)}, u32[]{:S(2)}, u32[]{:S(2)}) async-start(bf16[32,8,256]{2,1,0:T(8,128)(2,1)} %bitcast.47), calls=%async_computation.3 | async-start | bytes 262144 | tf_op jit(solution)/shard_map/all_to_all | solution.py:538
  48.9 81.3 %all-gather.5.cloned.1.call-start = ((), (), s32[]{:S(2)}) async-start(), calls=%async_computation.8 | async-start | bytes 2162688 | tf_op jit(solution)/shard_map/all_gather | solution.py:629
  49.0 8.8 %copy-start.6 = (bf16[256,256]{1,0:T(8,128)(2,1)S(1)}, bf16[256,256]{1,0:T(8,128)(2,1)}, u32[]{:S(2)}) copy-start(bf16[256,256]{1,0:T(8,128)(2,1)} %w_query.3) | copy-start | bytes 393220
  49.0 8.7 %copy-start.12 = (s32[1,128]{1,0:T(1,128)S(1)}, s32[1,128]{1,0:T(1,128)}, u32[]{:S(2)}) copy-start(s32[1,128]{1,0:T(1,128)} %get-tuple-element.58.dplace) | copy-start | bytes 1540
  58.7 5.9 %copy-start.10 = (s32[10,128]{1,0:T(8,128)S(1)}, s32[10,128]{1,0:T(8,128)}, u32[]{:S(2)}) copy-start(s32[10,128]{1,0:T(8,128)} %get-tuple-element.55.nrank) | copy-start | bytes 15364
  58.7 5.9 %copy-start.15 = (s32[128,10,1]{0,2,1:T(1,128)S(1)}, s32[128,10,1]{0,2,1:T(1,128)}, u32[]{:S(2)}) copy-start(s32[128,10,1]{0,2,1:T(1,128)} %param.24) | copy-start | bytes 15364
  58.7 5.9 %copy-start.2 = (s32[32,1,192]{2,0,1:T(8,128)S(1)}, s32[32,1,192]{2,0,1:T(8,128)}, u32[]{:S(2)}) copy-start(s32[32,1,192]{2,0,1:T(8,128)} %copy.38) | copy-start | bytes 73732
  58.7 11.6 %copy-start.3 = (bf16[512,256]{1,0:T(8,128)(2,1)S(1)}, bf16[512,256]{1,0:T(8,128)(2,1)}, u32[]{:S(2)}) copy-start(bf16[512,256]{1,0:T(8,128)(2,1)} %get-tuple-element.53.new) | copy-start | bytes 786436
  58.7 11.6 %copy-start.11 = (s32[1,512]{1,0:T(1,128)S(1)}, s32[1,512]{1,0:T(1,128)}, u32[]{:S(2)}) copy-start(s32[1,512]{1,0:T(1,128)} %get-tuple-element.54.sfirst) | copy-start | bytes 6148
  58.8 39.1 %all-to-all-start.2 = ((bf16[32,80,256]{2,1,0:T(8,128)(2,1)}), bf16[32,80,256]{2,1,0:T(8,128)(2,1)S(1)}, u32[]{:S(2)}, u32[]{:S(2)}) async-start(bf16[32,80,256]{2,1,0:T(8,128)(2,1)} %bitcast.42), calls=%async_computation.2 | async-start | bytes 2621440 | tf_op jit(solution)/shard_map/all_to_all | solution.py:538
  67.8 0.8 copy-start.1
  70.4 2.2 %copy-start = (bf16[8192,256]{1,0:T(8,128)(2,1)S(1)}, bf16[8192,256]{1,0:T(8,128)(2,1)}, u32[]{:S(2)}) copy-start(bf16[8192,256]{1,0:T(8,128)(2,1)} %old.1) | copy-start | bytes 12582916
  82.1 15.7 %copy-start.4 = (bf16[256,256]{1,0:T(8,128)(2,1)S(1)}, bf16[256,256]{1,0:T(8,128)(2,1)}, u32[]{:S(2)}) copy-start(bf16[256,256]{1,0:T(8,128)(2,1)} %w_key.3) | copy-start | bytes 393220
  82.1 15.7 %copy-start.5 = (bf16[256,256]{1,0:T(8,128)(2,1)S(1)}, bf16[256,256]{1,0:T(8,128)(2,1)}, u32[]{:S(2)}) copy-start(bf16[256,256]{1,0:T(8,128)(2,1)} %w_value.3) | copy-start | bytes 393220
  82.2 15.7 %copy-start.8 = (bf16[128,256]{1,0:T(8,128)(2,1)S(1)}, bf16[128,256]{1,0:T(8,128)(2,1)}, u32[]{:S(2)}) copy-start(bf16[128,256]{1,0:T(8,128)(2,1)} %grad.1) | copy-start | bytes 196612
  82.2 15.7 %copy-start.9 = (s32[128,10,1]{0,1,2:T(8,128)S(1)}, s32[128,10,1]{0,1,2:T(8,128)}, u32[]{:S(2)}) copy-start(s32[128,10,1]{0,1,2:T(8,128)} %copy.39) | copy-start | bytes 15364
  105.0 0.7 copy-start.7
  105.7 15.3 %all-to-all-start.4 = ((bf16[32,16,256]{2,1,0:T(8,128)(2,1)}), bf16[32,16,256]{2,1,0:T(8,128)(2,1)S(1)}, u32[]{:S(2)}, u32[]{:S(2)}) async-start(bf16[32,16,256]{2,1,0:T(8,128)(2,1)} %bitcast.14), calls=%async_computation.4 | async-start | bytes 524288 | tf_op jit(solution)/shard_map/all_to_all | solution.py:538
  121.0 0.7 copy-start.13
  140.8 2.2 %collective-permute-start = (bf16[2176,128]{1,0:T(8,128)(2,1)}, bf16[2176,128]{1,0:T(8,128)(2,1)S(1)}, u32[]{:S(2)}, u32[]{:S(2)}) collective-permute-start(bf16[2176,128]{1,0:T(8,128)(2,1)} %get-tuple-element.85), channel_id=1, source_target_pairs={{0,1},{1,0},{2,3},{3,2},{4,5},{5,4},{6,7},{7,6},{8,9},{9,8},{10,11... | collective-permute-start | bytes 1671176 | tf_op jit(solution)/shard_map/ppermute | solution.py:699
  185.2 2.0 %collective-permute-start.1 = (bf16[2176,128]{1,0:T(8,128)(2,1)S(1)}, bf16[2176,128]{1,0:T(8,128)(2,1)S(1)}, u32[]{:S(2)}, u32[]{:S(2)}) collective-permute-start(bf16[2176,128]{1,0:T(8,128)(2,1)S(1)} %bitcast.31), channel_id=1, source_target_pairs={{0,1},{1,0},{2,3},{3,2},{4,5},{5,4},{6,7},{7,6},{8,9},{9,8},{10,11... | collective-permute-start | bytes 1671176 | tf_op jit(solution)/shard_map/ppermute | solution.py:708
Sparse Core Ops, SparseCore 0:
  10.9 59.2 all-gather.2
  73.0 57.2 all-gather.4
